TPU v7x, 512 devices: a whole 4x4x16 slice. The times are simulated.
512 devices in a mesh: dp: 32 (over x, y, core), expert: 16 (over z).
Axes of the slice: x: 4, y: 4, z: 16, core: 2. Of those that a mesh axis runs over, the one named last changes fastest.
Arguments:
- tokens: bfloat16 [65536, 2048], P(('dp', 'expert')), may hold values from -200 to 200
- norm_gain: float32 [2048], replicated, may hold values from 0.1 to 1.9
- route_probs: float32 [65536, 8], P(('dp', 'expert')), may hold values from 0.02 to 4
- window_expert: int32 [65536], P(('dp', 'expert')), may hold values from 0 to 15, as said below
- w_gate_up: bfloat16 [16, 768, 4096], P('expert', 'dp'), may hold values from -0.125 to 0.125
- w_down: bfloat16 [16, 2048, 768], P('expert', 'dp'), may hold values from -0.21875 to 0.21875
Outputs:
- moe_out: bfloat16 [65536, 2048], P(('dp', 'expert'))
Inputs may be any that keep to these rules, and one draw needn't show every extreme that they name: `window_expert`: in the tokens of one device no expert is named by more than 24 tokens; one expert, the same for every device, is named by exactly 24 tokens of every device.
All inputs are finite; a program needn't handle non-finite values.
Results may differ from a plain program's by a relative error of at most 0.0071.
Values may be sent and summed in bfloat16 or wider, within the bound.
No kernel may reach another device: no remote copies, remote signals or barrier semaphores. Data moves between devices by JAX's collectives and lax.ppermute only.
A program may use at most 64 MiB of HBM per device.

v0:
```python
import functools

import jax
import jax.numpy as jnp
from jax import lax
from jax.experimental import pallas as pl
from jax.experimental.pallas import tpu as pltpu
from jax.sharding import PartitionSpec as P

F32, BF16 = jnp.float32, jnp.bfloat16
NT = (((1,), (1,)), ((), ()))
NN = (((1,), (0,)), ((), ()))
REACH = 5
HOPS = tuple(h for d in range(1, REACH + 1) for h in (d, -d))
FAR = 7 - REACH
VMEM = pl.BlockSpec(memory_space=pltpu.VMEM)
HBM = pl.BlockSpec(memory_space=pltpu.HBM)


def shift(x, hops):
    ring = lax.axis_size("expert")
    return lax.ppermute(x, "expert", [(i, (i + hops) % ring) for i in range(ring)])


def trade(x, mask):
    return lax.ppermute(x, "dp", [(i, i ^ mask) for i in range(lax.axis_size("dp"))])


X_STEPS, Y_STEPS, CORE = (8, 24), (2, 6), 1


def gather(x, steps):
    for mask in steps[:-1]:
        x = jnp.concatenate([x, trade(x, mask)], axis=0)
    y = trade(x, steps[-1])
    return x, y, trade(x, CORE), trade(y, CORE)


def gray(k):
    return k ^ (k >> 1)


def place_mask(slot, x_first):
    low, high = gray(slot & 3), gray((slot >> 2) & 3)
    px, py = (low, high) if x_first else (high, low)
    return (px << 3) | (py << 1) | (slot >> 4)


def hidden_order(ff):
    k = jnp.arange(ff, dtype=jnp.int32)[:, None]
    low = jnp.where(k < 512, k & 15, 16 + (k & 7))
    mask = jnp.where(k < 512, place_mask(k >> 4, True), place_mask((k - 512) >> 3, False))
    unit = (mask ^ lax.axis_index("dp")) * 24 + low
    return (unit == jnp.arange(ff, dtype=jnp.int32)[None, :]).astype(BF16)


def pack_kernel(both_ref, down_ref, a_ref, b_ref):
    a_ref[0] = both_ref[:16]
    b_ref[0, :, :768] = down_ref[...]
    for j in range(8):
        b_ref[0, 8 * j : 8 * (j + 1), 768:] = both_ref[16:, 512 * j : 512 * (j + 1)]


def send_kernel(tok_ref, gain_ref, rel_ref, *outs, ring, cap):
    values = tok_ref[...].astype(F32)
    meansq = jnp.mean(values * values, axis=1, keepdims=True)
    normed = (values * lax.rsqrt(meansq + 1e-06) * gain_ref[...]).astype(BF16)
    rel = rel_ref[...]
    count = rel.shape[1]
    member = lax.broadcasted_iota(jnp.int32, (ring, count), 0) == rel
    before = lax.broadcasted_iota(jnp.int32, (count, count), 0) < lax.broadcasted_iota(
        jnp.int32, (count, count), 1
    )
    earlier = lax.dot_general(
        member.astype(F32), before.astype(F32), NN, preferred_element_type=F32
    )
    slot = jnp.sum(jnp.where(member, earlier, 0.0), axis=0, keepdims=True).astype(jnp.int32)
    place = rel * cap + slot
    pick = lax.broadcasted_iota(jnp.int32, (ring * cap, count), 0) == place
    rows = lax.dot_general(
        pick.astype(F32).astype(BF16), normed, NN, preferred_element_type=F32
    )
    for hops, out in zip((0,) + HOPS, outs):
        own = (hops % ring) * cap
        out[0] = rows[own : own + cap].astype(BF16)
        if abs(hops) <= FAR:
            other = ((hops + ring // 2) % ring) * cap
            out[1] = rows[other : other + cap].astype(BF16)


def expert_kernel(x_ref, order_ref, *rest, cap):
    pieces_a, pieces_b = rest[:4], rest[4:8]
    outs, (wa, wb, wd, hid, sem_a, sem_b, sem_d) = rest[8:-7], rest[-7:]
    width = x_ref.shape[1]
    me = lax.axis_index("dp")
    each = pieces_a[0].shape[0]
    copies_a = [
        pltpu.make_async_copy(piece, wa.at[pl.ds(each * q, each)], sem_a.at[q])
        for q, piece in enumerate(pieces_a)
    ]
    copies_b, copies_d = [], []
    for q, piece in enumerate(pieces_b):
        for j in range(8):
            copies_b.append(
                pltpu.make_async_copy(
                    piece.at[:, pl.ds(8 * j, 8), pl.ds(768, 512)],
                    wb.at[pl.ds(each * q, each), :, pl.ds(512 * j, 512)],
                    sem_b.at[8 * q + j],
                )
            )
        for p in range(each):
            slot = each * q + p
            copies_d.append(
                pltpu.make_async_copy(
                    piece.at[p, :, pl.ds(0, 768)],
                    wd.at[me ^ place_mask(slot, False)],
                    sem_d.at[slot],
                )
            )
    for copy in copies_a + copies_b + copies_d:
        copy.start()
    x = x_ref[...]

    def units(w, cols):
        gate = lax.dot_general(x, w[:, :width], NT, preferred_element_type=F32)
        upper = lax.dot_general(x, w[:, width:], NT, preferred_element_type=F32)
        hid[:, cols] = (gate / (1.0 + jnp.exp(-gate)) * upper).astype(BF16)

    half = 2 * each * 16
    for c in range(2):
        copies_a[2 * c].wait()
        copies_a[2 * c + 1].wait()
        units(wa[2 * each * c : 2 * each * (c + 1)].reshape(half, 2 * width), slice(half * c, half * (c + 1)))
    for copy in copies_b:
        copy.wait()
    units(wb[...].reshape(256, 2 * width), slice(2 * half, 2 * half + 256))
    hidden = lax.dot_general(hid[...], order_ref[...], NN, preferred_element_type=F32).astype(BF16)
    for copy in copies_d:
        copy.wait()
    shards, feats, ff = wd.shape
    group = 8
    for n in range(shards // group):
        down = wd[group * n : group * (n + 1)].reshape(group * feats, ff)
        made = lax.dot_general(hidden, down, NT, preferred_element_type=F32)
        cols = slice(group * feats * n, group * feats * (n + 1))
        for b, out in enumerate(outs):
            out[:, cols] = made[cap * b : cap * (b + 1)].astype(BF16)


def run_expert(x, order, pieces_a, pieces_b, cap):
    rows, width = x.shape
    blocks = rows // cap
    ff = order.shape[0]
    shards = 4 * pieces_a[0].shape[0]
    return pl.pallas_call(
        functools.partial(expert_kernel, cap=cap),
        out_shape=[jax.ShapeDtypeStruct((cap, width), BF16)] * blocks,
        in_specs=[VMEM, VMEM] + [HBM] * 8,
        out_specs=[VMEM] * blocks,
        scratch_shapes=[
            pltpu.VMEM((shards, 16, 2 * width), BF16),
            pltpu.VMEM((shards, 8, 2 * width), BF16),
            pltpu.VMEM((shards, width // shards, ff), BF16),
            pltpu.VMEM((rows, ff), BF16),
            pltpu.SemaphoreType.DMA((4,)),
            pltpu.SemaphoreType.DMA((32,)),
            pltpu.SemaphoreType.DMA((32,)),
        ],
        compiler_params=pltpu.CompilerParams(vmem_limit_bytes=55 << 20),
        cost_estimate=pl.CostEstimate(
            flops=6 * rows * width * ff,
            bytes_accessed=6 * width * ff + 4 * x.size,
            transcendentals=rows * ff,
        ),
        name="expert",
    )(x, order, *pieces_a, *pieces_b)


def picks(rel, ring, cap, own):
    count = rel.shape[0]
    member = lax.broadcasted_iota(jnp.int32, (count, ring), 1) == rel
    before = lax.broadcasted_iota(jnp.int32, (count, count), 1) < lax.broadcasted_iota(
        jnp.int32, (count, count), 0
    )
    earlier = lax.dot_general(
        before.astype(F32), member.astype(F32), NN, preferred_element_type=F32
    )
    slot = jnp.sum(jnp.where(member, earlier, 0.0), axis=1, keepdims=True).astype(jnp.int32)
    half = ring // 2
    near = jnp.where(rel >= half, rel - ring, rel) if own else rel - half
    reach = REACH if own else FAR
    block = jnp.where(near > 0, 2 * near - 1, -2 * near)
    inside = jnp.abs(near) <= reach
    place = jnp.where(inside, block * cap + slot, -1)
    blocks = 2 * reach + 1
    cols = lax.broadcasted_iota(jnp.int32, (count, blocks * cap), 1)
    return (cols == place).astype(F32).astype(BF16)


def own_kernel(rel_ref, x_ref, out_ref, *, ring, cap):
    pick = picks(rel_ref[...], ring, cap, True)
    out_ref[...] = lax.dot_general(pick, x_ref[...], NN, preferred_element_type=F32).astype(BF16)


def last_kernel(rel_ref, probs_ref, part_ref, x_ref, out_ref, *, ring, cap):
    pick = picks(rel_ref[...], ring, cap, False)
    probs = probs_ref[...]
    share = probs[:, :1] / jnp.sum(probs, axis=1, keepdims=True)
    got = lax.dot_general(pick, x_ref[...], NN, preferred_element_type=F32)
    out_ref[...] = (share * (part_ref[...].astype(F32) + got)).astype(BF16)


def local(tokens, norm_gain, route_probs, window_expert, w_gate_up, w_down):
    tok_count, width = tokens.shape
    ring = lax.axis_size("expert")
    cap = 3 * tok_count // ring
    ff = w_down.shape[2]
    mine_a, mine_b = pl.pallas_call(
        pack_kernel,
        out_shape=[
            jax.ShapeDtypeStruct((1, 16, 2 * width), BF16),
            jax.ShapeDtypeStruct((1, 64, 1280), BF16),
        ],
        in_specs=[VMEM] * 2,
        out_specs=[VMEM] * 2,
        name="pack",
    )(w_gate_up[0], w_down[0])
    theirs_a, theirs_b = shift(mine_a, ring // 2), shift(mine_b, ring // 2)
    own_w = gather(mine_a, X_STEPS + Y_STEPS), gather(mine_b, Y_STEPS + X_STEPS)
    other_w = gather(theirs_a, X_STEPS + Y_STEPS), gather(theirs_b, Y_STEPS + X_STEPS)
    order = hidden_order(ff)

    rel = lax.rem(window_expert - lax.axis_index("expert") + ring, ring)
    sent = pl.pallas_call(
        functools.partial(send_kernel, ring=ring, cap=cap),
        out_shape=[
            jax.ShapeDtypeStruct((2 if abs(h) <= FAR else 1, cap, width), BF16) for h in (0,) + HOPS
        ],
        in_specs=[VMEM] * 3,
        out_specs=[VMEM] * (1 + len(HOPS)),
        compiler_params=pltpu.CompilerParams(vmem_limit_bytes=28 << 20),
        cost_estimate=pl.CostEstimate(
            flops=6 * tok_count * tok_count * width,
            bytes_accessed=8 * tokens.size,
            transcendentals=0,
        ),
        name="send",
    )(tokens, norm_gain[None, :], rel[None, :])
    got = [sent[0]] + [shift(x, h) for h, x in zip(HOPS, sent[1:])]
    own_x = jnp.concatenate([x[0] for x in got], axis=0)
    other_x = jnp.concatenate([x[1] for x in got[: 1 + 2 * FAR]], axis=0)

    def back(ys):
        return jnp.concatenate([ys[0]] + [shift(y, -h) for h, y in zip(HOPS, ys[1:])], axis=0)

    own_back = back(run_expert(own_x, order, *own_w, cap))
    rel_col = rel[:, None]
    pick_cost = pl.CostEstimate(
        flops=4 * tok_count * tok_count * width, bytes_accessed=8 * tokens.size, transcendentals=0
    )
    part = pl.pallas_call(
        functools.partial(own_kernel, ring=ring, cap=cap),
        out_shape=jax.ShapeDtypeStruct((tok_count, width), BF16),
        in_specs=[VMEM] * 2,
        out_specs=VMEM,
        cost_estimate=pick_cost,
        compiler_params=pltpu.CompilerParams(vmem_limit_bytes=12 << 20),
        name="own_back",
    )(rel_col, own_back)

    other_back = back(run_expert(other_x, order, *other_w, cap))
    return pl.pallas_call(
        functools.partial(last_kernel, ring=ring, cap=cap),
        out_shape=jax.ShapeDtypeStruct((tok_count, width), BF16),
        in_specs=[VMEM] * 4,
        out_specs=VMEM,
        cost_estimate=pick_cost,
        compiler_params=pltpu.CompilerParams(vmem_limit_bytes=12 << 20),
        name="last",
    )(rel_col, route_probs, part, other_back)


def solution(mesh):
    placed = (
        P(("dp", "expert"), None),
        P(),
        P(("dp", "expert"), None),
        P(("dp", "expert")),
        P("expert", "dp", None),
        P("expert", "dp", None),
    )
    return jax.shard_map(
        local, mesh=mesh, in_specs=placed, out_specs=P(("dp", "expert"), None), check_vma=False
    )
```

profile of v0, /device:TPU:38, one launch (start us, length us, event | category | flops | bytes accessed | tf_op | source)
XLA Modules:
  0.0 355.1 jit_solution(2409127138857620928)
XLA Ops:
  1.7 14.8 %collective-permute-start.39 = (bf16[1,64,1280]{2,1,0:T(8,128)(2,1)}, bf16[1,64,1280]{2,1,0:T(8,128)(2,1)S(1)}, u32[]{:S(2)}, u32[]{:S(2)}) collective-permute-start(bf16[1,64,1280]{2,1,0:T(8,128)(2,1)} %get-tuple-element.46), channel_id=1, source_target_pairs={{0,8},{1,9},{2,10},{3,11},{4,12},{5,13},{6,14},{7,15},{8,0},{9,1},... | collective-permute-start | bytes 491528 | tf_op jit(solution)/shard_map/ppermute | solution.py:22
  16.5 3.5 collective-permute-start.16
  27.9 3.1 collective-permute-start
  34.1 6.1 %collective-permute-done.32 = bf16[1,16,4096]{2,1,0:T(8,128)(2,1)S(1)} collective-permute-done((bf16[1,16,4096]{2,1,0:T(8,128)(2,1)}, bf16[1,16,4096]{2,1,0:T(8,128)(2,1)S(1)}, u32[]{:S(2)}, u32[]{:S(2)}) %collective-permute-start.32) | collective-permute-done | bytes 131104 | tf_op jit(solution)/shard_map/ppermute | solution.py:22
  40.2 10.4 %collective-permute-start.1 = (bf16[2,24,2048]{2,1,0:T(8,128)(2,1)S(1)}, bf16[2,24,2048]{2,1,0:T(8,128)(2,1)S(1)}, u32[]{:S(2)}, u32[]{:S(2)}) collective-permute-start(bf16[2,24,2048]{2,1,0:T(8,128)(2,1)S(1)} %get-tuple-element.36), channel_id=1, source_target_pairs={{0,15},{1,0},{2,1},{3,2},{4,3},{5,4},{6,5},{7,6},{8,7},{9,8},{10,9... | collective-permute-start | bytes 589832 | tf_op jit(solution)/shard_map/ppermute | solution.py:22
  50.7 5.0 %collective-permute-start.2 = (bf16[2,24,2048]{2,1,0:T(8,128)(2,1)S(1)}, bf16[2,24,2048]{2,1,0:T(8,128)(2,1)S(1)}, u32[]{:S(2)}, u32[]{:S(2)}) collective-permute-start(bf16[2,24,2048]{2,1,0:T(8,128)(2,1)S(1)} %get-tuple-element.37), channel_id=1, source_target_pairs={{0,2},{1,3},{2,4},{3,5},{4,6},{5,7},{6,8},{7,9},{8,10},{9,11},{10,... | collective-permute-start | bytes 589832 | tf_op jit(solution)/shard_map/ppermute | solution.py:22
  55.7 3.1 collective-permute-start.3
  61.8 6.0 %collective-permute-start.5 = (bf16[1,24,2048]{2,1,0:T(8,128)(2,1)S(1)}, bf16[1,24,2048]{2,1,0:T(8,128)(2,1)S(1)}, u32[]{:S(2)}, u32[]{:S(2)}) collective-permute-start(bf16[1,24,2048]{2,1,0:T(8,128)(2,1)S(1)} %get-tuple-element.40), channel_id=1, source_target_pairs={{0,13},{1,14},{2,15},{3,0},{4,1},{5,2},{6,3},{7,4},{8,5},{9,6},{10... | collective-permute-start | bytes 294920 | tf_op jit(solution)/shard_map/ppermute | solution.py:22
  68.8 4.3 %collective-permute-start.6 = (bf16[1,24,2048]{2,1,0:T(8,128)(2,1)S(1)}, bf16[1,24,2048]{2,1,0:T(8,128)(2,1)S(1)}, u32[]{:S(2)}, u32[]{:S(2)}) collective-permute-start(bf16[1,24,2048]{2,1,0:T(8,128)(2,1)S(1)} %get-tuple-element.41), channel_id=1, source_target_pairs={{0,4},{1,5},{2,6},{3,7},{4,8},{5,9},{6,10},{7,11},{8,12},{9,13},{1... | collective-permute-start | bytes 294920 | tf_op jit(solution)/shard_map/ppermute | solution.py:22
  78.4 3.1 collective-permute-start.17
  83.6 4.1 %collective-permute-start.34 = (bf16[2,16,4096]{2,1,0:T(8,128)(2,1)S(1)}, bf16[2,16,4096]{2,1,0:T(8,128)(2,1)S(1)}, u32[]{:S(2)}, u32[]{:S(2)}) collective-permute-start(bf16[2,16,4096]{2,1,0:T(8,128)(2,1)S(1)} %pad_maximum_fusion.7), channel_id=1, source_target_pairs={{0,384},{16,400},{32,416},{48,432},{64,448},{80,464},{96,480},{112... | collective-permute-start | bytes 786440 | tf_op jit(solution)/shard_map/ppermute | solution.py:26
  88.8 3.9 %collective-permute-start.41 = (bf16[2,64,1280]{2,1,0:T(8,128)(2,1)S(1)}, bf16[2,64,1280]{2,1,0:T(8,128)(2,1)S(1)}, u32[]{:S(2)}, u32[]{:S(2)}) collective-permute-start(bf16[2,64,1280]{2,1,0:T(8,128)(2,1)S(1)} %pad_maximum_fusion.5), channel_id=1, source_target_pairs={{0,96},{16,112},{32,64},{48,80},{64,32},{80,48},{96,0},{112,16},{1... | collective-permute-start | bytes 983048 | tf_op jit(solution)/shard_map/ppermute | solution.py:26
  95.1 3.1 collective-permute-start.18
  98.4 3.6 %collective-permute-start.35 = (bf16[4,16,4096]{2,1,0:T(8,128)(2,1)S(1)}, bf16[4,16,4096]{2,1,0:T(8,128)(2,1)S(1)}, u32[]{:S(2)}, u32[]{:S(2)}) collective-permute-start(bf16[4,16,4096]{2,1,0:T(8,128)(2,1)S(1)} %pad_maximum_fusion.3), channel_id=1, source_target_pairs={{0,32},{16,48},{32,0},{48,16},{64,96},{80,112},{96,64},{112,80},{1... | collective-permute-start | bytes 1572872 | tf_op jit(solution)/shard_map/ppermute | solution.py:26
  102.0 7.1 %collective-permute-done.18 = bf16[4,64,1280]{2,1,0:T(8,128)(2,1)S(1)} collective-permute-done((bf16[4,64,1280]{2,1,0:T(8,128)(2,1)S(1)}, bf16[4,64,1280]{2,1,0:T(8,128)(2,1)S(1)}, u32[]{:S(2)}, u32[]{:S(2)}) %collective-permute-start.18) | collective-permute-done | bytes 655392 | tf_op jit(solution)/shard_map/ppermute | solution.py:26
  109.1 4.5 %collective-permute-start.19 = (bf16[8,64,1280]{2,1,0:T(8,128)(2,1)S(1)}, bf16[8,64,1280]{2,1,0:T(8,128)(2,1)S(1)}, u32[]{:S(2)}, u32[]{:S(2)}) collective-permute-start(bf16[8,64,1280]{2,1,0:T(8,128)(2,1)S(1)} %constant_dynamic-update-slice_fusion.15.rest_4_), channel_id=1, source_target_pairs={{0,384},{16,400},{32,416},{48,432},{64,448},{80,464},{96,480},{112... | collective-permute-start | bytes 3932168 | tf_op jit(solution)/shard_map/ppermute | solution.py:26
  113.8 3.4 collective-permute-start.13
  119.2 3.0 collective-permute-start.42
  122.3 7.5 %collective-permute-start.7 = (bf16[1,24,2048]{2,1,0:T(8,128)(2,1)S(1)}, bf16[1,24,2048]{2,1,0:T(8,128)(2,1)S(1)}, u32[]{:S(2)}, u32[]{:S(2)}) collective-permute-start(bf16[1,24,2048]{2,1,0:T(8,128)(2,1)S(1)} %get-tuple-element.42), channel_id=1, source_target_pairs={{0,12},{1,13},{2,14},{3,15},{4,0},{5,1},{6,2},{7,3},{8,4},{9,5},{1... | collective-permute-start | bytes 294920 | tf_op jit(solution)/shard_map/ppermute | solution.py:22
  129.9 6.2 %collective-permute-done.7 = bf16[1,24,2048]{2,1,0:T(8,128)(2,1)S(1)} collective-permute-done((bf16[1,24,2048]{2,1,0:T(8,128)(2,1)S(1)}, bf16[1,24,2048]{2,1,0:T(8,128)(2,1)S(1)}, u32[]{:S(2)}, u32[]{:S(2)}) %collective-permute-start.7) | collective-permute-done | bytes 98336 | tf_op jit(solution)/shard_map/ppermute | solution.py:22
  136.1 3.6 %collective-permute-start.8 = (bf16[1,24,2048]{2,1,0:T(8,128)(2,1)S(1)}, bf16[1,24,2048]{2,1,0:T(8,128)(2,1)S(1)}, u32[]{:S(2)}, u32[]{:S(2)}) collective-permute-start(bf16[1,24,2048]{2,1,0:T(8,128)(2,1)S(1)} %get-tuple-element.43), channel_id=1, source_target_pairs={{0,5},{1,6},{2,7},{3,8},{4,9},{5,10},{6,11},{7,12},{8,13},{9,14},{... | collective-permute-start | bytes 294920 | tf_op jit(solution)/shard_map/ppermute | solution.py:22
  139.8 7.0 %collective-permute-start.9 = (bf16[1,24,2048]{2,1,0:T(8,128)(2,1)S(1)}, bf16[1,24,2048]{2,1,0:T(8,128)(2,1)S(1)}, u32[]{:S(2)}, u32[]{:S(2)}) collective-permute-start(bf16[1,24,2048]{2,1,0:T(8,128)(2,1)S(1)} %get-tuple-element.44), channel_id=1, source_target_pairs={{0,11},{1,12},{2,13},{3,14},{4,15},{5,0},{6,1},{7,2},{8,3},{9,4},{... | collective-permute-start | bytes 294920 | tf_op jit(solution)/shard_map/ppermute | solution.py:22
  146.8 5.3 %collective-permute-done.8 = bf16[1,24,2048]{2,1,0:T(8,128)(2,1)S(1)} collective-permute-done((bf16[1,24,2048]{2,1,0:T(8,128)(2,1)S(1)}, bf16[1,24,2048]{2,1,0:T(8,128)(2,1)S(1)}, u32[]{:S(2)}, u32[]{:S(2)}) %collective-permute-start.8) | collective-permute-done | bytes 98336 | tf_op jit(solution)/shard_map/ppermute | solution.py:22
  152.1 3.7 %collective-permute-start.36 = (bf16[8,16,4096]{2,1,0:T(8,128)(2,1)S(1)}, bf16[8,16,4096]{2,1,0:T(8,128)(2,1)}, u32[]{:S(2)}, u32[]{:S(2)}) collective-permute-start(bf16[8,16,4096]{2,1,0:T(8,128)(2,1)S(1)} %constant_dynamic-update-slice_fusion.35.rest_0_), channel_id=1, source_target_pairs={{0,96},{16,112},{32,64},{48,80},{64,32},{80,48},{96,0},{112,16},{1... | collective-permute-start | bytes 3145736 | tf_op jit(solution)/shard_map/ppermute | solution.py:26
  164.4 15.7 %collective-permute-done.36.rest_1_ = bf16[8,16,4096]{2,1,0:T(8,128)(2,1)} collective-permute-done((bf16[8,16,4096]{2,1,0:T(8,128)(2,1)S(1)}, bf16[8,16,4096]{2,1,0:T(8,128)(2,1)}, u32[]{:S(2)}, u32[]{:S(2)}) %collective-permute-start.36) | collective-permute-done | bytes 1048608 | tf_op jit(solution)/shard_map/ppermute | solution.py:26
  184.5 7.6 %collective-permute-done.43.rest_5_ = bf16[8,64,1280]{2,1,0:T(8,128)(2,1)S(1)} collective-permute-done((bf16[8,64,1280]{2,1,0:T(8,128)(2,1)S(1)}, bf16[8,64,1280]{2,1,0:T(8,128)(2,1)S(1)}, u32[]{:S(2)}, u32[]{:S(2)}) %collective-permute-start.43) | collective-permute-done | bytes 1310752 | tf_op jit(solution)/shard_map/ppermute | solution.py:26
  197.7 10.2 %expert.2 = (bf16[24,2048]{1,0:T(8,128)(2,1)}, bf16[24,2048]{1,0:T(8,128)(2,1)}, bf16[24,2048]{1,0:T(8,128)(2,1)}, bf16[24,2048]{1,0:T(8,128)(2,1)}, bf16[24,204...) custom-call(bf16[264,2048]{1,0:T(8,128)(2,1)} %copy-done.14, ...), custom_call_target="tpu_custom_call" | custom-call | flops 2491416576 | bytes 11599872 | tf_op jit(solution)/shard_map/expert/pallas_call | solution.py:155
  211.0 9.3 %collective-permute-done.22 = bf16[24,2048]{1,0:T(8,128)(2,1)S(1)} collective-permute-done((bf16[24,2048]{1,0:T(8,128)(2,1)}, bf16[24,2048]{1,0:T(8,128)(2,1)S(1)}, u32[]{:S(2)}, u32[]{:S(2)}) %collective-permute-start.22) | collective-permute-done | bytes 98336 | tf_op jit(solution)/shard_map/ppermute | solution.py:22
  220.3 3.6 %collective-permute-start.23 = (bf16[24,2048]{1,0:T(8,128)(2,1)}, bf16[24,2048]{1,0:T(8,128)(2,1)S(1)}, u32[]{:S(2)}, u32[]{:S(2)}) collective-permute-start(bf16[24,2048]{1,0:T(8,128)(2,1)} %get-tuple-element.49), channel_id=1, source_target_pairs={{0,1},{1,2},{2,3},{3,4},{4,5},{5,6},{6,7},{7,8},{8,9},{9,10},{10,1... | collective-permute-start | bytes 294920 | tf_op jit(solution)/shard_map/ppermute | solution.py:22
  223.9 3.1 collective-permute-done.23
  228.9 6.1 %collective-permute-done.24 = bf16[24,2048]{1,0:T(8,128)(2,1)S(1)} collective-permute-done((bf16[24,2048]{1,0:T(8,128)(2,1)}, bf16[24,2048]{1,0:T(8,128)(2,1)S(1)}, u32[]{:S(2)}, u32[]{:S(2)}) %collective-permute-start.24) | collective-permute-done | bytes 98336 | tf_op jit(solution)/shard_map/ppermute | solution.py:22
  235.1 5.4 %collective-permute-start.25 = (bf16[24,2048]{1,0:T(8,128)(2,1)}, bf16[24,2048]{1,0:T(8,128)(2,1)S(1)}, u32[]{:S(2)}, u32[]{:S(2)}) collective-permute-start(bf16[24,2048]{1,0:T(8,128)(2,1)} %get-tuple-element.51), channel_id=1, source_target_pairs={{0,2},{1,3},{2,4},{3,5},{4,6},{5,7},{6,8},{7,9},{8,10},{9,11},{10,... | collective-permute-start | bytes 294920 | tf_op jit(solution)/shard_map/ppermute | solution.py:22
  240.5 3.9 %collective-permute-done.25 = bf16[24,2048]{1,0:T(8,128)(2,1)S(1)} collective-permute-done((bf16[24,2048]{1,0:T(8,128)(2,1)}, bf16[24,2048]{1,0:T(8,128)(2,1)S(1)}, u32[]{:S(2)}, u32[]{:S(2)}) %collective-permute-start.25) | collective-permute-done | bytes 98336 | tf_op jit(solution)/shard_map/ppermute | solution.py:22
  247.3 6.8 %collective-permute-done.26 = bf16[24,2048]{1,0:T(8,128)(2,1)S(1)} collective-permute-done((bf16[24,2048]{1,0:T(8,128)(2,1)}, bf16[24,2048]{1,0:T(8,128)(2,1)S(1)}, u32[]{:S(2)}, u32[]{:S(2)}) %collective-permute-start.26) | collective-permute-done | bytes 98336 | tf_op jit(solution)/shard_map/ppermute | solution.py:22
  254.1 6.7 %collective-permute-start.27 = (bf16[24,2048]{1,0:T(8,128)(2,1)}, bf16[24,2048]{1,0:T(8,128)(2,1)S(1)}, u32[]{:S(2)}, u32[]{:S(2)}) collective-permute-start(bf16[24,2048]{1,0:T(8,128)(2,1)} %get-tuple-element.53), channel_id=1, source_target_pairs={{0,3},{1,4},{2,5},{3,6},{4,7},{5,8},{6,9},{7,10},{8,11},{9,12},{10... | collective-permute-start | bytes 294920 | tf_op jit(solution)/shard_map/ppermute | solution.py:22
  260.8 4.7 %collective-permute-done.27 = bf16[24,2048]{1,0:T(8,128)(2,1)S(1)} collective-permute-done((bf16[24,2048]{1,0:T(8,128)(2,1)}, bf16[24,2048]{1,0:T(8,128)(2,1)S(1)}, u32[]{:S(2)}, u32[]{:S(2)}) %collective-permute-start.27) | collective-permute-done | bytes 98336 | tf_op jit(solution)/shard_map/ppermute | solution.py:22
  265.6 7.2 %collective-permute-start.28 = (bf16[24,2048]{1,0:T(8,128)(2,1)S(1)}, bf16[24,2048]{1,0:T(8,128)(2,1)S(1)}, u32[]{:S(2)}, u32[]{:S(2)}) collective-permute-start(bf16[24,2048]{1,0:T(8,128)(2,1)S(1)} %copy-done.25), channel_id=1, source_target_pairs={{0,12},{1,13},{2,14},{3,15},{4,0},{5,1},{6,2},{7,3},{8,4},{9,5},{1... | collective-permute-start | bytes 294920 | tf_op jit(solution)/shard_map/ppermute | solution.py:22
  272.8 4.9 %collective-permute-done.28 = bf16[24,2048]{1,0:T(8,128)(2,1)S(1)} collective-permute-done((bf16[24,2048]{1,0:T(8,128)(2,1)S(1)}, bf16[24,2048]{1,0:T(8,128)(2,1)S(1)}, u32[]{:S(2)}, u32[]{:S(2)}) %collective-permute-start.28) | collective-permute-done | bytes 98336 | tf_op jit(solution)/shard_map/ppermute | solution.py:22
  277.6 4.4 %collective-permute-start.29 = (bf16[24,2048]{1,0:T(8,128)(2,1)S(1)}, bf16[24,2048]{1,0:T(8,128)(2,1)S(1)}, u32[]{:S(2)}, u32[]{:S(2)}) collective-permute-start(bf16[24,2048]{1,0:T(8,128)(2,1)S(1)} %copy-done.24), channel_id=1, source_target_pairs={{0,4},{1,5},{2,6},{3,7},{4,8},{5,9},{6,10},{7,11},{8,12},{9,13},{1... | collective-permute-start | bytes 294920 | tf_op jit(solution)/shard_map/ppermute | solution.py:22
  282.1 6.1 %collective-permute-done.29 = bf16[24,2048]{1,0:T(8,128)(2,1)S(1)} collective-permute-done((bf16[24,2048]{1,0:T(8,128)(2,1)S(1)}, bf16[24,2048]{1,0:T(8,128)(2,1)S(1)}, u32[]{:S(2)}, u32[]{:S(2)}) %collective-permute-start.29) | collective-permute-done | bytes 98336 | tf_op jit(solution)/shard_map/ppermute | solution.py:22
  288.2 4.8 %collective-permute-start.30 = (bf16[24,2048]{1,0:T(8,128)(2,1)S(1)}, bf16[24,2048]{1,0:T(8,128)(2,1)S(1)}, u32[]{:S(2)}, u32[]{:S(2)}) collective-permute-start(bf16[24,2048]{1,0:T(8,128)(2,1)S(1)} %copy-done.23), channel_id=1, source_target_pairs={{0,11},{1,12},{2,13},{3,14},{4,15},{5,0},{6,1},{7,2},{8,3},{9,4},{... | collective-permute-start | bytes 294920 | tf_op jit(solution)/shard_map/ppermute | solution.py:22
  293.0 6.8 %collective-permute-done.30 = bf16[24,2048]{1,0:T(8,128)(2,1)S(1)} collective-permute-done((bf16[24,2048]{1,0:T(8,128)(2,1)S(1)}, bf16[24,2048]{1,0:T(8,128)(2,1)S(1)}, u32[]{:S(2)}, u32[]{:S(2)}) %collective-permute-start.30) | collective-permute-done | bytes 98336 | tf_op jit(solution)/shard_map/ppermute | solution.py:22
  299.8 7.3 %collective-permute-start.31 = (bf16[24,2048]{1,0:T(8,128)(2,1)S(1)}, bf16[24,2048]{1,0:T(8,128)(2,1)S(1)}, u32[]{:S(2)}, u32[]{:S(2)}) collective-permute-start(bf16[24,2048]{1,0:T(8,128)(2,1)S(1)} %copy-done.22), channel_id=1, source_target_pairs={{0,5},{1,6},{2,7},{3,8},{4,9},{5,10},{6,11},{7,12},{8,13},{9,14},{... | collective-permute-start | bytes 294920 | tf_op jit(solution)/shard_map/ppermute | solution.py:22
  307.1 4.0 %collective-permute-done.31 = bf16[24,2048]{1,0:T(8,128)(2,1)S(1)} collective-permute-done((bf16[24,2048]{1,0:T(8,128)(2,1)S(1)}, bf16[24,2048]{1,0:T(8,128)(2,1)S(1)}, u32[]{:S(2)}, u32[]{:S(2)}) %collective-permute-start.31) | collective-permute-done | bytes 98336 | tf_op jit(solution)/shard_map/ppermute | solution.py:22
  313.4 9.9 %expert.3 = (bf16[24,2048]{1,0:T(8,128)(2,1)}, bf16[24,2048]{1,0:T(8,128)(2,1)}, bf16[24,2048]{1,0:T(8,128)(2,1)}, bf16[24,2048]{1,0:T(8,128)(2,1)}, bf16[24,2048]{1,0:T(8,128)(2,1)}) custom-call(bf16[120,2048]{1,0:T(8,128)(2,1)} %copy-done.20, bf16[768,768]{1,0:T(8,128)(2,1)} %fusion.order_ref, bf16[8,16,4096]{2,1,0:T(8,128)(2,1)} %copy-done.6, ...), custom_call_target="tpu_custom_call" | custom-call | flops 1132462080 | bytes 10420224 | tf_op jit(solution)/shard_map/expert/pallas_call | solution.py:155
  323.3 6.1 %collective-permute-start.46 = (bf16[24,2048]{1,0:T(8,128)(2,1)}, bf16[24,2048]{1,0:T(8,128)(2,1)S(1)}, u32[]{:S(2)}, u32[]{:S(2)}) collective-permute-start(bf16[24,2048]{1,0:T(8,128)(2,1)} %get-tuple-element.59), channel_id=1, source_target_pairs={{0,15},{1,0},{2,1},{3,2},{4,3},{5,4},{6,5},{7,6},{8,7},{9,8},{10,9... | collective-permute-start | bytes 294920 | tf_op jit(solution)/shard_map/ppermute | solution.py:22
  333.3 11.2 %collective-permute-start.48 = (bf16[24,2048]{1,0:T(8,128)(2,1)}, bf16[24,2048]{1,0:T(8,128)(2,1)S(1)}, u32[]{:S(2)}, u32[]{:S(2)}) collective-permute-start(bf16[24,2048]{1,0:T(8,128)(2,1)} %get-tuple-element.61), channel_id=1, source_target_pairs={{0,14},{1,15},{2,0},{3,1},{4,2},{5,3},{6,4},{7,5},{8,6},{9,7},{10,... | collective-permute-start | bytes 294920 | tf_op jit(solution)/shard_map/ppermute | solution.py:22
  347.0 6.7 %collective-permute-done.49 = bf16[24,2048]{1,0:T(8,128)(2,1)S(1)} collective-permute-done((bf16[24,2048]{1,0:T(8,128)(2,1)}, bf16[24,2048]{1,0:T(8,128)(2,1)S(1)}, u32[]{:S(2)}, u32[]{:S(2)}) %collective-permute-start.49) | collective-permute-done | bytes 98336 | tf_op jit(solution)/shard_map/ppermute | solution.py:22
  (169 shorter events, 65.6 us)
Async XLA Ops:
  1.7 54.0 %collective-permute-start.39 = (bf16[1,64,1280]{2,1,0:T(8,128)(2,1)}, bf16[1,64,1280]{2,1,0:T(8,128)(2,1)S(1)}, u32[]{:S(2)}, u32[]{:S(2)}) collective-permute-start(bf16[1,64,1280]{2,1,0:T(8,128)(2,1)} %get-tuple-element.46), channel_id=1, source_target_pairs={{0,8},{1,9},{2,10},{3,11},{4,12},{5,13},{6,14},{7,15},{8,0},{9,1},... | collective-permute-start | bytes 491528 | tf_op jit(solution)/shard_map/ppermute | solution.py:22
  16.5 42.3 %collective-permute-start.16 = (bf16[1,64,1280]{2,1,0:T(8,128)(2,1)}, bf16[1,64,1280]{2,1,0:T(8,128)(2,1)S(1)}, u32[]{:S(2)}, u32[]{:S(2)}) collective-permute-start(bf16[1,64,1280]{2,1,0:T(8,128)(2,1)} %get-tuple-element.46), channel_id=1, source_target_pairs={{0,32},{16,48},{32,0},{48,16},{64,96},{80,112},{96,64},{112,80},{1... | collective-permute-start | bytes 491528 | tf_op jit(solution)/shard_map/ppermute | solution.py:26
  20.0 20.1 %collective-permute-start.32 = (bf16[1,16,4096]{2,1,0:T(8,128)(2,1)}, bf16[1,16,4096]{2,1,0:T(8,128)(2,1)S(1)}, u32[]{:S(2)}, u32[]{:S(2)}) collective-permute-start(bf16[1,16,4096]{2,1,0:T(8,128)(2,1)} %get-tuple-element.45), channel_id=1, source_target_pairs={{0,8},{1,9},{2,10},{3,11},{4,12},{5,13},{6,14},{7,15},{8,0},{9,1},... | collective-permute-start | bytes 393224 | tf_op jit(solution)/shard_map/ppermute | solution.py:22
  22.0 28.7 %collective-permute-start.10 = (bf16[1,16,4096]{2,1,0:T(8,128)(2,1)}, bf16[1,16,4096]{2,1,0:T(8,128)(2,1)S(1)}, u32[]{:S(2)}, u32[]{:S(2)}) collective-permute-start(bf16[1,16,4096]{2,1,0:T(8,128)(2,1)} %get-tuple-element.45), channel_id=1, source_target_pairs={{0,128},{16,144},{32,160},{48,176},{64,192},{80,208},{96,224},{112... | collective-permute-start | bytes 393224 | tf_op jit(solution)/shard_map/ppermute | solution.py:26
  27.9 33.9 %collective-permute-start = (bf16[2,24,2048]{2,1,0:T(8,128)(2,1)S(1)}, bf16[2,24,2048]{2,1,0:T(8,128)(2,1)}, u32[]{:S(2)}, u32[]{:S(2)}) collective-permute-start(bf16[2,24,2048]{2,1,0:T(8,128)(2,1)S(1)} %get-tuple-element.35), channel_id=1, source_target_pairs={{0,1},{1,2},{2,3},{3,4},{4,5},{5,6},{6,7},{7,8},{8,9},{9,10},{10,1... | collective-permute-start | bytes 589832 | tf_op jit(solution)/shard_map/ppermute | solution.py:22
  40.2 28.6 %collective-permute-start.1 = (bf16[2,24,2048]{2,1,0:T(8,128)(2,1)S(1)}, bf16[2,24,2048]{2,1,0:T(8,128)(2,1)S(1)}, u32[]{:S(2)}, u32[]{:S(2)}) collective-permute-start(bf16[2,24,2048]{2,1,0:T(8,128)(2,1)S(1)} %get-tuple-element.36), channel_id=1, source_target_pairs={{0,15},{1,0},{2,1},{3,2},{4,3},{5,4},{6,5},{7,6},{8,7},{9,8},{10,9... | collective-permute-start | bytes 589832 | tf_op jit(solution)/shard_map/ppermute | solution.py:22
  50.7 22.4 %collective-permute-start.2 = (bf16[2,24,2048]{2,1,0:T(8,128)(2,1)S(1)}, bf16[2,24,2048]{2,1,0:T(8,128)(2,1)S(1)}, u32[]{:S(2)}, u32[]{:S(2)}) collective-permute-start(bf16[2,24,2048]{2,1,0:T(8,128)(2,1)S(1)} %get-tuple-element.37), channel_id=1, source_target_pairs={{0,2},{1,3},{2,4},{3,5},{4,6},{5,7},{6,8},{7,9},{8,10},{9,11},{10,... | collective-permute-start | bytes 589832 | tf_op jit(solution)/shard_map/ppermute | solution.py:22
  55.7 19.8 %collective-permute-start.3 = (bf16[2,24,2048]{2,1,0:T(8,128)(2,1)S(1)}, bf16[2,24,2048]{2,1,0:T(8,128)(2,1)S(1)}, u32[]{:S(2)}, u32[]{:S(2)}) collective-permute-start(bf16[2,24,2048]{2,1,0:T(8,128)(2,1)S(1)} %get-tuple-element.38), channel_id=1, source_target_pairs={{0,14},{1,15},{2,0},{3,1},{4,2},{5,3},{6,4},{7,5},{8,6},{9,7},{10,... | collective-permute-start | bytes 589832 | tf_op jit(solution)/shard_map/ppermute | solution.py:22
  58.9 19.5 %collective-permute-start.4 = (bf16[1,24,2048]{2,1,0:T(8,128)(2,1)S(1)}, bf16[1,24,2048]{2,1,0:T(8,128)(2,1)S(1)}, u32[]{:S(2)}, u32[]{:S(2)}) collective-permute-start(bf16[1,24,2048]{2,1,0:T(8,128)(2,1)S(1)} %get-tuple-element.39), channel_id=1, source_target_pairs={{0,3},{1,4},{2,5},{3,6},{4,7},{5,8},{6,9},{7,10},{8,11},{9,12},{10... | collective-permute-start | bytes 294920 | tf_op jit(solution)/shard_map/ppermute | solution.py:22
  61.8 19.8 %collective-permute-start.5 = (bf16[1,24,2048]{2,1,0:T(8,128)(2,1)S(1)}, bf16[1,24,2048]{2,1,0:T(8,128)(2,1)S(1)}, u32[]{:S(2)}, u32[]{:S(2)}) collective-permute-start(bf16[1,24,2048]{2,1,0:T(8,128)(2,1)S(1)} %get-tuple-element.40), channel_id=1, source_target_pairs={{0,13},{1,14},{2,15},{3,0},{4,1},{5,2},{6,3},{7,4},{8,5},{9,6},{10... | collective-permute-start | bytes 294920 | tf_op jit(solution)/shard_map/ppermute | solution.py:22
  68.8 14.7 %collective-permute-start.6 = (bf16[1,24,2048]{2,1,0:T(8,128)(2,1)S(1)}, bf16[1,24,2048]{2,1,0:T(8,128)(2,1)S(1)}, u32[]{:S(2)}, u32[]{:S(2)}) collective-permute-start(bf16[1,24,2048]{2,1,0:T(8,128)(2,1)S(1)} %get-tuple-element.41), channel_id=1, source_target_pairs={{0,4},{1,5},{2,6},{3,7},{4,8},{5,9},{6,10},{7,11},{8,12},{9,13},{1... | collective-permute-start | bytes 294920 | tf_op jit(solution)/shard_map/ppermute | solution.py:22
  73.1 19.6 %collective-permute-start.11 = (bf16[2,16,4096]{2,1,0:T(8,128)(2,1)S(1)}, bf16[2,16,4096]{2,1,0:T(8,128)(2,1)S(1)}, u32[]{:S(2)}, u32[]{:S(2)}) collective-permute-start(bf16[2,16,4096]{2,1,0:T(8,128)(2,1)S(1)} %pad_maximum_fusion.6), channel_id=1, source_target_pairs={{0,384},{16,400},{32,416},{48,432},{64,448},{80,464},{96,480},{112... | collective-permute-start | bytes 786440 | tf_op jit(solution)/shard_map/ppermute | solution.py:26
  75.5 8.0 %collective-permute-start.33 = (bf16[1,16,4096]{2,1,0:T(8,128)(2,1)S(1)}, bf16[1,16,4096]{2,1,0:T(8,128)(2,1)S(1)}, u32[]{:S(2)}, u32[]{:S(2)}) collective-permute-start(bf16[1,16,4096]{2,1,0:T(8,128)(2,1)S(1)} %collective-permute-done.32), channel_id=1, source_target_pairs={{0,128},{16,144},{32,160},{48,176},{64,192},{80,208},{96,224},{112... | collective-permute-start | bytes 393224 | tf_op jit(solution)/shard_map/ppermute | solution.py:26
  78.4 16.7 %collective-permute-start.17 = (bf16[2,64,1280]{2,1,0:T(8,128)(2,1)S(1)}, bf16[2,64,1280]{2,1,0:T(8,128)(2,1)S(1)}, u32[]{:S(2)}, u32[]{:S(2)}) collective-permute-start(bf16[2,64,1280]{2,1,0:T(8,128)(2,1)S(1)} %pad_maximum_fusion.4), channel_id=1, source_target_pairs={{0,96},{16,112},{32,64},{48,80},{64,32},{80,48},{96,0},{112,16},{1... | collective-permute-start | bytes 983048 | tf_op jit(solution)/shard_map/ppermute | solution.py:26
  83.6 14.7 %collective-permute-start.34 = (bf16[2,16,4096]{2,1,0:T(8,128)(2,1)S(1)}, bf16[2,16,4096]{2,1,0:T(8,128)(2,1)S(1)}, u32[]{:S(2)}, u32[]{:S(2)}) collective-permute-start(bf16[2,16,4096]{2,1,0:T(8,128)(2,1)S(1)} %pad_maximum_fusion.7), channel_id=1, source_target_pairs={{0,384},{16,400},{32,416},{48,432},{64,448},{80,464},{96,480},{112... | collective-permute-start | bytes 786440 | tf_op jit(solution)/shard_map/ppermute | solution.py:26
  88.8 30.3 %collective-permute-start.41 = (bf16[2,64,1280]{2,1,0:T(8,128)(2,1)S(1)}, bf16[2,64,1280]{2,1,0:T(8,128)(2,1)S(1)}, u32[]{:S(2)}, u32[]{:S(2)}) collective-permute-start(bf16[2,64,1280]{2,1,0:T(8,128)(2,1)S(1)} %pad_maximum_fusion.5), channel_id=1, source_target_pairs={{0,96},{16,112},{32,64},{48,80},{64,32},{80,48},{96,0},{112,16},{1... | collective-permute-start | bytes 983048 | tf_op jit(solution)/shard_map/ppermute | solution.py:26
  92.8 20.8 %collective-permute-start.12 = (bf16[4,16,4096]{2,1,0:T(8,128)(2,1)S(1)}, bf16[4,16,4096]{2,1,0:T(8,128)(2,1)S(1)}, u32[]{:S(2)}, u32[]{:S(2)}) collective-permute-start(bf16[4,16,4096]{2,1,0:T(8,128)(2,1)S(1)} %pad_maximum_fusion.2), channel_id=1, source_target_pairs={{0,32},{16,48},{32,0},{48,16},{64,96},{80,112},{96,64},{112,80},{1... | collective-permute-start | bytes 1572872 | tf_op jit(solution)/shard_map/ppermute | solution.py:26
  95.1 13.9 %collective-permute-start.18 = (bf16[4,64,1280]{2,1,0:T(8,128)(2,1)S(1)}, bf16[4,64,1280]{2,1,0:T(8,128)(2,1)S(1)}, u32[]{:S(2)}, u32[]{:S(2)}) collective-permute-start(bf16[4,64,1280]{2,1,0:T(8,128)(2,1)S(1)} %pad_maximum_fusion), channel_id=1, source_target_pairs={{0,128},{16,144},{32,160},{48,176},{64,192},{80,208},{96,224},{112... | collective-permute-start | bytes 1966088 | tf_op jit(solution)/shard_map/ppermute | solution.py:26
  98.4 23.9 %collective-permute-start.35 = (bf16[4,16,4096]{2,1,0:T(8,128)(2,1)S(1)}, bf16[4,16,4096]{2,1,0:T(8,128)(2,1)S(1)}, u32[]{:S(2)}, u32[]{:S(2)}) collective-permute-start(bf16[4,16,4096]{2,1,0:T(8,128)(2,1)S(1)} %pad_maximum_fusion.3), channel_id=1, source_target_pairs={{0,32},{16,48},{32,0},{48,16},{64,96},{80,112},{96,64},{112,80},{1... | collective-permute-start | bytes 1572872 | tf_op jit(solution)/shard_map/ppermute | solution.py:26
  109.1 53.1 %collective-permute-start.19 = (bf16[8,64,1280]{2,1,0:T(8,128)(2,1)S(1)}, bf16[8,64,1280]{2,1,0:T(8,128)(2,1)S(1)}, u32[]{:S(2)}, u32[]{:S(2)}) collective-permute-start(bf16[8,64,1280]{2,1,0:T(8,128)(2,1)S(1)} %constant_dynamic-update-slice_fusion.15.rest_4_), channel_id=1, source_target_pairs={{0,384},{16,400},{32,416},{48,432},{64,448},{80,464},{96,480},{112... | collective-permute-start | bytes 3932168 | tf_op jit(solution)/shard_map/ppermute | solution.py:26
  113.8 44.1 %collective-permute-start.13 = (bf16[8,16,4096]{2,1,0:T(8,128)(2,1)S(1)}, bf16[8,16,4096]{2,1,0:T(8,128)(2,1)S(1)}, u32[]{:S(2)}, u32[]{:S(2)}) collective-permute-start(bf16[8,16,4096]{2,1,0:T(8,128)(2,1)S(1)} %constant_dynamic-update-slice_fusion.11.rest_0_), channel_id=1, source_target_pairs={{0,96},{16,112},{32,64},{48,80},{64,32},{80,48},{96,0},{112,16},{1... | collective-permute-start | bytes 3145736 | tf_op jit(solution)/shard_map/ppermute | solution.py:26
  117.2 42.8 %collective-permute-start.14 = (bf16[8,16,4096]{2,1,0:T(8,128)(2,1)S(1)}, bf16[8,16,4096]{2,1,0:T(8,128)(2,1)S(1)}, u32[]{:S(2)}, u32[]{:S(2)}) collective-permute-start(bf16[8,16,4096]{2,1,0:T(8,128)(2,1)S(1)} %constant_dynamic-update-slice_fusion.11.rest_0_), channel_id=1, source_target_pairs={{0,16},{16,0},{32,48},{48,32},{64,80},{80,64},{96,112},{112,96},{1... | collective-permute-start | bytes 3145736 | tf_op jit(solution)/shard_map/ppermute | solution.py:26
  119.2 20.5 %collective-permute-start.42 = (bf16[4,64,1280]{2,1,0:T(8,128)(2,1)S(1)}, bf16[4,64,1280]{2,1,0:T(8,128)(2,1)S(1)}, u32[]{:S(2)}, u32[]{:S(2)}) collective-permute-start(bf16[4,64,1280]{2,1,0:T(8,128)(2,1)S(1)} %pad_maximum_fusion.1), channel_id=1, source_target_pairs={{0,128},{16,144},{32,160},{48,176},{64,192},{80,208},{96,224},{112... | collective-permute-start | bytes 1966088 | tf_op jit(solution)/shard_map/ppermute | solution.py:26
  122.3 13.8 %collective-permute-start.7 = (bf16[1,24,2048]{2,1,0:T(8,128)(2,1)S(1)}, bf16[1,24,2048]{2,1,0:T(8,128)(2,1)S(1)}, u32[]{:S(2)}, u32[]{:S(2)}) collective-permute-start(bf16[1,24,2048]{2,1,0:T(8,128)(2,1)S(1)} %get-tuple-element.42), channel_id=1, source_target_pairs={{0,12},{1,13},{2,14},{3,15},{4,0},{5,1},{6,2},{7,3},{8,4},{9,5},{1... | collective-permute-start | bytes 294920 | tf_op jit(solution)/shard_map/ppermute | solution.py:22
  136.1 16.0 %collective-permute-start.8 = (bf16[1,24,2048]{2,1,0:T(8,128)(2,1)S(1)}, bf16[1,24,2048]{2,1,0:T(8,128)(2,1)S(1)}, u32[]{:S(2)}, u32[]{:S(2)}) collective-permute-start(bf16[1,24,2048]{2,1,0:T(8,128)(2,1)S(1)} %get-tuple-element.43), channel_id=1, source_target_pairs={{0,5},{1,6},{2,7},{3,8},{4,9},{5,10},{6,11},{7,12},{8,13},{9,14},{... | collective-permute-start | bytes 294920 | tf_op jit(solution)/shard_map/ppermute | solution.py:22
  139.8 16.1 %collective-permute-start.9 = (bf16[1,24,2048]{2,1,0:T(8,128)(2,1)S(1)}, bf16[1,24,2048]{2,1,0:T(8,128)(2,1)S(1)}, u32[]{:S(2)}, u32[]{:S(2)}) collective-permute-start(bf16[1,24,2048]{2,1,0:T(8,128)(2,1)S(1)} %get-tuple-element.44), channel_id=1, source_target_pairs={{0,11},{1,12},{2,13},{3,14},{4,15},{5,0},{6,1},{7,2},{8,3},{9,4},{... | collective-permute-start | bytes 294920 | tf_op jit(solution)/shard_map/ppermute | solution.py:22
  152.1 28.0 %collective-permute-start.36 = (bf16[8,16,4096]{2,1,0:T(8,128)(2,1)S(1)}, bf16[8,16,4096]{2,1,0:T(8,128)(2,1)}, u32[]{:S(2)}, u32[]{:S(2)}) collective-permute-start(bf16[8,16,4096]{2,1,0:T(8,128)(2,1)S(1)} %constant_dynamic-update-slice_fusion.35.rest_0_), channel_id=1, source_target_pairs={{0,96},{16,112},{32,64},{48,80},{64,32},{80,48},{96,0},{112,16},{1... | collective-permute-start | bytes 3145736 | tf_op jit(solution)/shard_map/ppermute | solution.py:26
  155.9 26.2 %collective-permute-start.20 = (bf16[8,64,1280]{2,1,0:T(8,128)(2,1)S(1)}, bf16[8,64,1280]{2,1,0:T(8,128)(2,1)S(1)}, u32[]{:S(2)}, u32[]{:S(2)}) collective-permute-start(bf16[8,64,1280]{2,1,0:T(8,128)(2,1)S(1)} %constant_dynamic-update-slice_fusion.15.rest_4_), channel_id=1, source_target_pairs={{0,16},{16,0},{32,48},{48,32},{64,80},{80,64},{96,112},{112,96},{1... | collective-permute-start | bytes 3932168 | tf_op jit(solution)/shard_map/ppermute | solution.py:26
  157.8 34.3 %collective-permute-start.43 = (bf16[8,64,1280]{2,1,0:T(8,128)(2,1)S(1)}, bf16[8,64,1280]{2,1,0:T(8,128)(2,1)S(1)}, u32[]{:S(2)}, u32[]{:S(2)}) collective-permute-start(bf16[8,64,1280]{2,1,0:T(8,128)(2,1)S(1)} %constant_dynamic-update-slice_fusion.39.rest_4_), channel_id=1, source_target_pairs={{0,384},{16,400},{32,416},{48,432},{64,448},{80,464},{96,480},{112... | collective-permute-start | bytes 3932168 | tf_op jit(solution)/shard_map/ppermute | solution.py:26
  160.0 34.1 %collective-permute-start.15 = (bf16[8,16,4096]{2,1,0:T(8,128)(2,1)S(1)}, bf16[8,16,4096]{2,1,0:T(8,128)(2,1)S(1)}, u32[]{:S(2)}, u32[]{:S(2)}) collective-permute-start(bf16[8,16,4096]{2,1,0:T(8,128)(2,1)S(1)} %collective-permute-done.13.rest_1_), channel_id=1, source_target_pairs={{0,16},{16,0},{32,48},{48,32},{64,80},{80,64},{96,112},{112,96},{1... | collective-permute-start | bytes 3145736 | tf_op jit(solution)/shard_map/ppermute | solution.py:26
  162.2 34.3 %collective-permute-start.21 = (bf16[8,64,1280]{2,1,0:T(8,128)(2,1)S(1)}, bf16[8,64,1280]{2,1,0:T(8,128)(2,1)S(1)}, u32[]{:S(2)}, u32[]{:S(2)}) collective-permute-start(bf16[8,64,1280]{2,1,0:T(8,128)(2,1)S(1)} %collective-permute-done.19.rest_5_), channel_id=1, source_target_pairs={{0,16},{16,0},{32,48},{48,32},{64,80},{80,64},{96,112},{112,96},{1... | collective-permute-start | bytes 3932168 | tf_op jit(solution)/shard_map/ppermute | solution.py:26
  180.1 131.8 %collective-permute-start.37 = (bf16[8,16,4096]{2,1,0:T(8,128)(2,1)S(1)}, bf16[8,16,4096]{2,1,0:T(8,128)(2,1)}, u32[]{:S(2)}, u32[]{:S(2)}) collective-permute-start(bf16[8,16,4096]{2,1,0:T(8,128)(2,1)S(1)} %constant_dynamic-update-slice_fusion.35.rest_0_), channel_id=1, source_target_pairs={{0,16},{16,0},{32,48},{48,32},{64,80},{80,64},{96,112},{112,96},{1... | collective-permute-start | bytes 3145736 | tf_op jit(solution)/shard_map/ppermute | solution.py:26
  182.1 129.8 %collective-permute-start.44 = (bf16[8,64,1280]{2,1,0:T(8,128)(2,1)S(1)}, bf16[8,64,1280]{2,1,0:T(8,128)(2,1)S(1)}, u32[]{:S(2)}, u32[]{:S(2)}) collective-permute-start(bf16[8,64,1280]{2,1,0:T(8,128)(2,1)S(1)} %constant_dynamic-update-slice_fusion.39.rest_4_), channel_id=1, source_target_pairs={{0,16},{16,0},{32,48},{48,32},{64,80},{80,64},{96,112},{112,96},{1... | collective-permute-start | bytes 3932168 | tf_op jit(solution)/shard_map/ppermute | solution.py:26
  192.1 119.8 %collective-permute-start.38 = (bf16[8,16,4096]{2,1,0:T(8,128)(2,1)}, bf16[8,16,4096]{2,1,0:T(8,128)(2,1)}, u32[]{:S(2)}, u32[]{:S(2)}) collective-permute-start(bf16[8,16,4096]{2,1,0:T(8,128)(2,1)} %collective-permute-done.36.rest_1_), channel_id=1, source_target_pairs={{0,16},{16,0},{32,48},{48,32},{64,80},{80,64},{96,112},{112,96},{1... | collective-permute-start | bytes 3145736 | tf_op jit(solution)/shard_map/ppermute | solution.py:26
  194.1 117.9 %collective-permute-start.45 = (bf16[8,64,1280]{2,1,0:T(8,128)(2,1)S(1)}, bf16[8,64,1280]{2,1,0:T(8,128)(2,1)S(1)}, u32[]{:S(2)}, u32[]{:S(2)}) collective-permute-start(bf16[8,64,1280]{2,1,0:T(8,128)(2,1)S(1)} %collective-permute-done.43.rest_5_), channel_id=1, source_target_pairs={{0,16},{16,0},{32,48},{48,32},{64,80},{80,64},{96,112},{112,96},{1... | collective-permute-start | bytes 3932168 | tf_op jit(solution)/shard_map/ppermute | solution.py:26
  208.0 12.3 %collective-permute-start.22 = (bf16[24,2048]{1,0:T(8,128)(2,1)}, bf16[24,2048]{1,0:T(8,128)(2,1)S(1)}, u32[]{:S(2)}, u32[]{:S(2)}) collective-permute-start(bf16[24,2048]{1,0:T(8,128)(2,1)} %get-tuple-element.48), channel_id=1, source_target_pairs={{0,15},{1,0},{2,1},{3,2},{4,3},{5,4},{6,5},{7,6},{8,7},{9,8},{10,9... | collective-permute-start | bytes 294920 | tf_op jit(solution)/shard_map/ppermute | solution.py:22
  227.0 8.1 %collective-permute-start.24 = (bf16[24,2048]{1,0:T(8,128)(2,1)}, bf16[24,2048]{1,0:T(8,128)(2,1)S(1)}, u32[]{:S(2)}, u32[]{:S(2)}) collective-permute-start(bf16[24,2048]{1,0:T(8,128)(2,1)} %get-tuple-element.50), channel_id=1, source_target_pairs={{0,14},{1,15},{2,0},{3,1},{4,2},{5,3},{6,4},{7,5},{8,6},{9,7},{10,... | collective-permute-start | bytes 294920 | tf_op jit(solution)/shard_map/ppermute | solution.py:22
  235.1 9.3 %collective-permute-start.25 = (bf16[24,2048]{1,0:T(8,128)(2,1)}, bf16[24,2048]{1,0:T(8,128)(2,1)S(1)}, u32[]{:S(2)}, u32[]{:S(2)}) collective-permute-start(bf16[24,2048]{1,0:T(8,128)(2,1)} %get-tuple-element.51), channel_id=1, source_target_pairs={{0,2},{1,3},{2,4},{3,5},{4,6},{5,7},{6,8},{7,9},{8,10},{9,11},{10,... | collective-permute-start | bytes 294920 | tf_op jit(solution)/shard_map/ppermute | solution.py:22
  244.4 9.7 %collective-permute-start.26 = (bf16[24,2048]{1,0:T(8,128)(2,1)}, bf16[24,2048]{1,0:T(8,128)(2,1)S(1)}, u32[]{:S(2)}, u32[]{:S(2)}) collective-permute-start(bf16[24,2048]{1,0:T(8,128)(2,1)} %get-tuple-element.52), channel_id=1, source_target_pairs={{0,13},{1,14},{2,15},{3,0},{4,1},{5,2},{6,3},{7,4},{8,5},{9,6},{10... | collective-permute-start | bytes 294920 | tf_op jit(solution)/shard_map/ppermute | solution.py:22
  254.1 11.5 %collective-permute-start.27 = (bf16[24,2048]{1,0:T(8,128)(2,1)}, bf16[24,2048]{1,0:T(8,128)(2,1)S(1)}, u32[]{:S(2)}, u32[]{:S(2)}) collective-permute-start(bf16[24,2048]{1,0:T(8,128)(2,1)} %get-tuple-element.53), channel_id=1, source_target_pairs={{0,3},{1,4},{2,5},{3,6},{4,7},{5,8},{6,9},{7,10},{8,11},{9,12},{10... | collective-permute-start | bytes 294920 | tf_op jit(solution)/shard_map/ppermute | solution.py:22
  265.6 12.0 %collective-permute-start.28 = (bf16[24,2048]{1,0:T(8,128)(2,1)S(1)}, bf16[24,2048]{1,0:T(8,128)(2,1)S(1)}, u32[]{:S(2)}, u32[]{:S(2)}) collective-permute-start(bf16[24,2048]{1,0:T(8,128)(2,1)S(1)} %copy-done.25), channel_id=1, source_target_pairs={{0,12},{1,13},{2,14},{3,15},{4,0},{5,1},{6,2},{7,3},{8,4},{9,5},{1... | collective-permute-start | bytes 294920 | tf_op jit(solution)/shard_map/ppermute | solution.py:22
  277.6 10.5 %collective-permute-start.29 = (bf16[24,2048]{1,0:T(8,128)(2,1)S(1)}, bf16[24,2048]{1,0:T(8,128)(2,1)S(1)}, u32[]{:S(2)}, u32[]{:S(2)}) collective-permute-start(bf16[24,2048]{1,0:T(8,128)(2,1)S(1)} %copy-done.24), channel_id=1, source_target_pairs={{0,4},{1,5},{2,6},{3,7},{4,8},{5,9},{6,10},{7,11},{8,12},{9,13},{1... | collective-permute-start | bytes 294920 | tf_op jit(solution)/shard_map/ppermute | solution.py:22
  288.2 11.6 %collective-permute-start.30 = (bf16[24,2048]{1,0:T(8,128)(2,1)S(1)}, bf16[24,2048]{1,0:T(8,128)(2,1)S(1)}, u32[]{:S(2)}, u32[]{:S(2)}) collective-permute-start(bf16[24,2048]{1,0:T(8,128)(2,1)S(1)} %copy-done.23), channel_id=1, source_target_pairs={{0,11},{1,12},{2,13},{3,14},{4,15},{5,0},{6,1},{7,2},{8,3},{9,4},{... | collective-permute-start | bytes 294920 | tf_op jit(solution)/shard_map/ppermute | solution.py:22
  299.8 11.3 %collective-permute-start.31 = (bf16[24,2048]{1,0:T(8,128)(2,1)S(1)}, bf16[24,2048]{1,0:T(8,128)(2,1)S(1)}, u32[]{:S(2)}, u32[]{:S(2)}) collective-permute-start(bf16[24,2048]{1,0:T(8,128)(2,1)S(1)} %copy-done.22), channel_id=1, source_target_pairs={{0,5},{1,6},{2,7},{3,8},{4,9},{5,10},{6,11},{7,12},{8,13},{9,14},{... | collective-permute-start | bytes 294920 | tf_op jit(solution)/shard_map/ppermute | solution.py:22
  323.3 23.1 %collective-permute-start.46 = (bf16[24,2048]{1,0:T(8,128)(2,1)}, bf16[24,2048]{1,0:T(8,128)(2,1)S(1)}, u32[]{:S(2)}, u32[]{:S(2)}) collective-permute-start(bf16[24,2048]{1,0:T(8,128)(2,1)} %get-tuple-element.59), channel_id=1, source_target_pairs={{0,15},{1,0},{2,1},{3,2},{4,3},{5,4},{6,5},{7,6},{8,7},{9,8},{10,9... | collective-permute-start | bytes 294920 | tf_op jit(solution)/shard_map/ppermute | solution.py:22
  330.4 16.1 %collective-permute-start.47 = (bf16[24,2048]{1,0:T(8,128)(2,1)}, bf16[24,2048]{1,0:T(8,128)(2,1)S(1)}, u32[]{:S(2)}, u32[]{:S(2)}) collective-permute-start(bf16[24,2048]{1,0:T(8,128)(2,1)} %get-tuple-element.60), channel_id=1, source_target_pairs={{0,1},{1,2},{2,3},{3,4},{4,5},{5,6},{6,7},{7,8},{8,9},{9,10},{10,1... | collective-permute-start | bytes 294920 | tf_op jit(solution)/shard_map/ppermute | solution.py:22
  333.3 13.7 %collective-permute-start.48 = (bf16[24,2048]{1,0:T(8,128)(2,1)}, bf16[24,2048]{1,0:T(8,128)(2,1)S(1)}, u32[]{:S(2)}, u32[]{:S(2)}) collective-permute-start(bf16[24,2048]{1,0:T(8,128)(2,1)} %get-tuple-element.61), channel_id=1, source_target_pairs={{0,14},{1,15},{2,0},{3,1},{4,2},{5,3},{6,4},{7,5},{8,6},{9,7},{10,... | collective-permute-start | bytes 294920 | tf_op jit(solution)/shard_map/ppermute | solution.py:22
  344.5 9.2 %collective-permute-start.49 = (bf16[24,2048]{1,0:T(8,128)(2,1)}, bf16[24,2048]{1,0:T(8,128)(2,1)S(1)}, u32[]{:S(2)}, u32[]{:S(2)}) collective-permute-start(bf16[24,2048]{1,0:T(8,128)(2,1)} %get-tuple-element.62), channel_id=1, source_target_pairs={{0,2},{1,3},{2,4},{3,5},{4,6},{5,7},{6,8},{7,9},{8,10},{9,11},{10,... | collective-permute-start | bytes 294920 | tf_op jit(solution)/shard_map/ppermute | solution.py:22
  (29 other events, 795.1 us)
where the time goes:
time: 357 us; the launch traced here: 355 us
  starting transfers between devices  205 us (57%)
  waiting for transfers between devices  112 us (31%)
  Pallas kernels  24.8 us (7%)
  local copies, waits for them, and re-layouts  9.57 us (3%)
    ppermute x26, starting transfers between devices, shift(): lax.ppermute(x, 'expert', [(i, (i + hops) % ring) for i in range(ring)])  138 us
    ppermute x26, waiting for transfers between devices, shift(): lax.ppermute(x, 'expert', [(i, (i + hops) % ring) for i in range(ring)])  80.4 us
    ppermute x24, starting transfers between devices, trade(): lax.ppermute(x, 'dp', [(i, i ^ mask) for i in range(lax.axis_size('dp'))])  67 us
    ppermute x24, waiting for transfers between devices, trade(): lax.ppermute(x, 'dp', [(i, i ^ mask) for i in range(lax.axis_size('dp'))])  31.6 us
    pallas_call x2, Pallas kernels, run_expert(): pl.pallas_call(functools.partial(expert_kernel, cap=cap), out_shape=[jax....  20.1 us
    unnamed x90, local copies, waits for them, and re-layouts  9.26 us
  transfers between devices with their start and end apart: 50, of which 19 were waited for; matrix products, arithmetic and copies ran while one was open for 2% of the time, Pallas kernels for 3%

commit v1 on v0

v1 whole, which is shorter than its diff:
```python
import functools

import jax
import jax.numpy as jnp
from jax import lax
from jax.experimental import pallas as pl
from jax.experimental.pallas import tpu as pltpu
from jax.sharding import PartitionSpec as P

F32, BF16 = jnp.float32, jnp.bfloat16
NT = (((1,), (1,)), ((), ()))
NN = (((1,), (0,)), ((), ()))
VMEM = pl.BlockSpec(memory_space=pltpu.VMEM)
HBM = pl.BlockSpec(memory_space=pltpu.HBM)
ANY = pl.BlockSpec(memory_space=pl.ANY)


def trade(x, mask):
    return lax.ppermute(x, "dp", [(i, i ^ mask) for i in range(lax.axis_size("dp"))])


X_STEPS, Y_STEPS, CORE = (8, 24), (2, 6), 1


def gather(a, b):
    a_steps, b_steps = X_STEPS + Y_STEPS, Y_STEPS + X_STEPS
    for a_mask, b_mask in zip(a_steps[:-1], b_steps[:-1]):
        a_in, b_in = lax.optimization_barrier((trade(a, a_mask), trade(b, b_mask)))
        a, b = jnp.concatenate([a, a_in], axis=0), jnp.concatenate([b, b_in], axis=0)
    a_in, b_in, a_near, b_near = lax.optimization_barrier(
        (trade(a, a_steps[-1]), trade(b, b_steps[-1]), trade(a, CORE), trade(b, CORE))
    )
    return (a, a_in, a_near, trade(a_in, CORE)), (b, b_in, b_near, trade(b_in, CORE))


def gray(k):
    return k ^ (k >> 1)


def place_mask(slot, x_first):
    low, high = gray(slot & 3), gray((slot >> 2) & 3)
    px, py = (low, high) if x_first else (high, low)
    return (px << 3) | (py << 1) | (slot >> 4)


def hidden_order(ff):
    k = jnp.arange(ff, dtype=jnp.int32)[:, None]
    low = jnp.where(k < 512, k & 15, 16 + (k & 7))
    mask = jnp.where(k < 512, place_mask(k >> 4, True), place_mask((k - 512) >> 3, False))
    unit = (mask ^ lax.axis_index("dp")) * 24 + low
    return (unit == jnp.arange(ff, dtype=jnp.int32)[None, :]).astype(BF16)


def pack_kernel(both_ref, down_ref, a_ref, b_ref):
    a_ref[0] = both_ref[:16]
    b_ref[0, :, :768] = down_ref[...]
    for j in range(8):
        b_ref[0, 8 * j : 8 * (j + 1), 768:] = both_ref[16:, 512 * j : 512 * (j + 1)]


def send_kernel(tok_ref, gain_ref, expert_ref, out_ref, *, ring, cap):
    values = tok_ref[...].astype(F32)
    meansq = jnp.mean(values * values, axis=1, keepdims=True)
    normed = (values * lax.rsqrt(meansq + 1e-06) * gain_ref[...]).astype(BF16)
    expert = expert_ref[...]
    count = expert.shape[1]
    member = lax.broadcasted_iota(jnp.int32, (ring, count), 0) == expert
    before = lax.broadcasted_iota(jnp.int32, (count, count), 0) < lax.broadcasted_iota(
        jnp.int32, (count, count), 1
    )
    earlier = lax.dot_general(
        member.astype(F32), before.astype(F32), NN, preferred_element_type=F32
    )
    slot = jnp.sum(jnp.where(member, earlier, 0.0), axis=0, keepdims=True).astype(jnp.int32)
    place = expert * cap + slot
    pick = lax.broadcasted_iota(jnp.int32, (ring * cap, count), 0) == place
    out_ref[...] = lax.dot_general(
        pick.astype(F32).astype(BF16), normed, NN, preferred_element_type=F32
    ).astype(BF16)


def expert_kernel(x_ref, order_ref, *rest):
    pieces_a, pieces_b = rest[:4], rest[4:8]
    out_ref, wa, wb, wd, hid, sem_a, sem_b, sem_d = rest[8:]
    width = x_ref.shape[1]
    me = lax.axis_index("dp")
    each = pieces_a[0].shape[0]
    copies_a = [
        pltpu.make_async_copy(piece, wa.at[pl.ds(each * q, each)], sem_a.at[q])
        for q, piece in enumerate(pieces_a)
    ]
    copies_b, copies_d = [], []
    for q, piece in enumerate(pieces_b):
        for j in range(8):
            copies_b.append(
                pltpu.make_async_copy(
                    piece.at[:, pl.ds(8 * j, 8), pl.ds(768, 512)],
                    wb.at[pl.ds(each * q, each), :, pl.ds(512 * j, 512)],
                    sem_b.at[8 * q + j],
                )
            )
        for p in range(each):
            slot = each * q + p
            copies_d.append(
                pltpu.make_async_copy(
                    piece.at[p, :, pl.ds(0, 768)],
                    wd.at[me ^ place_mask(slot, False)],
                    sem_d.at[slot],
                )
            )
    for copy in copies_a + copies_b + copies_d:
        copy.start()
    x = x_ref[...]

    def units(w, cols):
        gate = lax.dot_general(x, w[:, :width], NT, preferred_element_type=F32)
        upper = lax.dot_general(x, w[:, width:], NT, preferred_element_type=F32)
        hid[:, cols] = (gate / (1.0 + jnp.exp(-gate)) * upper).astype(BF16)

    half = 2 * each * 16
    for c in range(2):
        copies_a[2 * c].wait()
        copies_a[2 * c + 1].wait()
        units(wa[2 * each * c : 2 * each * (c + 1)].reshape(half, 2 * width), slice(half * c, half * (c + 1)))
    for copy in copies_b:
        copy.wait()
    units(wb[...].reshape(256, 2 * width), slice(2 * half, 2 * half + 256))
    hidden = lax.dot_general(hid[...], order_ref[...], NN, preferred_element_type=F32).astype(BF16)
    for copy in copies_d:
        copy.wait()
    shards, feats, ff = wd.shape
    group = 8
    for n in range(shards // group):
        down = wd[group * n : group * (n + 1)].reshape(group * feats, ff)
        made = lax.dot_general(hidden, down, NT, preferred_element_type=F32)
        cols = slice(group * feats * n, group * feats * (n + 1))
        out_ref[:, cols] = made.astype(BF16)


def run_expert(x, order, pieces_a, pieces_b):
    rows, width = x.shape
    ff = order.shape[0]
    shards = 4 * pieces_a[0].shape[0]
    return pl.pallas_call(
        expert_kernel,
        out_shape=jax.ShapeDtypeStruct((rows, width), BF16),
        in_specs=[VMEM, VMEM] + [ANY] * 8,
        out_specs=VMEM,
        scratch_shapes=[
            pltpu.VMEM((shards, 16, 2 * width), BF16),
            pltpu.VMEM((shards, 8, 2 * width), BF16),
            pltpu.VMEM((shards, width // shards, ff), BF16),
            pltpu.VMEM((rows, ff), BF16),
            pltpu.SemaphoreType.DMA((4,)),
            pltpu.SemaphoreType.DMA((32,)),
            pltpu.SemaphoreType.DMA((32,)),
        ],
        compiler_params=pltpu.CompilerParams(vmem_limit_bytes=55 << 20),
        cost_estimate=pl.CostEstimate(
            flops=6 * rows * width * ff,
            bytes_accessed=6 * width * ff + 4 * x.size,
            transcendentals=rows * ff,
        ),
        name="expert",
    )(x, order, *pieces_a, *pieces_b)


def last_kernel(expert_ref, probs_ref, x_ref, out_ref, *, ring, cap):
    expert = expert_ref[...]
    count = expert.shape[0]
    member = lax.broadcasted_iota(jnp.int32, (count, ring), 1) == expert
    before = lax.broadcasted_iota(jnp.int32, (count, count), 1) < lax.broadcasted_iota(
        jnp.int32, (count, count), 0
    )
    earlier = lax.dot_general(
        before.astype(F32), member.astype(F32), NN, preferred_element_type=F32
    )
    slot = jnp.sum(jnp.where(member, earlier, 0.0), axis=1, keepdims=True).astype(jnp.int32)
    place = expert * cap + slot
    pick = lax.broadcasted_iota(jnp.int32, (count, ring * cap), 1) == place
    probs = probs_ref[...]
    share = probs[:, :1] / jnp.sum(probs, axis=1, keepdims=True)
    got = lax.dot_general(
        pick.astype(F32).astype(BF16), x_ref[...], NN, preferred_element_type=F32
    )
    out_ref[...] = (share * got).astype(BF16)


def exchange(x, ring):
    blocks = x.reshape(ring, x.shape[0] // ring, x.shape[1])
    return lax.all_to_all(blocks, "expert", split_axis=0, concat_axis=0, tiled=True).reshape(x.shape)


def local(tokens, norm_gain, route_probs, window_expert, w_gate_up, w_down):
    tok_count, width = tokens.shape
    ring = lax.axis_size("expert")
    cap = 3 * tok_count // ring
    rows = ring * cap
    ff = w_down.shape[2]
    sent = pl.pallas_call(
        functools.partial(send_kernel, ring=ring, cap=cap),
        out_shape=jax.ShapeDtypeStruct((rows, width), BF16),
        in_specs=[VMEM] * 3,
        out_specs=VMEM,
        compiler_params=pltpu.CompilerParams(vmem_limit_bytes=20 << 20),
        cost_estimate=pl.CostEstimate(
            flops=6 * tok_count * tok_count * width,
            bytes_accessed=8 * tokens.size,
            transcendentals=0,
        ),
        name="send",
    )(tokens, norm_gain[None, :], window_expert[None, :])
    x = exchange(sent, ring)
    mine_a, mine_b = pl.pallas_call(
        pack_kernel,
        out_shape=[
            jax.ShapeDtypeStruct((1, 16, 2 * width), BF16),
            jax.ShapeDtypeStruct((1, 64, 1280), BF16),
        ],
        in_specs=[VMEM] * 2,
        out_specs=[VMEM] * 2,
        name="pack",
    )(w_gate_up[0], w_down[0])
    made = run_expert(x, hidden_order(ff), *gather(mine_a, mine_b))
    return pl.pallas_call(
        functools.partial(last_kernel, ring=ring, cap=cap),
        out_shape=jax.ShapeDtypeStruct((tok_count, width), BF16),
        in_specs=[VMEM] * 3,
        out_specs=VMEM,
        cost_estimate=pl.CostEstimate(
            flops=6 * tok_count * tok_count * width, bytes_accessed=8 * tokens.size, transcendentals=0
        ),
        compiler_params=pltpu.CompilerParams(vmem_limit_bytes=16 << 20),
        name="last",
    )(window_expert[:, None], route_probs, exchange(made, ring))


def solution(mesh):
    placed = (
        P(("dp", "expert"), None),
        P(),
        P(("dp", "expert"), None),
        P(("dp", "expert")),
        P("expert", "dp", None),
        P("expert", "dp", None),
    )
    return jax.shard_map(
        local, mesh=mesh, in_specs=placed, out_specs=P(("dp", "expert"), None), check_vma=False
    )
```

time: 357 us -> 201 us (0.56)
  the two profiles are of different devices: /device:TPU:38 before, /device:TPU:32 now
where the time goes in v1:
time: 201 us; the launch traced here: 200 us
  waiting for transfers between devices  115 us (57%)
  starting transfers between devices  62.2 us (31%)
  Pallas kernels  17 us (8%)
  local copies, waits for them, and re-layouts  3.98 us (2%)
    all_to_all x2, waiting for transfers between devices, exchange(): lax.all_to_all(blocks, 'expert', split_axis=0, concat_axis=0, tiled=True)  73.3 us
    ppermute x12, waiting for transfers between devices, trade(): lax.ppermute(x, 'dp', [(i, i ^ mask) for i in range(lax.axis_size('dp'))])  42 us
    ppermute x12, starting transfers between devices, trade(): lax.ppermute(x, 'dp', [(i, i ^ mask) for i in range(lax.axis_size('dp'))])  34.8 us
    all_to_all x2, starting transfers between devices, exchange(): lax.all_to_all(blocks, 'expert', split_axis=0, concat_axis=0, tiled=True)  27.4 us
    pallas_call x1, Pallas kernels, run_expert(): pl.pallas_call(expert_kernel, out_shape=jax.ShapeDtypeStruct((rows, width...  11.8 us
  transfers between devices with their start and end apart: 14, of which 6 were waited for; matrix products, arithmetic and copies ran while one was open for 1% of the time, Pallas kernels for 0%

profile of v1, /device:TPU:32, one launch (start us, length us, event | category | flops | bytes accessed | tf_op | source)
XLA Modules:
  0.0 200.5 jit_solution(9061791633213688679)
XLA Ops:
  0.0 1.7 pack.1
  1.7 3.5 %collective-permute-start.1 = (bf16[1,64,1280]{2,1,0:T(8,128)(2,1)}, bf16[1,64,1280]{2,1,0:T(8,128)(2,1)S(1)}, u32[]{:S(2)}, u32[]{:S(2)}) collective-permute-start(bf16[1,64,1280]{2,1,0:T(8,128)(2,1)} %get-tuple-element.18), channel_id=1, source_target_pairs={{0,32},{16,48},{32,0},{48,16},{64,96},{80,112},{96,64},{112,80},{1... | collective-permute-start | bytes 491528 | tf_op jit(solution)/shard_map/ppermute | solution.py:19
  5.2 3.4 %collective-permute-start = (bf16[1,16,4096]{2,1,0:T(8,128)(2,1)}, bf16[1,16,4096]{2,1,0:T(8,128)(2,1)S(1)}, u32[]{:S(2)}, u32[]{:S(2)}) collective-permute-start(bf16[1,16,4096]{2,1,0:T(8,128)(2,1)} %get-tuple-element.17), channel_id=1, source_target_pairs={{0,128},{16,144},{32,160},{48,176},{64,192},{80,208},{96,224},{112... | collective-permute-start | bytes 393224 | tf_op jit(solution)/shard_map/ppermute | solution.py:19
  8.6 0.0 copy-start
  8.6 1.0 copy-done
  9.6 0.7 copy-done.1
  10.3 0.7 copy-done.2
  11.0 1.9 send.1
  12.9 15.3 %all-to-all-start = ((bf16[16,24,2048]{2,1,0:T(8,128)(2,1)}), bf16[16,24,2048]{2,1,0:T(8,128)(2,1)S(1)}, u32[]{:S(2)}, u32[]{:S(2)}) async-start(bf16[16,24,2048]{2,1,0:T(8,128)(2,1)} %bitcast.3), calls=%async_computation | async-start | bytes 3145728 | tf_op jit(solution)/shard_map/all_to_all | solution.py:191
  28.3 0.0 copy-done.6
  28.3 0.0 collective-permute-done
  28.3 0.0 collective-permute-done.1
  28.4 4.1 %collective-permute-start.3 = (bf16[2,64,1280]{2,1,0:T(8,128)(2,1)S(1)}, bf16[2,64,1280]{2,1,0:T(8,128)(2,1)S(1)}, u32[]{:S(2)}, u32[]{:S(2)}) collective-permute-start(bf16[2,64,1280]{2,1,0:T(8,128)(2,1)S(1)} %pad_maximum_fusion.2), channel_id=1, source_target_pairs={{0,96},{16,112},{32,64},{48,80},{64,32},{80,48},{96,0},{112,16},{1... | collective-permute-start | bytes 983048 | tf_op jit(solution)/shard_map/ppermute | solution.py:19
  32.5 4.0 %collective-permute-start.2 = (bf16[2,16,4096]{2,1,0:T(8,128)(2,1)S(1)}, bf16[2,16,4096]{2,1,0:T(8,128)(2,1)S(1)}, u32[]{:S(2)}, u32[]{:S(2)}) collective-permute-start(bf16[2,16,4096]{2,1,0:T(8,128)(2,1)S(1)} %pad_maximum_fusion.3), channel_id=1, source_target_pairs={{0,384},{16,400},{32,416},{48,432},{64,448},{80,464},{96,480},{112... | collective-permute-start | bytes 786440 | tf_op jit(solution)/shard_map/ppermute | solution.py:19
  36.6 5.7 %collective-permute-done.2 = bf16[2,16,4096]{2,1,0:T(8,128)(2,1)S(1)} collective-permute-done((bf16[2,16,4096]{2,1,0:T(8,128)(2,1)S(1)}, bf16[2,16,4096]{2,1,0:T(8,128)(2,1)S(1)}, u32[]{:S(2)}, u32[]{:S(2)}) %collective-permute-start.2) | collective-permute-done | bytes 262176 | tf_op jit(solution)/shard_map/ppermute | solution.py:19
  42.3 0.0 collective-permute-done.3
  42.3 0.1 pad_maximum_fusion
  42.3 1.9 collective-permute-start.5
  44.3 0.1 pad_maximum_fusion.1
  44.3 2.6 %collective-permute-start.4 = (bf16[4,16,4096]{2,1,0:T(8,128)(2,1)S(1)}, bf16[4,16,4096]{2,1,0:T(8,128)(2,1)S(1)}, u32[]{:S(2)}, u32[]{:S(2)}) collective-permute-start(bf16[4,16,4096]{2,1,0:T(8,128)(2,1)S(1)} %pad_maximum_fusion.1), channel_id=1, source_target_pairs={{0,32},{16,48},{32,0},{48,16},{64,96},{80,112},{96,64},{112,80},{1... | collective-permute-start | bytes 1572872 | tf_op jit(solution)/shard_map/ppermute | solution.py:19
  47.0 10.6 %collective-permute-done.4 = bf16[4,16,4096]{2,1,0:T(8,128)(2,1)S(1)} collective-permute-done((bf16[4,16,4096]{2,1,0:T(8,128)(2,1)S(1)}, bf16[4,16,4096]{2,1,0:T(8,128)(2,1)S(1)}, u32[]{:S(2)}, u32[]{:S(2)}) %collective-permute-start.4) | collective-permute-done | bytes 524320 | tf_op jit(solution)/shard_map/ppermute | solution.py:19
  57.6 0.8 collective-permute-done.5
  58.4 4.0 %collective-permute-start.7 = (bf16[8,64,1280]{2,1,0:T(8,128)(2,1)S(1)}, bf16[8,64,1280]{2,1,0:T(8,128)(2,1)}, u32[]{:S(2)}, u32[]{:S(2)}) collective-permute-start(bf16[8,64,1280]{2,1,0:T(8,128)(2,1)S(1)} %constant_dynamic-update-slice_fusion.4.rest_4_), channel_id=1, source_target_pairs={{0,384},{16,400},{32,416},{48,432},{64,448},{80,464},{96,480},{112... | collective-permute-start | bytes 3932168 | tf_op jit(solution)/shard_map/ppermute | solution.py:19
  62.5 1.9 collective-permute-start.9
  64.4 3.0 %collective-permute-start.6 = (bf16[8,16,4096]{2,1,0:T(8,128)(2,1)S(1)}, bf16[8,16,4096]{2,1,0:T(8,128)(2,1)}, u32[]{:S(2)}, u32[]{:S(2)}) collective-permute-start(bf16[8,16,4096]{2,1,0:T(8,128)(2,1)S(1)} %constant_dynamic-update-slice_fusion.rest_0_), channel_id=1, source_target_pairs={{0,96},{16,112},{32,64},{48,80},{64,32},{80,48},{96,0},{112,16},{1... | collective-permute-start | bytes 3145736 | tf_op jit(solution)/shard_map/ppermute | solution.py:19
  67.4 2.1 %collective-permute-start.8 = (bf16[8,16,4096]{2,1,0:T(8,128)(2,1)S(1)}, bf16[8,16,4096]{2,1,0:T(8,128)(2,1)S(1)}, u32[]{:S(2)}, u32[]{:S(2)}) collective-permute-start(bf16[8,16,4096]{2,1,0:T(8,128)(2,1)S(1)} %constant_dynamic-update-slice_fusion.rest_0_), channel_id=1, source_target_pairs={{0,16},{16,0},{32,48},{48,32},{64,80},{80,64},{96,112},{112,96},{1... | collective-permute-start | bytes 3145736 | tf_op jit(solution)/shard_map/ppermute | solution.py:19
  69.6 23.7 %collective-permute-done.6.rest_1_ = bf16[8,16,4096]{2,1,0:T(8,128)(2,1)} collective-permute-done((bf16[8,16,4096]{2,1,0:T(8,128)(2,1)S(1)}, bf16[8,16,4096]{2,1,0:T(8,128)(2,1)}, u32[]{:S(2)}, u32[]{:S(2)}) %collective-permute-start.6) | collective-permute-done | bytes 1048608 | tf_op jit(solution)/shard_map/ppermute | solution.py:19
  93.2 0.0 collective-permute-done.8.rest_2_
  93.2 0.0 collective-permute-done.7.rest_5_
  93.2 0.0 collective-permute-done.9.rest_6_
  93.3 1.9 collective-permute-start.11
  95.2 0.0 copy-done.8
  95.2 2.4 %collective-permute-start.10 = (bf16[8,16,4096]{2,1,0:T(8,128)(2,1)}, bf16[8,16,4096]{2,1,0:T(8,128)(2,1)}, u32[]{:S(2)}, u32[]{:S(2)}) collective-permute-start(bf16[8,16,4096]{2,1,0:T(8,128)(2,1)} %collective-permute-done.6.rest_1_), channel_id=1, source_target_pairs={{0,16},{16,0},{32,48},{48,32},{64,80},{80,64},{96,112},{112,96},{1... | collective-permute-start | bytes 3145736 | tf_op jit(solution)/shard_map/ppermute | solution.py:19
  97.6 0.0 copy-done.10
  97.6 1.4 fusion.order_ref
  99.0 1.2 collective-permute-done.10.rest_3_
  100.2 0.0 collective-permute-done.11.rest_7_
  100.2 0.0 all-to-all-done
  100.2 1.2 copy-done.4
  101.4 11.8 %expert.1 = bf16[384,2048]{1,0:T(8,128)(2,1)} custom-call(bf16[384,2048]{1,0:T(8,128)(2,1)} %bitcast.13, bf16[768,768]{1,0:T(8,128)(2,1)} %fusion.order_ref, bf16[8,16,4096]{2,1,0:T(8,128)(2,1)} %copy-done.7, bf16[8,16,4096]{2,1,0:T(8,128)(2,1)} %collective-permute-done.6.rest_1_, bf16[8,16,4096]{2,1,0:T(8,128)(2,1)} %copy-done.10, ...), custom_call_target="tpu_custom_call" | custom-call | flops 3623878656 | bytes 12582912 | tf_op jit(solution)/shard_map/expert/pallas_call | solution.py:144
  113.3 0.0 copy-start.3
  113.3 0.0 copy-start.11
  113.3 12.1 %all-to-all-start.1 = ((bf16[16,24,2048]{2,1,0:T(8,128)(2,1)}), bf16[16,24,2048]{2,1,0:T(8,128)(2,1)S(1)}, u32[]{:S(2)}, u32[]{:S(2)}) async-start(bf16[16,24,2048]{2,1,0:T(8,128)(2,1)} %bitcast.14), calls=%async_computation.1 | async-start | bytes 3145728 | tf_op jit(solution)/shard_map/all_to_all | solution.py:191
  125.3 0.1 copy.7.expert_ref
  125.5 0.0 copy-done.11
  125.5 0.1 copy.8.probs_ref
  125.6 73.3 %all-to-all-done.1 = bf16[16,24,2048]{2,1,0:T(8,128)(2,1)S(1)} async-done(((bf16[16,24,2048]{2,1,0:T(8,128)(2,1)}), bf16[16,24,2048]{2,1,0:T(8,128)(2,1)S(1)}, u32[]{:S(2)}, u32[]{:S(2)}) %all-to-all-start.1) | async-done | bytes 1572896 | tf_op jit(solution)/shard_map/all_to_all | solution.py:191
  198.9 1.6 last.1
  (24 shorter events, 0.3 us)
Async XLA Ops:
  1.7 26.6 %collective-permute-start.1 = (bf16[1,64,1280]{2,1,0:T(8,128)(2,1)}, bf16[1,64,1280]{2,1,0:T(8,128)(2,1)S(1)}, u32[]{:S(2)}, u32[]{:S(2)}) collective-permute-start(bf16[1,64,1280]{2,1,0:T(8,128)(2,1)} %get-tuple-element.18), channel_id=1, source_target_pairs={{0,32},{16,48},{32,0},{48,16},{64,96},{80,112},{96,64},{112,80},{1... | collective-permute-start | bytes 491528 | tf_op jit(solution)/shard_map/ppermute | solution.py:19
  5.2 23.1 %collective-permute-start = (bf16[1,16,4096]{2,1,0:T(8,128)(2,1)}, bf16[1,16,4096]{2,1,0:T(8,128)(2,1)S(1)}, u32[]{:S(2)}, u32[]{:S(2)}) collective-permute-start(bf16[1,16,4096]{2,1,0:T(8,128)(2,1)} %get-tuple-element.17), channel_id=1, source_target_pairs={{0,128},{16,144},{32,160},{48,176},{64,192},{80,208},{96,224},{112... | collective-permute-start | bytes 393224 | tf_op jit(solution)/shard_map/ppermute | solution.py:19
  8.6 1.0 copy-start
  9.6 0.7 copy-start.1
  10.3 0.7 copy-start.2
  12.9 15.3 %copy-start.9 = (bf16[1,16,4096]{2,1,0:T(8,128)(2,1)S(1)}, bf16[1,16,4096]{2,1,0:T(8,128)(2,1)}, u32[]{:S(2)}) copy-start(bf16[1,16,4096]{2,1,0:T(8,128)(2,1)} %get-tuple-element.17) | copy-start | bytes 393220
  12.9 15.4 %copy-start.6 = (bf16[1,64,1280]{2,1,0:T(8,128)(2,1)S(1)}, bf16[1,64,1280]{2,1,0:T(8,128)(2,1)}, u32[]{:S(2)}) copy-start(bf16[1,64,1280]{2,1,0:T(8,128)(2,1)} %get-tuple-element.18) | copy-start | bytes 491524
  12.9 87.3 %all-to-all-start = ((bf16[16,24,2048]{2,1,0:T(8,128)(2,1)}), bf16[16,24,2048]{2,1,0:T(8,128)(2,1)S(1)}, u32[]{:S(2)}, u32[]{:S(2)}) async-start(bf16[16,24,2048]{2,1,0:T(8,128)(2,1)} %bitcast.3), calls=%async_computation | async-start | bytes 3145728 | tf_op jit(solution)/shard_map/all_to_all | solution.py:191
  28.4 13.9 %collective-permute-start.3 = (bf16[2,64,1280]{2,1,0:T(8,128)(2,1)S(1)}, bf16[2,64,1280]{2,1,0:T(8,128)(2,1)S(1)}, u32[]{:S(2)}, u32[]{:S(2)}) collective-permute-start(bf16[2,64,1280]{2,1,0:T(8,128)(2,1)S(1)} %pad_maximum_fusion.2), channel_id=1, source_target_pairs={{0,96},{16,112},{32,64},{48,80},{64,32},{80,48},{96,0},{112,16},{1... | collective-permute-start | bytes 983048 | tf_op jit(solution)/shard_map/ppermute | solution.py:19
  32.5 9.7 %collective-permute-start.2 = (bf16[2,16,4096]{2,1,0:T(8,128)(2,1)S(1)}, bf16[2,16,4096]{2,1,0:T(8,128)(2,1)S(1)}, u32[]{:S(2)}, u32[]{:S(2)}) collective-permute-start(bf16[2,16,4096]{2,1,0:T(8,128)(2,1)S(1)} %pad_maximum_fusion.3), channel_id=1, source_target_pairs={{0,384},{16,400},{32,416},{48,432},{64,448},{80,464},{96,480},{112... | collective-permute-start | bytes 786440 | tf_op jit(solution)/shard_map/ppermute | solution.py:19
  42.3 16.0 %collective-permute-start.5 = (bf16[4,64,1280]{2,1,0:T(8,128)(2,1)S(1)}, bf16[4,64,1280]{2,1,0:T(8,128)(2,1)S(1)}, u32[]{:S(2)}, u32[]{:S(2)}) collective-permute-start(bf16[4,64,1280]{2,1,0:T(8,128)(2,1)S(1)} %pad_maximum_fusion), channel_id=1, source_target_pairs={{0,128},{16,144},{32,160},{48,176},{64,192},{80,208},{96,224},{112... | collective-permute-start | bytes 1966088 | tf_op jit(solution)/shard_map/ppermute | solution.py:19
  44.3 13.2 %collective-permute-start.4 = (bf16[4,16,4096]{2,1,0:T(8,128)(2,1)S(1)}, bf16[4,16,4096]{2,1,0:T(8,128)(2,1)S(1)}, u32[]{:S(2)}, u32[]{:S(2)}) collective-permute-start(bf16[4,16,4096]{2,1,0:T(8,128)(2,1)S(1)} %pad_maximum_fusion.1), channel_id=1, source_target_pairs={{0,32},{16,48},{32,0},{48,16},{64,96},{80,112},{96,64},{112,80},{1... | collective-permute-start | bytes 1572872 | tf_op jit(solution)/shard_map/ppermute | solution.py:19
  58.4 41.8 %copy-start.5 = (bf16[8,64,1280]{2,1,0:T(8,128)(2,1)}, bf16[8,64,1280]{2,1,0:T(8,128)(2,1)S(1)}, u32[]{:S(2)}) copy-start(bf16[8,64,1280]{2,1,0:T(8,128)(2,1)S(1)} %constant_dynamic-update-slice_fusion.4.rest_4_) | copy-start | bytes 3932164
  58.4 34.8 %collective-permute-start.7 = (bf16[8,64,1280]{2,1,0:T(8,128)(2,1)S(1)}, bf16[8,64,1280]{2,1,0:T(8,128)(2,1)}, u32[]{:S(2)}, u32[]{:S(2)}) collective-permute-start(bf16[8,64,1280]{2,1,0:T(8,128)(2,1)S(1)} %constant_dynamic-update-slice_fusion.4.rest_4_), channel_id=1, source_target_pairs={{0,384},{16,400},{32,416},{48,432},{64,448},{80,464},{96,480},{112... | collective-permute-start | bytes 3932168 | tf_op jit(solution)/shard_map/ppermute | solution.py:19
  62.5 30.8 %collective-permute-start.9 = (bf16[8,64,1280]{2,1,0:T(8,128)(2,1)S(1)}, bf16[8,64,1280]{2,1,0:T(8,128)(2,1)S(1)}, u32[]{:S(2)}, u32[]{:S(2)}) collective-permute-start(bf16[8,64,1280]{2,1,0:T(8,128)(2,1)S(1)} %constant_dynamic-update-slice_fusion.4.rest_4_), channel_id=1, source_target_pairs={{0,16},{16,0},{32,48},{48,32},{64,80},{80,64},{96,112},{112,96},{1... | collective-permute-start | bytes 3932168 | tf_op jit(solution)/shard_map/ppermute | solution.py:19
  64.4 28.8 %copy-start.7 = (bf16[8,16,4096]{2,1,0:T(8,128)(2,1)}, bf16[8,16,4096]{2,1,0:T(8,128)(2,1)S(1)}, u32[]{:S(2)}) copy-start(bf16[8,16,4096]{2,1,0:T(8,128)(2,1)S(1)} %constant_dynamic-update-slice_fusion.rest_0_) | copy-start | bytes 3145732
  64.4 28.8 %collective-permute-start.6 = (bf16[8,16,4096]{2,1,0:T(8,128)(2,1)S(1)}, bf16[8,16,4096]{2,1,0:T(8,128)(2,1)}, u32[]{:S(2)}, u32[]{:S(2)}) collective-permute-start(bf16[8,16,4096]{2,1,0:T(8,128)(2,1)S(1)} %constant_dynamic-update-slice_fusion.rest_0_), channel_id=1, source_target_pairs={{0,96},{16,112},{32,64},{48,80},{64,32},{80,48},{96,0},{112,16},{1... | collective-permute-start | bytes 3145736 | tf_op jit(solution)/shard_map/ppermute | solution.py:19
  67.4 25.8 %collective-permute-start.8 = (bf16[8,16,4096]{2,1,0:T(8,128)(2,1)S(1)}, bf16[8,16,4096]{2,1,0:T(8,128)(2,1)S(1)}, u32[]{:S(2)}, u32[]{:S(2)}) collective-permute-start(bf16[8,16,4096]{2,1,0:T(8,128)(2,1)S(1)} %constant_dynamic-update-slice_fusion.rest_0_), channel_id=1, source_target_pairs={{0,16},{16,0},{32,48},{48,32},{64,80},{80,64},{96,112},{112,96},{1... | collective-permute-start | bytes 3145736 | tf_op jit(solution)/shard_map/ppermute | solution.py:19
  93.2 4.4 %copy-start.10 = (bf16[8,16,4096]{2,1,0:T(8,128)(2,1)}, bf16[8,16,4096]{2,1,0:T(8,128)(2,1)S(1)}, u32[]{:S(2)}) copy-start(bf16[8,16,4096]{2,1,0:T(8,128)(2,1)S(1)} %collective-permute-done.8.rest_2_) | copy-start | bytes 3145732
  93.2 1.9 copy-start.8
  93.3 7.0 %collective-permute-start.11 = (bf16[8,64,1280]{2,1,0:T(8,128)(2,1)}, bf16[8,64,1280]{2,1,0:T(8,128)(2,1)}, u32[]{:S(2)}, u32[]{:S(2)}) collective-permute-start(bf16[8,64,1280]{2,1,0:T(8,128)(2,1)} %collective-permute-done.7.rest_5_), channel_id=1, source_target_pairs={{0,16},{16,0},{32,48},{48,32},{64,80},{80,64},{96,112},{112,96},{1... | collective-permute-start | bytes 3932168 | tf_op jit(solution)/shard_map/ppermute | solution.py:19
  95.2 5.0 %collective-permute-start.10 = (bf16[8,16,4096]{2,1,0:T(8,128)(2,1)}, bf16[8,16,4096]{2,1,0:T(8,128)(2,1)}, u32[]{:S(2)}, u32[]{:S(2)}) collective-permute-start(bf16[8,16,4096]{2,1,0:T(8,128)(2,1)} %collective-permute-done.6.rest_1_), channel_id=1, source_target_pairs={{0,16},{16,0},{32,48},{48,32},{64,80},{80,64},{96,112},{112,96},{1... | collective-permute-start | bytes 3145736 | tf_op jit(solution)/shard_map/ppermute | solution.py:19
  100.2 1.2 copy-start.4
  113.3 12.1 %copy-start.3 = (s32[128]{0:T(128)S(1)}, s32[128]{0:T(128)}, u32[]{:S(2)}) copy-start(s32[128]{0:T(128)} %param.9) | copy-start | bytes 1540
  113.3 12.2 %copy-start.11 = (f32[128,8]{0,1:T(8,128)S(1)}, f32[128,8]{0,1:T(8,128)}, u32[]{:S(2)}) copy-start(f32[128,8]{0,1:T(8,128)} %param.8) | copy-start | bytes 12292
  113.3 85.6 %all-to-all-start.1 = ((bf16[16,24,2048]{2,1,0:T(8,128)(2,1)}), bf16[16,24,2048]{2,1,0:T(8,128)(2,1)S(1)}, u32[]{:S(2)}, u32[]{:S(2)}) async-start(bf16[16,24,2048]{2,1,0:T(8,128)(2,1)} %bitcast.14), calls=%async_computation.1 | async-start | bytes 3145728 | tf_op jit(solution)/shard_map/all_to_all | solution.py:191

commit v2 on v1

--- a/solution.py
+++ b/solution.py
@@ -2,6 +2,7 @@
 
 import jax
 import jax.numpy as jnp
+import numpy as np
 from jax import lax
 from jax.experimental import pallas as pl
 from jax.experimental.pallas import tpu as pltpu
@@ -15,40 +16,71 @@
 ANY = pl.BlockSpec(memory_space=pl.ANY)
 
 
-def trade(x, mask):
-    return lax.ppermute(x, "dp", [(i, i ^ mask) for i in range(lax.axis_size("dp"))])
-
-
-X_STEPS, Y_STEPS, CORE = (8, 24), (2, 6), 1
+def trade(x, where):
+    return lax.ppermute(x, "dp", [(i, where(i)) for i in range(lax.axis_size("dp"))])
+
+
+def flip(mask):
+    return lambda i: i ^ mask
+
+
+def turn(bit, hops):
+    return lambda i: (i & ~(3 << bit)) | ((((i >> bit) + hops) & 3) << bit)
+
+
+X_BIT, Y_BIT, CORE = 3, 1, 1
+GRAY = (0, 1, 3, 2)
+TURNS = (0, -1, 1, 2)
 
 
 def gather(a, b):
-    a_steps, b_steps = X_STEPS + Y_STEPS, Y_STEPS + X_STEPS
-    for a_mask, b_mask in zip(a_steps[:-1], b_steps[:-1]):
-        a_in, b_in = lax.optimization_barrier((trade(a, a_mask), trade(b, b_mask)))
+    for step in (1, 3):
+        a_in, b_in = lax.optimization_barrier(
+            (trade(a, flip(step << X_BIT)), trade(b, flip(step << Y_BIT)))
+        )
         a, b = jnp.concatenate([a, a_in], axis=0), jnp.concatenate([b, b_in], axis=0)
-    a_in, b_in, a_near, b_near = lax.optimization_barrier(
-        (trade(a, a_steps[-1]), trade(b, b_steps[-1]), trade(a, CORE), trade(b, CORE))
-    )
-    return (a, a_in, a_near, trade(a_in, CORE)), (b, b_in, b_near, trade(b_in, CORE))
-
-
-def gray(k):
-    return k ^ (k >> 1)
-
-
-def place_mask(slot, x_first):
-    low, high = gray(slot & 3), gray((slot >> 2) & 3)
-    px, py = (low, high) if x_first else (high, low)
-    return (px << 3) | (py << 1) | (slot >> 4)
+    a_l, b_l, a_r, b_r = lax.optimization_barrier(
+        (
+            trade(a, turn(Y_BIT, 1)),
+            trade(b, turn(X_BIT, 1)),
+            trade(a, turn(Y_BIT, -1)),
+            trade(b, turn(X_BIT, -1)),
+        )
+    )
+    a12, b12 = jnp.concatenate([a, a_l, a_r], axis=0), jnp.concatenate([b, b_l, b_r], axis=0)
+    a_0, b_0, a_1, b_1 = (
+        trade(a_l[:2], turn(Y_BIT, 1)),
+        trade(b_l[:2], turn(X_BIT, 1)),
+        trade(a_r[2:], turn(Y_BIT, -1)),
+        trade(b_r[2:], turn(X_BIT, -1)),
+    )
+    a4, b4 = jnp.concatenate([a_0, a_1], axis=0), jnp.concatenate([b_0, b_1], axis=0)
+    near = flip(CORE)
+    return (a12, a4, trade(a12, near), trade(a4, near)), (b12, b4, trade(b12, near), trade(b4, near))
+
+
+def shard_of(me, slot, x_first):
+    x, y, core = me >> X_BIT, (me >> Y_BIT) & 3, me & 1
+    group, k = (slot >> 2) & 3, slot & 3
+    if x_first:
+        x, y = x ^ GRAY[k], (y + TURNS[group]) & 3
+    else:
+        x, y = (x + TURNS[group]) & 3, y ^ GRAY[k]
+    return (x << X_BIT) | (y << Y_BIT) | (core ^ (slot >> 4))
 
 
 def hidden_order(ff):
-    k = jnp.arange(ff, dtype=jnp.int32)[:, None]
-    low = jnp.where(k < 512, k & 15, 16 + (k & 7))
-    mask = jnp.where(k < 512, place_mask(k >> 4, True), place_mask((k - 512) >> 3, False))
-    unit = (mask ^ lax.axis_index("dp")) * 24 + low
-    return (unit == jnp.arange(ff, dtype=jnp.int32)[None, :]).astype(BF16)
+    me = lax.axis_index("dp")
+    k = np.arange(ff)
+    x_first = k < 512
+    slot = np.where(x_first, k >> 4, (k - 512) >> 3)
+    low = np.where(x_first, k & 15, 16 + (k & 7))
+    pair, ring = np.array(GRAY)[slot & 3], np.array(TURNS)[(slot >> 2) & 3]
+    x = (((me >> X_BIT) ^ np.where(x_first, pair, 0)) + np.where(x_first, 0, ring)) & 3
+    y = ((((me >> Y_BIT) & 3) ^ np.where(x_first, 0, pair)) + np.where(x_first, ring, 0)) & 3
+    shard = (x << X_BIT) | (y << Y_BIT) | ((me & 1) ^ (slot >> 4))
+    unit = (shard * 24 + low).astype(jnp.int32)
+    return (unit[:, None] == jnp.arange(ff, dtype=jnp.int32)[None, :]).astype(BF16)
 
 
 def pack_kernel(both_ref, down_ref, a_ref, b_ref):
@@ -58,7 +90,17 @@
         b_ref[0, 8 * j : 8 * (j + 1), 768:] = both_ref[16:, 512 * j : 512 * (j + 1)]
 
 
-def send_kernel(tok_ref, gain_ref, expert_ref, out_ref, *, ring, cap):
+def send_kernel(tok_hbm, gain_hbm, expert_hbm, out_ref, tok_ref, gain_ref, expert_ref, sems, *, ring, cap):
+    copies = [
+        pltpu.make_async_copy(source, target, sems.at[i])
+        for i, (source, target) in enumerate(
+            ((tok_hbm, tok_ref), (gain_hbm, gain_ref), (expert_hbm, expert_ref))
+        )
+    ]
+    for copy in copies:
+        copy.start()
+    for copy in copies:
+        copy.wait()
     values = tok_ref[...].astype(F32)
     meansq = jnp.mean(values * values, axis=1, keepdims=True)
     normed = (values * lax.rsqrt(meansq + 1e-06) * gain_ref[...]).astype(BF16)
@@ -79,37 +121,40 @@
     ).astype(BF16)
 
 
-def expert_kernel(x_ref, order_ref, *rest):
+def expert_kernel(x_hbm, order_ref, *rest):
     pieces_a, pieces_b = rest[:4], rest[4:8]
-    out_ref, wa, wb, wd, hid, sem_a, sem_b, sem_d = rest[8:]
+    out_hbm, x_ref, out_ref, wa, wb, wd, hid, sem_x, sem_a, sem_b, sem_d, sem_o = rest[8:]
     width = x_ref.shape[1]
     me = lax.axis_index("dp")
-    each = pieces_a[0].shape[0]
-    copies_a = [
-        pltpu.make_async_copy(piece, wa.at[pl.ds(each * q, each)], sem_a.at[q])
-        for q, piece in enumerate(pieces_a)
-    ]
-    copies_b, copies_d = [], []
-    for q, piece in enumerate(pieces_b):
+    copy_x = pltpu.make_async_copy(x_hbm, x_ref, sem_x)
+    copies_a, copies_b, copies_d = [], [], []
+    start = 0
+    for q, (piece_a, piece_b) in enumerate(zip(pieces_a, pieces_b)):
+        each = piece_a.shape[0]
+        copies_a.append(
+            pltpu.make_async_copy(piece_a, wa.at[pl.ds(start, each)], sem_a.at[q])
+        )
         for j in range(8):
             copies_b.append(
                 pltpu.make_async_copy(
-                    piece.at[:, pl.ds(8 * j, 8), pl.ds(768, 512)],
-                    wb.at[pl.ds(each * q, each), :, pl.ds(512 * j, 512)],
+                    piece_b.at[:, pl.ds(8 * j, 8), pl.ds(768, 512)],
+                    wb.at[pl.ds(start, each), :, pl.ds(512 * j, 512)],
                     sem_b.at[8 * q + j],
                 )
             )
         for p in range(each):
-            slot = each * q + p
+            slot = start + p
             copies_d.append(
                 pltpu.make_async_copy(
-                    piece.at[p, :, pl.ds(0, 768)],
-                    wd.at[me ^ place_mask(slot, False)],
+                    piece_b.at[p, :, pl.ds(0, 768)],
+                    wd.at[shard_of(me, slot, False)],
                     sem_d.at[slot],
                 )
             )
-    for copy in copies_a + copies_b + copies_d:
+        start += each
+    for copy in [copy_x] + copies_a + copies_b + copies_d:
         copy.start()
+    copy_x.wait()
     x = x_ref[...]
 
     def units(w, cols):
@@ -117,45 +162,56 @@
         upper = lax.dot_general(x, w[:, width:], NT, preferred_element_type=F32)
         hid[:, cols] = (gate / (1.0 + jnp.exp(-gate)) * upper).astype(BF16)
 
-    half = 2 * each * 16
     for c in range(2):
         copies_a[2 * c].wait()
         copies_a[2 * c + 1].wait()
-        units(wa[2 * each * c : 2 * each * (c + 1)].reshape(half, 2 * width), slice(half * c, half * (c + 1)))
+        units(wa[16 * c : 16 * (c + 1)].reshape(256, 2 * width), slice(256 * c, 256 * (c + 1)))
     for copy in copies_b:
         copy.wait()
-    units(wb[...].reshape(256, 2 * width), slice(2 * half, 2 * half + 256))
+    units(wb[...].reshape(256, 2 * width), slice(512, 768))
     hidden = lax.dot_general(hid[...], order_ref[...], NN, preferred_element_type=F32).astype(BF16)
     for copy in copies_d:
         copy.wait()
     shards, feats, ff = wd.shape
-    group = 8
+    group = shards // sem_o.shape[0]
+    copies_o = []
     for n in range(shards // group):
         down = wd[group * n : group * (n + 1)].reshape(group * feats, ff)
-        made = lax.dot_general(hidden, down, NT, preferred_element_type=F32)
-        cols = slice(group * feats * n, group * feats * (n + 1))
-        out_ref[:, cols] = made.astype(BF16)
+        cols = pl.ds(group * feats * n, group * feats)
+        out_ref[:, cols] = lax.dot_general(
+            hidden, down, NT, preferred_element_type=F32
+        ).astype(BF16)
+        copies_o.append(
+            pltpu.make_async_copy(out_ref.at[:, cols], out_hbm.at[:, cols], sem_o.at[n])
+        )
+        copies_o[-1].start()
+    for copy in copies_o:
+        copy.wait()
 
 
 def run_expert(x, order, pieces_a, pieces_b):
     rows, width = x.shape
     ff = order.shape[0]
-    shards = 4 * pieces_a[0].shape[0]
+    shards = 32
     return pl.pallas_call(
         expert_kernel,
         out_shape=jax.ShapeDtypeStruct((rows, width), BF16),
-        in_specs=[VMEM, VMEM] + [ANY] * 8,
-        out_specs=VMEM,
+        in_specs=[ANY, VMEM] + [ANY] * 8,
+        out_specs=ANY,
         scratch_shapes=[
+            pltpu.VMEM((rows, width), BF16),
+            pltpu.VMEM((rows, width), BF16),
             pltpu.VMEM((shards, 16, 2 * width), BF16),
             pltpu.VMEM((shards, 8, 2 * width), BF16),
             pltpu.VMEM((shards, width // shards, ff), BF16),
             pltpu.VMEM((rows, ff), BF16),
+            pltpu.SemaphoreType.DMA,
             pltpu.SemaphoreType.DMA((4,)),
             pltpu.SemaphoreType.DMA((32,)),
             pltpu.SemaphoreType.DMA((32,)),
+            pltpu.SemaphoreType.DMA((4,)),
         ],
-        compiler_params=pltpu.CompilerParams(vmem_limit_bytes=55 << 20),
+        compiler_params=pltpu.CompilerParams(vmem_limit_bytes=46 << 20),
         cost_estimate=pl.CostEstimate(
             flops=6 * rows * width * ff,
             bytes_accessed=6 * width * ff + 4 * x.size,
@@ -200,8 +256,14 @@
     sent = pl.pallas_call(
         functools.partial(send_kernel, ring=ring, cap=cap),
         out_shape=jax.ShapeDtypeStruct((rows, width), BF16),
-        in_specs=[VMEM] * 3,
+        in_specs=[ANY] * 3,
         out_specs=VMEM,
+        scratch_shapes=[
+            pltpu.VMEM((tok_count, width), BF16),
+            pltpu.VMEM((1, width), F32),
+            pltpu.VMEM((1, tok_count), jnp.int32),
+            pltpu.SemaphoreType.DMA((3,)),
+        ],
         compiler_params=pltpu.CompilerParams(vmem_limit_bytes=20 << 20),
         cost_estimate=pl.CostEstimate(
             flops=6 * tok_count * tok_count * width,
@@ -210,6 +272,7 @@
         ),
         name="send",
     )(tokens, norm_gain[None, :], window_expert[None, :])
+    w_gate_up, w_down, sent = lax.optimization_barrier((w_gate_up, w_down, sent))
     x = exchange(sent, ring)
     mine_a, mine_b = pl.pallas_call(
         pack_kernel,

time: 201 us -> 197 us (0.980)
  the two profiles are of different devices: /device:TPU:32 before, /device:TPU:24 now
where the time goes in v2:
time: 197 us; the launch traced here: 196 us
  waiting for transfers between devices  97 us (49%)
  starting transfers between devices  72.8 us (37%)
  Pallas kernels  13.9 us (7%)
  local copies, waits for them, and re-layouts  11.9 us (6%)
    all_to_all x2, waiting for transfers between devices, exchange(): lax.all_to_all(blocks, 'expert', split_axis=0, concat_axis=0, tiled=True)  75.5 us
    ppermute x16, starting transfers between devices, trade(): lax.ppermute(x, 'dp', [(i, where(i)) for i in range(lax.axis_size('dp'))])  47.1 us
    all_to_all x2, starting transfers between devices, exchange(): lax.all_to_all(blocks, 'expert', split_axis=0, concat_axis=0, tiled=True)  25.7 us
    ppermute x16, waiting for transfers between devices, trade(): lax.ppermute(x, 'dp', [(i, where(i)) for i in range(lax.axis_size('dp'))])  21.4 us
    pallas_call x1, Pallas kernels, run_expert(): pl.pallas_call(expert_kernel, out_shape=jax.ShapeDtypeStruct((rows, width...  8.57 us
    unnamed x36, local copies, waits for them, and re-layouts  8.5 us
  transfers between devices with their start and end apart: 18, of which 7 were waited for; matrix products, arithmetic and copies ran while one was open for 5% of the time, Pallas kernels for 0%

profile of v2, /device:TPU:24, one launch (start us, length us, event | category | flops | bytes accessed | tf_op | source)
XLA Modules:
  0.0 196.2 jit_solution(2531302253616678414)
XLA Ops:
  0.0 1.0 copy-done
  1.0 0.7 copy-done.1
  1.7 0.7 copy-done.2
  2.4 2.0 %send.1 = bf16[384,2048]{1,0:T(8,128)(2,1)} custom-call(bf16[128,2048]{1,0:T(8,128)(2,1)S(1)} %copy-done, f32[1,2048]{1,0:T(1,128)S(1)} %bitcast.11, s32[1,128]{1,0:T(1,128)S(1)} %bitcast.12), custom_call_target="tpu_custom_call" | custom-call | flops 201326592 | bytes 2097152 | tf_op jit(solution)/shard_map/send/pallas_call | solution.py:256
  4.4 1.7 pack.1
  6.1 2.6 %collective-permute-start.1 = (bf16[1,64,1280]{2,1,0:T(8,128)(2,1)}, bf16[1,64,1280]{2,1,0:T(8,128)(2,1)S(1)}, u32[]{:S(2)}, u32[]{:S(2)}) collective-permute-start(bf16[1,64,1280]{2,1,0:T(8,128)(2,1)} %get-tuple-element.22), channel_id=1, source_target_pairs={{0,32},{16,48},{32,0},{48,16},{64,96},{80,112},{96,64},{112,80},{1... | collective-permute-start | bytes 491528 | tf_op jit(solution)/shard_map/ppermute | solution.py:20
  8.8 3.4 %collective-permute-start = (bf16[1,16,4096]{2,1,0:T(8,128)(2,1)}, bf16[1,16,4096]{2,1,0:T(8,128)(2,1)S(1)}, u32[]{:S(2)}, u32[]{:S(2)}) collective-permute-start(bf16[1,16,4096]{2,1,0:T(8,128)(2,1)} %get-tuple-element.21), channel_id=1, source_target_pairs={{0,128},{16,144},{32,160},{48,176},{64,192},{80,208},{96,224},{112... | collective-permute-start | bytes 393224 | tf_op jit(solution)/shard_map/ppermute | solution.py:20
  12.2 15.3 %all-to-all-start = ((bf16[16,24,2048]{2,1,0:T(8,128)(2,1)}), bf16[16,24,2048]{2,1,0:T(8,128)(2,1)S(1)}, u32[]{:S(2)}, u32[]{:S(2)}) async-start(bf16[16,24,2048]{2,1,0:T(8,128)(2,1)} %bitcast.3), calls=%async_computation | async-start | bytes 3145728 | tf_op jit(solution)/shard_map/all_to_all | solution.py:247
  27.6 0.7 constant_dynamic-update-slice_fusion.2
  28.2 0.7 constant_dynamic-update-slice_fusion.17
  28.9 3.0 %collective-permute-start.3 = (bf16[2,64,1280]{2,1,0:T(8,128)(2,1)S(1)}, bf16[2,64,1280]{2,1,0:T(8,128)(2,1)S(1)}, u32[]{:S(2)}, u32[]{:S(2)}) collective-permute-start(bf16[2,64,1280]{2,1,0:T(8,128)(2,1)S(1)} %pad_maximum_fusion), channel_id=1, source_target_pairs={{0,96},{16,112},{32,64},{48,80},{64,32},{80,48},{96,0},{112,16},{1... | collective-permute-start | bytes 983048 | tf_op jit(solution)/shard_map/ppermute | solution.py:20
  31.9 4.0 %collective-permute-start.2 = (bf16[2,16,4096]{2,1,0:T(8,128)(2,1)S(1)}, bf16[2,16,4096]{2,1,0:T(8,128)(2,1)S(1)}, u32[]{:S(2)}, u32[]{:S(2)}) collective-permute-start(bf16[2,16,4096]{2,1,0:T(8,128)(2,1)S(1)} %pad_maximum_fusion.1), channel_id=1, source_target_pairs={{0,384},{16,400},{32,416},{48,432},{64,448},{80,464},{96,480},{112... | collective-permute-start | bytes 786440 | tf_op jit(solution)/shard_map/ppermute | solution.py:20
  36.0 0.7 constant_dynamic-update-slice_fusion.1
  36.6 0.7 constant_dynamic-update-slice_fusion.16
  37.3 4.7 %collective-permute-done.2 = bf16[2,16,4096]{2,1,0:T(8,128)(2,1)S(1)} collective-permute-done((bf16[2,16,4096]{2,1,0:T(8,128)(2,1)S(1)}, bf16[2,16,4096]{2,1,0:T(8,128)(2,1)S(1)}, u32[]{:S(2)}, u32[]{:S(2)}) %collective-permute-start.2) | collective-permute-done | bytes 262176 | tf_op jit(solution)/shard_map/ppermute | solution.py:20
  42.0 0.8 constant_dynamic-update-slice_fusion.15
  42.8 1.9 collective-permute-start.5
  44.7 5.1 %collective-permute-start.7 = (bf16[4,64,1280]{2,1,0:T(8,128)(2,1)S(1)}, bf16[4,64,1280]{2,1,0:T(8,128)(2,1)S(1)}, u32[]{:S(2)}, u32[]{:S(2)}) collective-permute-start(bf16[4,64,1280]{2,1,0:T(8,128)(2,1)S(1)} %get-tuple-element.32), channel_id=1, source_target_pairs={{0,384},{16,400},{32,416},{48,432},{64,448},{80,464},{96,480},{112... | collective-permute-start | bytes 1966088 | tf_op jit(solution)/shard_map/ppermute | solution.py:20
  49.8 0.7 constant_dynamic-update-slice_fusion
  50.6 4.1 %collective-permute-start.4 = (bf16[4,16,4096]{2,1,0:T(8,128)(2,1)S(1)}, bf16[4,16,4096]{2,1,0:T(8,128)(2,1)S(1)}, u32[]{:S(2)}, u32[]{:S(2)}) collective-permute-start(bf16[4,16,4096]{2,1,0:T(8,128)(2,1)S(1)} %get-tuple-element.33), channel_id=1, source_target_pairs={{0,32},{16,48},{32,64},{48,80},{64,96},{80,112},{96,0},{112,16},{1... | collective-permute-start | bytes 1572872 | tf_op jit(solution)/shard_map/ppermute | solution.py:20
  54.6 1.9 collective-permute-start.6
  56.6 6.9 %collective-permute-done.4 = bf16[4,16,4096]{2,1,0:T(8,128)(2,1)S(1)} collective-permute-done((bf16[4,16,4096]{2,1,0:T(8,128)(2,1)S(1)}, bf16[4,16,4096]{2,1,0:T(8,128)(2,1)S(1)}, u32[]{:S(2)}, u32[]{:S(2)}) %collective-permute-start.4) | collective-permute-done | bytes 524320 | tf_op jit(solution)/shard_map/ppermute | solution.py:20
  63.5 5.0 %collective-permute-done.6 = bf16[4,16,4096]{2,1,0:T(8,128)(2,1)S(1)} collective-permute-done((bf16[4,16,4096]{2,1,0:T(8,128)(2,1)S(1)}, bf16[4,16,4096]{2,1,0:T(8,128)(2,1)S(1)}, u32[]{:S(2)}, u32[]{:S(2)}) %collective-permute-start.6) | collective-permute-done | bytes 524320 | tf_op jit(solution)/shard_map/ppermute | solution.py:20
  68.6 1.9 collective-permute-start.12
  70.5 5.1 %collective-permute-start.13 = (bf16[2,64,1280]{2,1,0:T(8,128)(2,1)S(1)}, bf16[2,64,1280]{2,1,0:T(8,128)(2,1)S(1)}, u32[]{:S(2)}, u32[]{:S(2)}) collective-permute-start(bf16[2,64,1280]{2,1,0:T(8,128)(2,1)S(1)} %slice.15), channel_id=1, source_target_pairs={{0,384},{16,400},{32,416},{48,432},{64,448},{80,464},{96,480},{112... | collective-permute-start | bytes 983048 | tf_op jit(solution)/shard_map/ppermute | solution.py:20
  75.7 0.9 constant_dynamic-update-slice_fusion.14
  76.5 0.9 constant_dynamic-update-slice_fusion.13.rest_4_
  77.4 1.9 collective-permute-start.14
  79.4 1.9 collective-permute-start.8
  81.3 3.9 %collective-permute-start.9 = (bf16[2,16,4096]{2,1,0:T(8,128)(2,1)S(1)}, bf16[2,16,4096]{2,1,0:T(8,128)(2,1)S(1)}, u32[]{:S(2)}, u32[]{:S(2)}) collective-permute-start(bf16[2,16,4096]{2,1,0:T(8,128)(2,1)S(1)} %slice.13), channel_id=1, source_target_pairs={{0,96},{16,112},{32,0},{48,16},{64,32},{80,48},{96,64},{112,80},{1... | collective-permute-start | bytes 786440 | tf_op jit(solution)/shard_map/ppermute | solution.py:20
  85.2 0.9 constant_dynamic-update-slice_fusion.7
  86.1 0.0 copy-start.11
  86.2 0.9 constant_dynamic-update-slice_fusion.6.rest_0_
  87.0 2.9 %collective-permute-done.8 = bf16[2,16,4096]{2,1,0:T(8,128)(2,1)S(1)} collective-permute-done((bf16[2,16,4096]{2,1,0:T(8,128)(2,1)S(1)}, bf16[2,16,4096]{2,1,0:T(8,128)(2,1)S(1)}, u32[]{:S(2)}, u32[]{:S(2)}) %collective-permute-start.8) | collective-permute-done | bytes 262176 | tf_op jit(solution)/shard_map/ppermute | solution.py:20
  90.0 1.9 collective-permute-start.10
  91.9 0.7 constant_dynamic-update-slice_fusion.12
  92.7 2.4 %collective-permute-start.15 = (bf16[4,64,1280]{2,1,0:T(8,128)(2,1)S(1)}, bf16[4,64,1280]{2,1,0:T(8,128)(2,1)}, u32[]{:S(2)}, u32[]{:S(2)}) collective-permute-start(bf16[4,64,1280]{2,1,0:T(8,128)(2,1)S(1)} %constant_dynamic-update-slice_fusion.18.rest_5_), channel_id=1, source_target_pairs={{0,16},{16,0},{32,48},{48,32},{64,80},{80,64},{96,112},{112,96},{1... | collective-permute-start | bytes 1966088 | tf_op jit(solution)/shard_map/ppermute | solution.py:20
  95.1 0.7 constant_dynamic-update-slice_fusion.11.rest_1_
  95.8 1.9 collective-permute-start.11
  97.8 0.3 fusion.order_ref
  98.1 1.9 collective-permute-done.11.rest_3_
  100.0 1.2 all-to-all-done
  101.1 8.6 %expert.1 = bf16[384,2048]{1,0:T(8,128)(2,1)} custom-call(bf16[384,2048]{1,0:T(8,128)(2,1)S(1)} %bitcast.10, bf16[768,768]{1,0:T(8,128)(2,1)S(1)} %fusion.order_ref, bf16[12,16,4096]{2,1,0:T(8,128)(2,1)} %constant_dynamic-update-slice_fusion.6.rest_0_, bf16[4,16,4096]{2,1,0:T(8,128)(2,1)} %constant_dynamic-update-slice_fusion.11.rest_1_, ...), custom_call_target="tpu_custom_call" | custom-call | flops 3623878656 | bytes 12582912 | tf_op jit(solution)/shard_map/expert/pallas_call | solution.py:196
  109.7 10.4 %all-to-all-start.1 = ((bf16[16,24,2048]{2,1,0:T(8,128)(2,1)}), bf16[16,24,2048]{2,1,0:T(8,128)(2,1)S(1)}, u32[]{:S(2)}, u32[]{:S(2)}) async-start(bf16[16,24,2048]{2,1,0:T(8,128)(2,1)} %bitcast.7), calls=%async_computation.1 | async-start | bytes 3145728 | tf_op jit(solution)/shard_map/all_to_all | solution.py:247
  120.1 0.1 copy.13.expert_ref
  120.2 0.1 copy.14.probs_ref
  120.3 74.3 %all-to-all-done.1 = bf16[16,24,2048]{2,1,0:T(8,128)(2,1)S(1)} async-done(((bf16[16,24,2048]{2,1,0:T(8,128)(2,1)}), bf16[16,24,2048]{2,1,0:T(8,128)(2,1)S(1)}, u32[]{:S(2)}, u32[]{:S(2)}) %all-to-all-start.1) | async-done | bytes 1572896 | tf_op jit(solution)/shard_map/all_to_all | solution.py:247
  194.7 1.6 last.1
  (42 shorter events, 0.3 us)
Async XLA Ops:
  0.0 1.0 copy-start
  1.0 0.7 copy-start.1
  1.7 0.7 copy-start.2
  6.1 22.8 %collective-permute-start.1 = (bf16[1,64,1280]{2,1,0:T(8,128)(2,1)}, bf16[1,64,1280]{2,1,0:T(8,128)(2,1)S(1)}, u32[]{:S(2)}, u32[]{:S(2)}) collective-permute-start(bf16[1,64,1280]{2,1,0:T(8,128)(2,1)} %get-tuple-element.22), channel_id=1, source_target_pairs={{0,32},{16,48},{32,0},{48,16},{64,96},{80,112},{96,64},{112,80},{1... | collective-permute-start | bytes 491528 | tf_op jit(solution)/shard_map/ppermute | solution.py:20
  8.8 20.1 %collective-permute-start = (bf16[1,16,4096]{2,1,0:T(8,128)(2,1)}, bf16[1,16,4096]{2,1,0:T(8,128)(2,1)S(1)}, u32[]{:S(2)}, u32[]{:S(2)}) collective-permute-start(bf16[1,16,4096]{2,1,0:T(8,128)(2,1)} %get-tuple-element.21), channel_id=1, source_target_pairs={{0,128},{16,144},{32,160},{48,176},{64,192},{80,208},{96,224},{112... | collective-permute-start | bytes 393224 | tf_op jit(solution)/shard_map/ppermute | solution.py:20
  12.2 15.4 %copy-start.5 = (bf16[1,16,4096]{2,1,0:T(8,128)(2,1)S(1)}, bf16[1,16,4096]{2,1,0:T(8,128)(2,1)}, u32[]{:S(2)}) copy-start(bf16[1,16,4096]{2,1,0:T(8,128)(2,1)} %get-tuple-element.21) | copy-start | bytes 393220
  12.2 16.0 %copy-start.4 = (bf16[1,64,1280]{2,1,0:T(8,128)(2,1)S(1)}, bf16[1,64,1280]{2,1,0:T(8,128)(2,1)}, u32[]{:S(2)}) copy-start(bf16[1,64,1280]{2,1,0:T(8,128)(2,1)} %get-tuple-element.22) | copy-start | bytes 491524
  12.2 88.9 %all-to-all-start = ((bf16[16,24,2048]{2,1,0:T(8,128)(2,1)}), bf16[16,24,2048]{2,1,0:T(8,128)(2,1)S(1)}, u32[]{:S(2)}, u32[]{:S(2)}) async-start(bf16[16,24,2048]{2,1,0:T(8,128)(2,1)} %bitcast.3), calls=%async_computation | async-start | bytes 3145728 | tf_op jit(solution)/shard_map/all_to_all | solution.py:247
  28.9 13.0 %collective-permute-start.3 = (bf16[2,64,1280]{2,1,0:T(8,128)(2,1)S(1)}, bf16[2,64,1280]{2,1,0:T(8,128)(2,1)S(1)}, u32[]{:S(2)}, u32[]{:S(2)}) collective-permute-start(bf16[2,64,1280]{2,1,0:T(8,128)(2,1)S(1)} %pad_maximum_fusion), channel_id=1, source_target_pairs={{0,96},{16,112},{32,64},{48,80},{64,32},{80,48},{96,0},{112,16},{1... | collective-permute-start | bytes 983048 | tf_op jit(solution)/shard_map/ppermute | solution.py:20
  31.9 10.0 %collective-permute-start.2 = (bf16[2,16,4096]{2,1,0:T(8,128)(2,1)S(1)}, bf16[2,16,4096]{2,1,0:T(8,128)(2,1)S(1)}, u32[]{:S(2)}, u32[]{:S(2)}) collective-permute-start(bf16[2,16,4096]{2,1,0:T(8,128)(2,1)S(1)} %pad_maximum_fusion.1), channel_id=1, source_target_pairs={{0,384},{16,400},{32,416},{48,432},{64,448},{80,464},{96,480},{112... | collective-permute-start | bytes 786440 | tf_op jit(solution)/shard_map/ppermute | solution.py:20
  42.8 25.8 %collective-permute-start.5 = (bf16[4,64,1280]{2,1,0:T(8,128)(2,1)S(1)}, bf16[4,64,1280]{2,1,0:T(8,128)(2,1)S(1)}, u32[]{:S(2)}, u32[]{:S(2)}) collective-permute-start(bf16[4,64,1280]{2,1,0:T(8,128)(2,1)S(1)} %get-tuple-element.32), channel_id=1, source_target_pairs={{0,128},{16,144},{32,160},{48,176},{64,192},{80,208},{96,224},{112... | collective-permute-start | bytes 1966088 | tf_op jit(solution)/shard_map/ppermute | solution.py:20
  44.7 23.8 %collective-permute-start.7 = (bf16[4,64,1280]{2,1,0:T(8,128)(2,1)S(1)}, bf16[4,64,1280]{2,1,0:T(8,128)(2,1)S(1)}, u32[]{:S(2)}, u32[]{:S(2)}) collective-permute-start(bf16[4,64,1280]{2,1,0:T(8,128)(2,1)S(1)} %get-tuple-element.32), channel_id=1, source_target_pairs={{0,384},{16,400},{32,416},{48,432},{64,448},{80,464},{96,480},{112... | collective-permute-start | bytes 1966088 | tf_op jit(solution)/shard_map/ppermute | solution.py:20
  50.6 12.9 %collective-permute-start.4 = (bf16[4,16,4096]{2,1,0:T(8,128)(2,1)S(1)}, bf16[4,16,4096]{2,1,0:T(8,128)(2,1)S(1)}, u32[]{:S(2)}, u32[]{:S(2)}) collective-permute-start(bf16[4,16,4096]{2,1,0:T(8,128)(2,1)S(1)} %get-tuple-element.33), channel_id=1, source_target_pairs={{0,32},{16,48},{32,64},{48,80},{64,96},{80,112},{96,0},{112,16},{1... | collective-permute-start | bytes 1572872 | tf_op jit(solution)/shard_map/ppermute | solution.py:20
  54.6 13.9 %collective-permute-start.6 = (bf16[4,16,4096]{2,1,0:T(8,128)(2,1)S(1)}, bf16[4,16,4096]{2,1,0:T(8,128)(2,1)S(1)}, u32[]{:S(2)}, u32[]{:S(2)}) collective-permute-start(bf16[4,16,4096]{2,1,0:T(8,128)(2,1)S(1)} %get-tuple-element.33), channel_id=1, source_target_pairs={{0,96},{16,112},{32,0},{48,16},{64,32},{80,48},{96,64},{112,80},{1... | collective-permute-start | bytes 1572872 | tf_op jit(solution)/shard_map/ppermute | solution.py:20
  68.6 24.1 %collective-permute-start.12 = (bf16[2,64,1280]{2,1,0:T(8,128)(2,1)S(1)}, bf16[2,64,1280]{2,1,0:T(8,128)(2,1)S(1)}, u32[]{:S(2)}, u32[]{:S(2)}) collective-permute-start(bf16[2,64,1280]{2,1,0:T(8,128)(2,1)S(1)} %slice.14), channel_id=1, source_target_pairs={{0,128},{16,144},{32,160},{48,176},{64,192},{80,208},{96,224},{112... | collective-permute-start | bytes 983048 | tf_op jit(solution)/shard_map/ppermute | solution.py:20
  70.5 22.1 %collective-permute-start.13 = (bf16[2,64,1280]{2,1,0:T(8,128)(2,1)S(1)}, bf16[2,64,1280]{2,1,0:T(8,128)(2,1)S(1)}, u32[]{:S(2)}, u32[]{:S(2)}) collective-permute-start(bf16[2,64,1280]{2,1,0:T(8,128)(2,1)S(1)} %slice.15), channel_id=1, source_target_pairs={{0,384},{16,400},{32,416},{48,432},{64,448},{80,464},{96,480},{112... | collective-permute-start | bytes 983048 | tf_op jit(solution)/shard_map/ppermute | solution.py:20
  77.4 22.6 %collective-permute-start.14 = (bf16[12,64,1280]{2,1,0:T(8,128)(2,1)}, bf16[12,64,1280]{2,1,0:T(8,128)(2,1)}, u32[]{:S(2)}, u32[]{:S(2)}) collective-permute-start(bf16[12,64,1280]{2,1,0:T(8,128)(2,1)} %constant_dynamic-update-slice_fusion.13.rest_4_), channel_id=1, source_target_pairs={{0,16},{16,0},{32,48},{48,32},{64,80},{80,64},{96,112},{112,96},{1... | collective-permute-start | bytes 5898248 | tf_op jit(solution)/shard_map/ppermute | solution.py:20
  79.4 10.6 %collective-permute-start.8 = (bf16[2,16,4096]{2,1,0:T(8,128)(2,1)S(1)}, bf16[2,16,4096]{2,1,0:T(8,128)(2,1)S(1)}, u32[]{:S(2)}, u32[]{:S(2)}) collective-permute-start(bf16[2,16,4096]{2,1,0:T(8,128)(2,1)S(1)} %slice.12), channel_id=1, source_target_pairs={{0,32},{16,48},{32,64},{48,80},{64,96},{80,112},{96,0},{112,16},{1... | collective-permute-start | bytes 786440 | tf_op jit(solution)/shard_map/ppermute | solution.py:20
  81.3 13.8 %collective-permute-start.9 = (bf16[2,16,4096]{2,1,0:T(8,128)(2,1)S(1)}, bf16[2,16,4096]{2,1,0:T(8,128)(2,1)S(1)}, u32[]{:S(2)}, u32[]{:S(2)}) collective-permute-start(bf16[2,16,4096]{2,1,0:T(8,128)(2,1)S(1)} %slice.13), channel_id=1, source_target_pairs={{0,96},{16,112},{32,0},{48,16},{64,32},{80,48},{96,64},{112,80},{1... | collective-permute-start | bytes 786440 | tf_op jit(solution)/shard_map/ppermute | solution.py:20
  86.1 11.6 %copy-start.7 = (s32[768]{0:T(1024)S(1)}, s32[768]{0:T(1024)}, u32[]{:S(2)}) copy-start(s32[768]{0:T(1024)} %constant.26.clone) | copy-start | bytes 9220
  86.1 11.6 %copy-start.8 = (s32[768]{0:T(1024)S(1)}, s32[768]{0:T(1024)}, u32[]{:S(2)}) copy-start(s32[768]{0:T(1024)} %constant.27.clone) | copy-start | bytes 9220
  86.1 11.6 %copy-start.9 = (s32[768]{0:T(1024)S(1)}, s32[768]{0:T(1024)}, u32[]{:S(2)}) copy-start(s32[768]{0:T(1024)} %constant.28.clone) | copy-start | bytes 9220
  86.1 11.7 %copy-start.10 = (s32[768]{0:T(1024)S(1)}, s32[768]{0:T(1024)}, u32[]{:S(2)}) copy-start(s32[768]{0:T(1024)} %constant.29.clone) | copy-start | bytes 9220
  86.1 11.7 %copy-start.11 = (s32[768]{0:T(1024)S(1)}, s32[768]{0:T(1024)}, u32[]{:S(2)}) copy-start(s32[768]{0:T(1024)} %constant.30.clone) | copy-start | bytes 9220
  86.1 11.7 %copy-start.12 = (s32[768]{0:T(1024)S(1)}, s32[768]{0:T(1024)}, u32[]{:S(2)}) copy-start(s32[768]{0:T(1024)} %constant.31.clone) | copy-start | bytes 9220
  90.0 10.0 %collective-permute-start.10 = (bf16[12,16,4096]{2,1,0:T(8,128)(2,1)}, bf16[12,16,4096]{2,1,0:T(8,128)(2,1)}, u32[]{:S(2)}, u32[]{:S(2)}) collective-permute-start(bf16[12,16,4096]{2,1,0:T(8,128)(2,1)} %constant_dynamic-update-slice_fusion.6.rest_0_), channel_id=1, source_target_pairs={{0,16},{16,0},{32,48},{48,32},{64,80},{80,64},{96,112},{112,96},{1... | collective-permute-start | bytes 4718600 | tf_op jit(solution)/shard_map/ppermute | solution.py:20
  92.7 7.3 %collective-permute-start.15 = (bf16[4,64,1280]{2,1,0:T(8,128)(2,1)S(1)}, bf16[4,64,1280]{2,1,0:T(8,128)(2,1)}, u32[]{:S(2)}, u32[]{:S(2)}) collective-permute-start(bf16[4,64,1280]{2,1,0:T(8,128)(2,1)S(1)} %constant_dynamic-update-slice_fusion.18.rest_5_), channel_id=1, source_target_pairs={{0,16},{16,0},{32,48},{48,32},{64,80},{80,64},{96,112},{112,96},{1... | collective-permute-start | bytes 1966088 | tf_op jit(solution)/shard_map/ppermute | solution.py:20
  95.8 4.1 %collective-permute-start.11 = (bf16[4,16,4096]{2,1,0:T(8,128)(2,1)}, bf16[4,16,4096]{2,1,0:T(8,128)(2,1)}, u32[]{:S(2)}, u32[]{:S(2)}) collective-permute-start(bf16[4,16,4096]{2,1,0:T(8,128)(2,1)} %constant_dynamic-update-slice_fusion.11.rest_1_), channel_id=1, source_target_pairs={{0,16},{16,0},{32,48},{48,32},{64,80},{80,64},{96,112},{112,96},{1... | collective-permute-start | bytes 1572872 | tf_op jit(solution)/shard_map/ppermute | solution.py:20
  109.7 10.4 %copy-start.3 = (s32[128]{0:T(128)S(1)}, s32[128]{0:T(128)}, u32[]{:S(2)}) copy-start(s32[128]{0:T(128)} %param.15) | copy-start | bytes 1540
  109.7 10.5 %copy-start.6 = (f32[128,8]{0,1:T(8,128)S(1)}, f32[128,8]{0,1:T(8,128)}, u32[]{:S(2)}) copy-start(f32[128,8]{0,1:T(8,128)} %param.14) | copy-start | bytes 12292
  109.7 85.0 %all-to-all-start.1 = ((bf16[16,24,2048]{2,1,0:T(8,128)(2,1)}), bf16[16,24,2048]{2,1,0:T(8,128)(2,1)S(1)}, u32[]{:S(2)}, u32[]{:S(2)}) async-start(bf16[16,24,2048]{2,1,0:T(8,128)(2,1)} %bitcast.7), calls=%async_computation.1 | async-start | bytes 3145728 | tf_op jit(solution)/shard_map/all_to_all | solution.py:247

commit v3 on v2

--- a/solution.py
+++ b/solution.py
@@ -83,23 +83,23 @@
     return (unit[:, None] == jnp.arange(ff, dtype=jnp.int32)[None, :]).astype(BF16)
 
 
-def pack_kernel(both_ref, down_ref, a_ref, b_ref):
-    a_ref[0] = both_ref[:16]
-    b_ref[0, :, :768] = down_ref[...]
-    for j in range(8):
-        b_ref[0, 8 * j : 8 * (j + 1), 768:] = both_ref[16:, 512 * j : 512 * (j + 1)]
-
-
-def send_kernel(tok_hbm, gain_hbm, expert_hbm, out_ref, tok_ref, gain_ref, expert_ref, sems, *, ring, cap):
-    copies = [
-        pltpu.make_async_copy(source, target, sems.at[i])
-        for i, (source, target) in enumerate(
-            ((tok_hbm, tok_ref), (gain_hbm, gain_ref), (expert_hbm, expert_ref))
-        )
+def prepare_kernel(*refs, ring, cap):
+    tok_hbm, gain_hbm, expert_hbm, both_hbm, down_hbm = refs[:5]
+    out_ref, a_ref, b_ref, tok_ref, gain_ref, expert_ref, sems = refs[5:]
+    moves = [
+        (tok_hbm, tok_ref),
+        (gain_hbm, gain_ref),
+        (expert_hbm, expert_ref),
+        (both_hbm.at[pl.ds(0, 16)], a_ref.at[0]),
+        (down_hbm, b_ref.at[0, :, pl.ds(0, 768)]),
+    ] + [
+        (both_hbm.at[pl.ds(16, 8), pl.ds(512 * j, 512)], b_ref.at[0, pl.ds(8 * j, 8), pl.ds(768, 512)])
+        for j in range(8)
     ]
+    copies = [pltpu.make_async_copy(*move, sems.at[i]) for i, move in enumerate(moves)]
     for copy in copies:
         copy.start()
-    for copy in copies:
+    for copy in copies[:3]:
         copy.wait()
     values = tok_ref[...].astype(F32)
     meansq = jnp.mean(values * values, axis=1, keepdims=True)
@@ -119,6 +119,8 @@
     out_ref[...] = lax.dot_general(
         pick.astype(F32).astype(BF16), normed, NN, preferred_element_type=F32
     ).astype(BF16)
+    for copy in copies[3:]:
+        copy.wait()
 
 
 def expert_kernel(x_hbm, order_ref, *rest):
@@ -253,37 +255,30 @@
     cap = 3 * tok_count // ring
     rows = ring * cap
     ff = w_down.shape[2]
-    sent = pl.pallas_call(
-        functools.partial(send_kernel, ring=ring, cap=cap),
-        out_shape=jax.ShapeDtypeStruct((rows, width), BF16),
-        in_specs=[ANY] * 3,
-        out_specs=VMEM,
+    sent, mine_a, mine_b = pl.pallas_call(
+        functools.partial(prepare_kernel, ring=ring, cap=cap),
+        out_shape=[
+            jax.ShapeDtypeStruct((rows, width), BF16),
+            jax.ShapeDtypeStruct((1, 16, 2 * width), BF16),
+            jax.ShapeDtypeStruct((1, 64, 1280), BF16),
+        ],
+        in_specs=[ANY] * 5,
+        out_specs=[VMEM] * 3,
         scratch_shapes=[
             pltpu.VMEM((tok_count, width), BF16),
             pltpu.VMEM((1, width), F32),
             pltpu.VMEM((1, tok_count), jnp.int32),
-            pltpu.SemaphoreType.DMA((3,)),
+            pltpu.SemaphoreType.DMA((13,)),
         ],
-        compiler_params=pltpu.CompilerParams(vmem_limit_bytes=20 << 20),
+        compiler_params=pltpu.CompilerParams(vmem_limit_bytes=60 << 20),
         cost_estimate=pl.CostEstimate(
             flops=6 * tok_count * tok_count * width,
             bytes_accessed=8 * tokens.size,
             transcendentals=0,
         ),
-        name="send",
-    )(tokens, norm_gain[None, :], window_expert[None, :])
-    w_gate_up, w_down, sent = lax.optimization_barrier((w_gate_up, w_down, sent))
+        name="prepare",
+    )(tokens, norm_gain[None, :], window_expert[None, :], w_gate_up[0], w_down[0])
     x = exchange(sent, ring)
-    mine_a, mine_b = pl.pallas_call(
-        pack_kernel,
-        out_shape=[
-            jax.ShapeDtypeStruct((1, 16, 2 * width), BF16),
-            jax.ShapeDtypeStruct((1, 64, 1280), BF16),
-        ],
-        in_specs=[VMEM] * 2,
-        out_specs=[VMEM] * 2,
-        name="pack",
-    )(w_gate_up[0], w_down[0])
     made = run_expert(x, hidden_order(ff), *gather(mine_a, mine_b))
     return pl.pallas_call(
         functools.partial(last_kernel, ring=ring, cap=cap),

time: 197 us -> 194 us (0.985)
  local copies, waits for them, and re-layouts: 11.9 us -> 9.61 us
    unnamed x36 -> x30, local copies, waits for them, and re-layouts: 8.5 us -> 6.15 us
where the time goes in v3:
time: 194 us; the launch traced here: 193 us
  waiting for transfers between devices  96.9 us (50%)
  starting transfers between devices  72.8 us (38%)
  Pallas kernels  13.3 us (7%)
  local copies, waits for them, and re-layouts  9.61 us (5%)
    all_to_all x2, waiting for transfers between devices, exchange(): lax.all_to_all(blocks, 'expert', split_axis=0, concat_axis=0, tiled=True)  75.5 us
    ppermute x16, starting transfers between devices, trade(): lax.ppermute(x, 'dp', [(i, where(i)) for i in range(lax.axis_size('dp'))])  47.1 us
    all_to_all x2, starting transfers between devices, exchange(): lax.all_to_all(blocks, 'expert', split_axis=0, concat_axis=0, tiled=True)  25.7 us
    ppermute x16, waiting for transfers between devices, trade(): lax.ppermute(x, 'dp', [(i, where(i)) for i in range(lax.axis_size('dp'))])  21.4 us
    pallas_call x1, Pallas kernels, run_expert(): pl.pallas_call(expert_kernel, out_shape=jax.ShapeDtypeStruct((rows, width...  8.59 us
    unnamed x30, local copies, waits for them, and re-layouts  6.15 us
  transfers between devices with their start and end apart: 18, of which 7 were waited for; matrix products, arithmetic and copies ran while one was open for 5% of the time, Pallas kernels for 0%

profile of v3, /device:TPU:24, one launch (start us, length us, event | category | flops | bytes accessed | tf_op | source)
XLA Modules:
  0.0 193.4 jit_solution(4262293836280969380)
XLA Ops:
  0.0 3.2 %prepare.1 = (bf16[384,2048]{1,0:T(8,128)(2,1)}, bf16[1,16,4096]{2,1,0:T(8,128)(2,1)}, bf16[1,64,1280]{2,1,0:T(8,128)(2,1)}) custom-call(bf16[128,2048]{1,0:T(8,128)(2,1)} %refs_0_.1, f32[1,2048]{1,0:T(1,128)} %bitcast.14, s32[1,128]{1,0:T(1,128)} %bitcast.15, bf16[24,4096]{1,0:T(8,128)(2,1)} %bitcast.12, bf16[64,768]{1,0:T(8,128)(2,1)} %bitcast.13), custom_call_target="tpu_custom_call" | custom-call | flops 201326592 | bytes 2097152 | tf_op jit(solution)/shard_map/prepare/pallas_call | solution.py:258
  3.2 2.7 %collective-permute-start.1 = (bf16[1,64,1280]{2,1,0:T(8,128)(2,1)}, bf16[1,64,1280]{2,1,0:T(8,128)(2,1)S(1)}, u32[]{:S(2)}, u32[]{:S(2)}) collective-permute-start(bf16[1,64,1280]{2,1,0:T(8,128)(2,1)} %get-tuple-element.18), channel_id=1, source_target_pairs={{0,32},{16,48},{32,0},{48,16},{64,96},{80,112},{96,64},{112,80},{1... | collective-permute-start | bytes 491528 | tf_op jit(solution)/shard_map/ppermute | solution.py:20
  5.8 3.4 %collective-permute-start = (bf16[1,16,4096]{2,1,0:T(8,128)(2,1)}, bf16[1,16,4096]{2,1,0:T(8,128)(2,1)S(1)}, u32[]{:S(2)}, u32[]{:S(2)}) collective-permute-start(bf16[1,16,4096]{2,1,0:T(8,128)(2,1)} %get-tuple-element.17), channel_id=1, source_target_pairs={{0,128},{16,144},{32,160},{48,176},{64,192},{80,208},{96,224},{112... | collective-permute-start | bytes 393224 | tf_op jit(solution)/shard_map/ppermute | solution.py:20
  9.3 0.0 copy-start
  9.3 15.3 %all-to-all-start = ((bf16[16,24,2048]{2,1,0:T(8,128)(2,1)}), bf16[16,24,2048]{2,1,0:T(8,128)(2,1)S(1)}, u32[]{:S(2)}, u32[]{:S(2)}) async-start(bf16[16,24,2048]{2,1,0:T(8,128)(2,1)} %bitcast.11), calls=%async_computation | async-start | bytes 3145728 | tf_op jit(solution)/shard_map/all_to_all | solution.py:249
  24.6 0.7 constant_dynamic-update-slice_fusion.2
  25.3 0.7 constant_dynamic-update-slice_fusion.17
  26.0 3.0 %collective-permute-start.3 = (bf16[2,64,1280]{2,1,0:T(8,128)(2,1)S(1)}, bf16[2,64,1280]{2,1,0:T(8,128)(2,1)S(1)}, u32[]{:S(2)}, u32[]{:S(2)}) collective-permute-start(bf16[2,64,1280]{2,1,0:T(8,128)(2,1)S(1)} %pad_maximum_fusion), channel_id=1, source_target_pairs={{0,96},{16,112},{32,64},{48,80},{64,32},{80,48},{96,0},{112,16},{1... | collective-permute-start | bytes 983048 | tf_op jit(solution)/shard_map/ppermute | solution.py:20
  29.0 4.0 %collective-permute-start.2 = (bf16[2,16,4096]{2,1,0:T(8,128)(2,1)S(1)}, bf16[2,16,4096]{2,1,0:T(8,128)(2,1)S(1)}, u32[]{:S(2)}, u32[]{:S(2)}) collective-permute-start(bf16[2,16,4096]{2,1,0:T(8,128)(2,1)S(1)} %pad_maximum_fusion.1), channel_id=1, source_target_pairs={{0,384},{16,400},{32,416},{48,432},{64,448},{80,464},{96,480},{112... | collective-permute-start | bytes 786440 | tf_op jit(solution)/shard_map/ppermute | solution.py:20
  33.0 0.7 constant_dynamic-update-slice_fusion.1
  33.7 0.7 constant_dynamic-update-slice_fusion.16
  34.4 4.7 %collective-permute-done.2 = bf16[2,16,4096]{2,1,0:T(8,128)(2,1)S(1)} collective-permute-done((bf16[2,16,4096]{2,1,0:T(8,128)(2,1)S(1)}, bf16[2,16,4096]{2,1,0:T(8,128)(2,1)S(1)}, u32[]{:S(2)}, u32[]{:S(2)}) %collective-permute-start.2) | collective-permute-done | bytes 262176 | tf_op jit(solution)/shard_map/ppermute | solution.py:20
  39.0 0.8 constant_dynamic-update-slice_fusion.15
  39.8 1.9 collective-permute-start.5
  41.7 5.1 %collective-permute-start.7 = (bf16[4,64,1280]{2,1,0:T(8,128)(2,1)S(1)}, bf16[4,64,1280]{2,1,0:T(8,128)(2,1)S(1)}, u32[]{:S(2)}, u32[]{:S(2)}) collective-permute-start(bf16[4,64,1280]{2,1,0:T(8,128)(2,1)S(1)} %get-tuple-element.28), channel_id=1, source_target_pairs={{0,384},{16,400},{32,416},{48,432},{64,448},{80,464},{96,480},{112... | collective-permute-start | bytes 1966088 | tf_op jit(solution)/shard_map/ppermute | solution.py:20
  46.9 0.7 constant_dynamic-update-slice_fusion
  47.6 4.1 %collective-permute-start.4 = (bf16[4,16,4096]{2,1,0:T(8,128)(2,1)S(1)}, bf16[4,16,4096]{2,1,0:T(8,128)(2,1)S(1)}, u32[]{:S(2)}, u32[]{:S(2)}) collective-permute-start(bf16[4,16,4096]{2,1,0:T(8,128)(2,1)S(1)} %get-tuple-element.29), channel_id=1, source_target_pairs={{0,32},{16,48},{32,64},{48,80},{64,96},{80,112},{96,0},{112,16},{1... | collective-permute-start | bytes 1572872 | tf_op jit(solution)/shard_map/ppermute | solution.py:20
  51.7 1.9 collective-permute-start.6
  53.6 6.9 %collective-permute-done.4 = bf16[4,16,4096]{2,1,0:T(8,128)(2,1)S(1)} collective-permute-done((bf16[4,16,4096]{2,1,0:T(8,128)(2,1)S(1)}, bf16[4,16,4096]{2,1,0:T(8,128)(2,1)S(1)}, u32[]{:S(2)}, u32[]{:S(2)}) %collective-permute-start.4) | collective-permute-done | bytes 524320 | tf_op jit(solution)/shard_map/ppermute | solution.py:20
  60.6 5.0 %collective-permute-done.6 = bf16[4,16,4096]{2,1,0:T(8,128)(2,1)S(1)} collective-permute-done((bf16[4,16,4096]{2,1,0:T(8,128)(2,1)S(1)}, bf16[4,16,4096]{2,1,0:T(8,128)(2,1)S(1)}, u32[]{:S(2)}, u32[]{:S(2)}) %collective-permute-start.6) | collective-permute-done | bytes 524320 | tf_op jit(solution)/shard_map/ppermute | solution.py:20
  65.6 1.9 collective-permute-start.12
  67.6 5.1 %collective-permute-start.13 = (bf16[2,64,1280]{2,1,0:T(8,128)(2,1)S(1)}, bf16[2,64,1280]{2,1,0:T(8,128)(2,1)S(1)}, u32[]{:S(2)}, u32[]{:S(2)}) collective-permute-start(bf16[2,64,1280]{2,1,0:T(8,128)(2,1)S(1)} %slice.15), channel_id=1, source_target_pairs={{0,384},{16,400},{32,416},{48,432},{64,448},{80,464},{96,480},{112... | collective-permute-start | bytes 983048 | tf_op jit(solution)/shard_map/ppermute | solution.py:20
  72.7 0.9 constant_dynamic-update-slice_fusion.14
  73.6 0.9 constant_dynamic-update-slice_fusion.13.rest_4_
  74.5 1.9 collective-permute-start.14
  76.5 1.9 collective-permute-start.8
  78.4 3.9 %collective-permute-start.9 = (bf16[2,16,4096]{2,1,0:T(8,128)(2,1)S(1)}, bf16[2,16,4096]{2,1,0:T(8,128)(2,1)S(1)}, u32[]{:S(2)}, u32[]{:S(2)}) collective-permute-start(bf16[2,16,4096]{2,1,0:T(8,128)(2,1)S(1)} %slice.13), channel_id=1, source_target_pairs={{0,96},{16,112},{32,0},{48,16},{64,32},{80,48},{96,64},{112,80},{1... | collective-permute-start | bytes 786440 | tf_op jit(solution)/shard_map/ppermute | solution.py:20
  82.3 0.9 constant_dynamic-update-slice_fusion.7
  83.2 0.0 copy-start.7
  83.2 0.0 copy-start.8
  83.2 0.9 constant_dynamic-update-slice_fusion.6.rest_0_
  84.1 2.9 %collective-permute-done.8 = bf16[2,16,4096]{2,1,0:T(8,128)(2,1)S(1)} collective-permute-done((bf16[2,16,4096]{2,1,0:T(8,128)(2,1)S(1)}, bf16[2,16,4096]{2,1,0:T(8,128)(2,1)S(1)}, u32[]{:S(2)}, u32[]{:S(2)}) %collective-permute-start.8) | collective-permute-done | bytes 262176 | tf_op jit(solution)/shard_map/ppermute | solution.py:20
  87.1 1.9 collective-permute-start.10
  89.0 0.7 constant_dynamic-update-slice_fusion.12
  89.8 2.4 %collective-permute-start.15 = (bf16[4,64,1280]{2,1,0:T(8,128)(2,1)S(1)}, bf16[4,64,1280]{2,1,0:T(8,128)(2,1)}, u32[]{:S(2)}, u32[]{:S(2)}) collective-permute-start(bf16[4,64,1280]{2,1,0:T(8,128)(2,1)S(1)} %constant_dynamic-update-slice_fusion.18.rest_5_), channel_id=1, source_target_pairs={{0,16},{16,0},{32,48},{48,32},{64,80},{80,64},{96,112},{112,96},{1... | collective-permute-start | bytes 1966088 | tf_op jit(solution)/shard_map/ppermute | solution.py:20
  92.2 0.7 constant_dynamic-update-slice_fusion.11.rest_1_
  92.9 1.9 collective-permute-start.11
  94.9 0.3 fusion.order_ref
  95.2 1.9 collective-permute-done.11.rest_3_
  97.1 1.1 all-to-all-done
  98.2 8.6 %expert.1 = bf16[384,2048]{1,0:T(8,128)(2,1)} custom-call(bf16[384,2048]{1,0:T(8,128)(2,1)S(1)} %bitcast.10, bf16[768,768]{1,0:T(8,128)(2,1)S(1)} %fusion.order_ref, bf16[12,16,4096]{2,1,0:T(8,128)(2,1)} %constant_dynamic-update-slice_fusion.6.rest_0_, bf16[4,16,4096]{2,1,0:T(8,128)(2,1)} %constant_dynamic-update-slice_fusion.11.rest_1_, ...), custom_call_target="tpu_custom_call" | custom-call | flops 3623878656 | bytes 12582912 | tf_op jit(solution)/shard_map/expert/pallas_call | solution.py:198
  106.8 0.0 copy-start.9
  106.8 0.0 copy-start.2
  106.8 10.4 %all-to-all-start.1 = ((bf16[16,24,2048]{2,1,0:T(8,128)(2,1)}), bf16[16,24,2048]{2,1,0:T(8,128)(2,1)S(1)}, u32[]{:S(2)}, u32[]{:S(2)}) async-start(bf16[16,24,2048]{2,1,0:T(8,128)(2,1)} %bitcast.7), calls=%async_computation.1 | async-start | bytes 3145728 | tf_op jit(solution)/shard_map/all_to_all | solution.py:249
  117.2 0.1 copy.13.expert_ref
  117.3 0.1 copy.14.probs_ref
  117.4 74.3 %all-to-all-done.1 = bf16[16,24,2048]{2,1,0:T(8,128)(2,1)S(1)} async-done(((bf16[16,24,2048]{2,1,0:T(8,128)(2,1)}), bf16[16,24,2048]{2,1,0:T(8,128)(2,1)S(1)}, u32[]{:S(2)}, u32[]{:S(2)}) %all-to-all-start.1) | async-done | bytes 1572896 | tf_op jit(solution)/shard_map/all_to_all | solution.py:249
  191.8 1.6 last.1
  (35 shorter events, 0.3 us)
Async XLA Ops:
  3.2 22.8 %collective-permute-start.1 = (bf16[1,64,1280]{2,1,0:T(8,128)(2,1)}, bf16[1,64,1280]{2,1,0:T(8,128)(2,1)S(1)}, u32[]{:S(2)}, u32[]{:S(2)}) collective-permute-start(bf16[1,64,1280]{2,1,0:T(8,128)(2,1)} %get-tuple-element.18), channel_id=1, source_target_pairs={{0,32},{16,48},{32,0},{48,16},{64,96},{80,112},{96,64},{112,80},{1... | collective-permute-start | bytes 491528 | tf_op jit(solution)/shard_map/ppermute | solution.py:20
  5.8 20.1 %collective-permute-start = (bf16[1,16,4096]{2,1,0:T(8,128)(2,1)}, bf16[1,16,4096]{2,1,0:T(8,128)(2,1)S(1)}, u32[]{:S(2)}, u32[]{:S(2)}) collective-permute-start(bf16[1,16,4096]{2,1,0:T(8,128)(2,1)} %get-tuple-element.17), channel_id=1, source_target_pairs={{0,128},{16,144},{32,160},{48,176},{64,192},{80,208},{96,224},{112... | collective-permute-start | bytes 393224 | tf_op jit(solution)/shard_map/ppermute | solution.py:20
  9.2 15.4 %copy-start.1 = (bf16[1,16,4096]{2,1,0:T(8,128)(2,1)S(1)}, bf16[1,16,4096]{2,1,0:T(8,128)(2,1)}, u32[]{:S(2)}) copy-start(bf16[1,16,4096]{2,1,0:T(8,128)(2,1)} %get-tuple-element.17) | copy-start | bytes 393220
  9.3 16.0 %copy-start = (bf16[1,64,1280]{2,1,0:T(8,128)(2,1)S(1)}, bf16[1,64,1280]{2,1,0:T(8,128)(2,1)}, u32[]{:S(2)}) copy-start(bf16[1,64,1280]{2,1,0:T(8,128)(2,1)} %get-tuple-element.18) | copy-start | bytes 491524
  9.3 88.9 %all-to-all-start = ((bf16[16,24,2048]{2,1,0:T(8,128)(2,1)}), bf16[16,24,2048]{2,1,0:T(8,128)(2,1)S(1)}, u32[]{:S(2)}, u32[]{:S(2)}) async-start(bf16[16,24,2048]{2,1,0:T(8,128)(2,1)} %bitcast.11), calls=%async_computation | async-start | bytes 3145728 | tf_op jit(solution)/shard_map/all_to_all | solution.py:249
  26.0 13.0 %collective-permute-start.3 = (bf16[2,64,1280]{2,1,0:T(8,128)(2,1)S(1)}, bf16[2,64,1280]{2,1,0:T(8,128)(2,1)S(1)}, u32[]{:S(2)}, u32[]{:S(2)}) collective-permute-start(bf16[2,64,1280]{2,1,0:T(8,128)(2,1)S(1)} %pad_maximum_fusion), channel_id=1, source_target_pairs={{0,96},{16,112},{32,64},{48,80},{64,32},{80,48},{96,0},{112,16},{1... | collective-permute-start | bytes 983048 | tf_op jit(solution)/shard_map/ppermute | solution.py:20
  29.0 10.0 %collective-permute-start.2 = (bf16[2,16,4096]{2,1,0:T(8,128)(2,1)S(1)}, bf16[2,16,4096]{2,1,0:T(8,128)(2,1)S(1)}, u32[]{:S(2)}, u32[]{:S(2)}) collective-permute-start(bf16[2,16,4096]{2,1,0:T(8,128)(2,1)S(1)} %pad_maximum_fusion.1), channel_id=1, source_target_pairs={{0,384},{16,400},{32,416},{48,432},{64,448},{80,464},{96,480},{112... | collective-permute-start | bytes 786440 | tf_op jit(solution)/shard_map/ppermute | solution.py:20
  39.8 25.8 %collective-permute-start.5 = (bf16[4,64,1280]{2,1,0:T(8,128)(2,1)S(1)}, bf16[4,64,1280]{2,1,0:T(8,128)(2,1)S(1)}, u32[]{:S(2)}, u32[]{:S(2)}) collective-permute-start(bf16[4,64,1280]{2,1,0:T(8,128)(2,1)S(1)} %get-tuple-element.28), channel_id=1, source_target_pairs={{0,128},{16,144},{32,160},{48,176},{64,192},{80,208},{96,224},{112... | collective-permute-start | bytes 1966088 | tf_op jit(solution)/shard_map/ppermute | solution.py:20
  41.7 23.9 %collective-permute-start.7 = (bf16[4,64,1280]{2,1,0:T(8,128)(2,1)S(1)}, bf16[4,64,1280]{2,1,0:T(8,128)(2,1)S(1)}, u32[]{:S(2)}, u32[]{:S(2)}) collective-permute-start(bf16[4,64,1280]{2,1,0:T(8,128)(2,1)S(1)} %get-tuple-element.28), channel_id=1, source_target_pairs={{0,384},{16,400},{32,416},{48,432},{64,448},{80,464},{96,480},{112... | collective-permute-start | bytes 1966088 | tf_op jit(solution)/shard_map/ppermute | solution.py:20
  47.6 12.9 %collective-permute-start.4 = (bf16[4,16,4096]{2,1,0:T(8,128)(2,1)S(1)}, bf16[4,16,4096]{2,1,0:T(8,128)(2,1)S(1)}, u32[]{:S(2)}, u32[]{:S(2)}) collective-permute-start(bf16[4,16,4096]{2,1,0:T(8,128)(2,1)S(1)} %get-tuple-element.29), channel_id=1, source_target_pairs={{0,32},{16,48},{32,64},{48,80},{64,96},{80,112},{96,0},{112,16},{1... | collective-permute-start | bytes 1572872 | tf_op jit(solution)/shard_map/ppermute | solution.py:20
  51.7 13.9 %collective-permute-start.6 = (bf16[4,16,4096]{2,1,0:T(8,128)(2,1)S(1)}, bf16[4,16,4096]{2,1,0:T(8,128)(2,1)S(1)}, u32[]{:S(2)}, u32[]{:S(2)}) collective-permute-start(bf16[4,16,4096]{2,1,0:T(8,128)(2,1)S(1)} %get-tuple-element.29), channel_id=1, source_target_pairs={{0,96},{16,112},{32,0},{48,16},{64,32},{80,48},{96,64},{112,80},{1... | collective-permute-start | bytes 1572872 | tf_op jit(solution)/shard_map/ppermute | solution.py:20
  65.6 24.1 %collective-permute-start.12 = (bf16[2,64,1280]{2,1,0:T(8,128)(2,1)S(1)}, bf16[2,64,1280]{2,1,0:T(8,128)(2,1)S(1)}, u32[]{:S(2)}, u32[]{:S(2)}) collective-permute-start(bf16[2,64,1280]{2,1,0:T(8,128)(2,1)S(1)} %slice.14), channel_id=1, source_target_pairs={{0,128},{16,144},{32,160},{48,176},{64,192},{80,208},{96,224},{112... | collective-permute-start | bytes 983048 | tf_op jit(solution)/shard_map/ppermute | solution.py:20
  67.6 22.1 %collective-permute-start.13 = (bf16[2,64,1280]{2,1,0:T(8,128)(2,1)S(1)}, bf16[2,64,1280]{2,1,0:T(8,128)(2,1)S(1)}, u32[]{:S(2)}, u32[]{:S(2)}) collective-permute-start(bf16[2,64,1280]{2,1,0:T(8,128)(2,1)S(1)} %slice.15), channel_id=1, source_target_pairs={{0,384},{16,400},{32,416},{48,432},{64,448},{80,464},{96,480},{112... | collective-permute-start | bytes 983048 | tf_op jit(solution)/shard_map/ppermute | solution.py:20
  74.5 22.6 %collective-permute-start.14 = (bf16[12,64,1280]{2,1,0:T(8,128)(2,1)}, bf16[12,64,1280]{2,1,0:T(8,128)(2,1)}, u32[]{:S(2)}, u32[]{:S(2)}) collective-permute-start(bf16[12,64,1280]{2,1,0:T(8,128)(2,1)} %constant_dynamic-update-slice_fusion.13.rest_4_), channel_id=1, source_target_pairs={{0,16},{16,0},{32,48},{48,32},{64,80},{80,64},{96,112},{112,96},{1... | collective-permute-start | bytes 5898248 | tf_op jit(solution)/shard_map/ppermute | solution.py:20
  76.5 10.6 %collective-permute-start.8 = (bf16[2,16,4096]{2,1,0:T(8,128)(2,1)S(1)}, bf16[2,16,4096]{2,1,0:T(8,128)(2,1)S(1)}, u32[]{:S(2)}, u32[]{:S(2)}) collective-permute-start(bf16[2,16,4096]{2,1,0:T(8,128)(2,1)S(1)} %slice.12), channel_id=1, source_target_pairs={{0,32},{16,48},{32,64},{48,80},{64,96},{80,112},{96,0},{112,16},{1... | collective-permute-start | bytes 786440 | tf_op jit(solution)/shard_map/ppermute | solution.py:20
  78.4 13.8 %collective-permute-start.9 = (bf16[2,16,4096]{2,1,0:T(8,128)(2,1)S(1)}, bf16[2,16,4096]{2,1,0:T(8,128)(2,1)S(1)}, u32[]{:S(2)}, u32[]{:S(2)}) collective-permute-start(bf16[2,16,4096]{2,1,0:T(8,128)(2,1)S(1)} %slice.13), channel_id=1, source_target_pairs={{0,96},{16,112},{32,0},{48,16},{64,32},{80,48},{96,64},{112,80},{1... | collective-permute-start | bytes 786440 | tf_op jit(solution)/shard_map/ppermute | solution.py:20
  83.2 11.6 %copy-start.3 = (s32[768]{0:T(1024)S(1)}, s32[768]{0:T(1024)}, u32[]{:S(2)}) copy-start(s32[768]{0:T(1024)} %constant.26.clone) | copy-start | bytes 9220
  83.2 11.6 %copy-start.4 = (s32[768]{0:T(1024)S(1)}, s32[768]{0:T(1024)}, u32[]{:S(2)}) copy-start(s32[768]{0:T(1024)} %constant.27.clone) | copy-start | bytes 9220
  83.2 11.7 %copy-start.5 = (s32[768]{0:T(1024)S(1)}, s32[768]{0:T(1024)}, u32[]{:S(2)}) copy-start(s32[768]{0:T(1024)} %constant.28.clone) | copy-start | bytes 9220
  83.2 11.7 %copy-start.6 = (s32[768]{0:T(1024)S(1)}, s32[768]{0:T(1024)}, u32[]{:S(2)}) copy-start(s32[768]{0:T(1024)} %constant.29.clone) | copy-start | bytes 9220
  83.2 11.7 %copy-start.7 = (s32[768]{0:T(1024)S(1)}, s32[768]{0:T(1024)}, u32[]{:S(2)}) copy-start(s32[768]{0:T(1024)} %constant.30.clone) | copy-start | bytes 9220
  83.2 11.7 %copy-start.8 = (s32[768]{0:T(1024)S(1)}, s32[768]{0:T(1024)}, u32[]{:S(2)}) copy-start(s32[768]{0:T(1024)} %constant.31.clone) | copy-start | bytes 9220
  87.1 10.0 %collective-permute-start.10 = (bf16[12,16,4096]{2,1,0:T(8,128)(2,1)}, bf16[12,16,4096]{2,1,0:T(8,128)(2,1)}, u32[]{:S(2)}, u32[]{:S(2)}) collective-permute-start(bf16[12,16,4096]{2,1,0:T(8,128)(2,1)} %constant_dynamic-update-slice_fusion.6.rest_0_), channel_id=1, source_target_pairs={{0,16},{16,0},{32,48},{48,32},{64,80},{80,64},{96,112},{112,96},{1... | collective-permute-start | bytes 4718600 | tf_op jit(solution)/shard_map/ppermute | solution.py:20
  89.8 7.3 %collective-permute-start.15 = (bf16[4,64,1280]{2,1,0:T(8,128)(2,1)S(1)}, bf16[4,64,1280]{2,1,0:T(8,128)(2,1)}, u32[]{:S(2)}, u32[]{:S(2)}) collective-permute-start(bf16[4,64,1280]{2,1,0:T(8,128)(2,1)S(1)} %constant_dynamic-update-slice_fusion.18.rest_5_), channel_id=1, source_target_pairs={{0,16},{16,0},{32,48},{48,32},{64,80},{80,64},{96,112},{112,96},{1... | collective-permute-start | bytes 1966088 | tf_op jit(solution)/shard_map/ppermute | solution.py:20
  92.9 4.1 %collective-permute-start.11 = (bf16[4,16,4096]{2,1,0:T(8,128)(2,1)}, bf16[4,16,4096]{2,1,0:T(8,128)(2,1)}, u32[]{:S(2)}, u32[]{:S(2)}) collective-permute-start(bf16[4,16,4096]{2,1,0:T(8,128)(2,1)} %constant_dynamic-update-slice_fusion.11.rest_1_), channel_id=1, source_target_pairs={{0,16},{16,0},{32,48},{48,32},{64,80},{80,64},{96,112},{112,96},{1... | collective-permute-start | bytes 1572872 | tf_op jit(solution)/shard_map/ppermute | solution.py:20
  106.8 10.4 %copy-start.9 = (s32[128]{0:T(128)S(1)}, s32[128]{0:T(128)}, u32[]{:S(2)}) copy-start(s32[128]{0:T(128)} %param.15) | copy-start | bytes 1540
  106.8 10.5 %copy-start.2 = (f32[128,8]{0,1:T(8,128)S(1)}, f32[128,8]{0,1:T(8,128)}, u32[]{:S(2)}) copy-start(f32[128,8]{0,1:T(8,128)} %param.14) | copy-start | bytes 12292
  106.8 85.0 %all-to-all-start.1 = ((bf16[16,24,2048]{2,1,0:T(8,128)(2,1)}), bf16[16,24,2048]{2,1,0:T(8,128)(2,1)S(1)}, u32[]{:S(2)}, u32[]{:S(2)}) async-start(bf16[16,24,2048]{2,1,0:T(8,128)(2,1)} %bitcast.7), calls=%async_computation.1 | async-start | bytes 3145728 | tf_op jit(solution)/shard_map/all_to_all | solution.py:249

commit v4 on v3

--- a/solution.py
+++ b/solution.py
@@ -35,19 +35,23 @@
 
 def gather(a, b):
     for step in (1, 3):
-        a_in, b_in = lax.optimization_barrier(
-            (trade(a, flip(step << X_BIT)), trade(b, flip(step << Y_BIT)))
-        )
+        a_in = trade(a, flip(step << X_BIT))
+        if step == 1:
+            a_in, b = lax.optimization_barrier((a_in, b))
+        a_in, b_in = lax.optimization_barrier((a_in, trade(b, flip(step << Y_BIT))))
         a, b = jnp.concatenate([a, a_in], axis=0), jnp.concatenate([b, b_in], axis=0)
-    a_l, b_l, a_r, b_r = lax.optimization_barrier(
+    near = flip(CORE)
+    a_l, b_l, a_r, b_r, a_near, b_near = lax.optimization_barrier(
         (
             trade(a, turn(Y_BIT, 1)),
             trade(b, turn(X_BIT, 1)),
             trade(a, turn(Y_BIT, -1)),
             trade(b, turn(X_BIT, -1)),
+            trade(a, near),
+            trade(b, near),
         )
     )
-    a12, b12 = jnp.concatenate([a, a_l, a_r], axis=0), jnp.concatenate([b, b_l, b_r], axis=0)
+    a8, b8 = jnp.concatenate([a_l, a_r], axis=0), jnp.concatenate([b_l, b_r], axis=0)
     a_0, b_0, a_1, b_1 = (
         trade(a_l[:2], turn(Y_BIT, 1)),
         trade(b_l[:2], turn(X_BIT, 1)),
@@ -55,8 +59,10 @@
         trade(b_r[2:], turn(X_BIT, -1)),
     )
     a4, b4 = jnp.concatenate([a_0, a_1], axis=0), jnp.concatenate([b_0, b_1], axis=0)
-    near = flip(CORE)
-    return (a12, a4, trade(a12, near), trade(a4, near)), (b12, b4, trade(b12, near), trade(b4, near))
+    return (
+        (a, a8, a4, a_near, trade(a8, near), trade(a4, near)),
+        (b, b8, b4, b_near, trade(b8, near), trade(b4, near)),
+    )
 
 
 def shard_of(me, slot, x_first):
@@ -85,7 +91,7 @@
 
 def prepare_kernel(*refs, ring, cap):
     tok_hbm, gain_hbm, expert_hbm, both_hbm, down_hbm = refs[:5]
-    out_ref, a_ref, b_ref, tok_ref, gain_ref, expert_ref, sems = refs[5:]
+    out_hbm, a_ref, b_ref, out_ref, tok_ref, gain_ref, expert_ref, sems, sem_o = refs[5:]
     moves = [
         (tok_hbm, tok_ref),
         (gain_hbm, gain_ref),
@@ -115,27 +121,35 @@
     )
     slot = jnp.sum(jnp.where(member, earlier, 0.0), axis=0, keepdims=True).astype(jnp.int32)
     place = expert * cap + slot
-    pick = lax.broadcasted_iota(jnp.int32, (ring * cap, count), 0) == place
-    out_ref[...] = lax.dot_general(
-        pick.astype(F32).astype(BF16), normed, NN, preferred_element_type=F32
-    ).astype(BF16)
+    parts = sem_o.shape[0]
+    part = ring * cap // parts
+    for n in range(parts):
+        rows = pl.ds(n * part, part)
+        pick = lax.broadcasted_iota(jnp.int32, (part, count), 0) + n * part == place
+        out_ref[rows] = lax.dot_general(
+            pick.astype(F32).astype(BF16), normed, NN, preferred_element_type=F32
+        ).astype(BF16)
+        copies.append(pltpu.make_async_copy(out_ref.at[rows], out_hbm.at[rows], sem_o.at[n]))
+        copies[-1].start()
     for copy in copies[3:]:
         copy.wait()
 
 
-def expert_kernel(x_hbm, order_ref, *rest):
-    pieces_a, pieces_b = rest[:4], rest[4:8]
-    out_hbm, x_ref, out_ref, wa, wb, wd, hid, sem_x, sem_a, sem_b, sem_d, sem_o = rest[8:]
+def expert_kernel(x_ref, order_ref, *rest):
+    pieces_a, pieces_b = rest[:6], rest[6:12]
+    out_hbm, out_ref, wa, wb, wd, hid, sem_a, sem_b, sem_d, sem_o = rest[12:]
     width = x_ref.shape[1]
     me = lax.axis_index("dp")
-    copy_x = pltpu.make_async_copy(x_hbm, x_ref, sem_x)
     copies_a, copies_b, copies_d = [], [], []
     start = 0
     for q, (piece_a, piece_b) in enumerate(zip(pieces_a, pieces_b)):
         each = piece_a.shape[0]
-        copies_a.append(
-            pltpu.make_async_copy(piece_a, wa.at[pl.ds(start, each)], sem_a.at[q])
-        )
+        for p in range(0, each, 4):
+            copies_a.append(
+                pltpu.make_async_copy(
+                    piece_a.at[pl.ds(p, 4)], wa.at[pl.ds(start + p, 4)], sem_a.at[(start + p) // 4]
+                )
+            )
         for j in range(8):
             copies_b.append(
                 pltpu.make_async_copy(
@@ -154,9 +168,8 @@
                 )
             )
         start += each
-    for copy in [copy_x] + copies_a + copies_b + copies_d:
+    for copy in copies_a + copies_b + copies_d:
         copy.start()
-    copy_x.wait()
     x = x_ref[...]
 
     def units(w, cols):
@@ -165,8 +178,8 @@
         hid[:, cols] = (gate / (1.0 + jnp.exp(-gate)) * upper).astype(BF16)
 
     for c in range(2):
-        copies_a[2 * c].wait()
-        copies_a[2 * c + 1].wait()
+        for copy in copies_a[4 * c : 4 * (c + 1)]:
+            copy.wait()
         units(wa[16 * c : 16 * (c + 1)].reshape(256, 2 * width), slice(256 * c, 256 * (c + 1)))
     for copy in copies_b:
         copy.wait()
@@ -198,22 +211,20 @@
     return pl.pallas_call(
         expert_kernel,
         out_shape=jax.ShapeDtypeStruct((rows, width), BF16),
-        in_specs=[ANY, VMEM] + [ANY] * 8,
+        in_specs=[VMEM, VMEM] + [ANY] * 12,
         out_specs=ANY,
         scratch_shapes=[
-            pltpu.VMEM((rows, width), BF16),
             pltpu.VMEM((rows, width), BF16),
             pltpu.VMEM((shards, 16, 2 * width), BF16),
             pltpu.VMEM((shards, 8, 2 * width), BF16),
             pltpu.VMEM((shards, width // shards, ff), BF16),
             pltpu.VMEM((rows, ff), BF16),
-            pltpu.SemaphoreType.DMA,
-            pltpu.SemaphoreType.DMA((4,)),
-            pltpu.SemaphoreType.DMA((32,)),
+            pltpu.SemaphoreType.DMA((8,)),
+            pltpu.SemaphoreType.DMA((48,)),
             pltpu.SemaphoreType.DMA((32,)),
             pltpu.SemaphoreType.DMA((4,)),
         ],
-        compiler_params=pltpu.CompilerParams(vmem_limit_bytes=46 << 20),
+        compiler_params=pltpu.CompilerParams(vmem_limit_bytes=50 << 20),
         cost_estimate=pl.CostEstimate(
             flops=6 * rows * width * ff,
             bytes_accessed=6 * width * ff + 4 * x.size,
@@ -263,12 +274,14 @@
             jax.ShapeDtypeStruct((1, 64, 1280), BF16),
         ],
         in_specs=[ANY] * 5,
-        out_specs=[VMEM] * 3,
+        out_specs=[ANY, VMEM, VMEM],
         scratch_shapes=[
+            pltpu.VMEM((rows, width), BF16),
             pltpu.VMEM((tok_count, width), BF16),
             pltpu.VMEM((1, width), F32),
             pltpu.VMEM((1, tok_count), jnp.int32),
             pltpu.SemaphoreType.DMA((13,)),
+            pltpu.SemaphoreType.DMA((3,)),
         ],
         compiler_params=pltpu.CompilerParams(vmem_limit_bytes=60 << 20),
         cost_estimate=pl.CostEstimate(

time: 194 us -> 200 us (1.031)
  starting transfers between devices: 72.8 us -> 78.8 us
  local copies, waits for them, and re-layouts: 9.61 us -> 4.03 us
    ppermute x16 -> x18, waiting for transfers between devices: 21.4 us -> 26.1 us  [trade(): lax.ppermute(x, 'dp', [(i, where(i)) for i in range(lax.axis_size('dp'))])]
    ppermute x16 -> x18, starting transfers between devices: 47.1 us -> 51.4 us  [trade(): lax.ppermute(x, 'dp', [(i, where(i)) for i in range(lax.axis_size('dp'))])]
    all_to_all x2, waiting for transfers between devices: 75.5 us -> 71.2 us  [exchange(): lax.all_to_all(blocks, 'expert', split_axis=0, concat_axis=0, tiled=True)]
    unnamed x30 -> x25, local copies, waits for them, and re-layouts: 6.15 us -> 1.99 us
  transfers between devices with their start and end apart: 18 -> 20, of which waited for: 7 -> 5; matrix products, arithmetic and copies ran while one was open for 5% -> 3% of each run, Pallas kernels for 0% -> 0%
where the time goes in v4:
time: 200 us; the launch traced here: 198 us
  waiting for transfers between devices  97.3 us (49%)
  starting transfers between devices  78.8 us (39%)
  Pallas kernels  14.9 us (7%)
  local copies, waits for them, and re-layouts  4.03 us (2%)
  other arithmetic  2.08 us (1%)
    all_to_all x2, waiting for transfers between devices, exchange(): lax.all_to_all(blocks, 'expert', split_axis=0, concat_axis=0, tiled=True)  71.2 us
    ppermute x18, starting transfers between devices, trade(): lax.ppermute(x, 'dp', [(i, where(i)) for i in range(lax.axis_size('dp'))])  51.4 us
    all_to_all x2, starting transfers between devices, exchange(): lax.all_to_all(blocks, 'expert', split_axis=0, concat_axis=0, tiled=True)  27.3 us
    ppermute x18, waiting for transfers between devices, trade(): lax.ppermute(x, 'dp', [(i, where(i)) for i in range(lax.axis_size('dp'))])  26.1 us
    pallas_call x1, Pallas kernels, run_expert(): pl.pallas_call(expert_kernel, out_shape=jax.ShapeDtypeStruct((rows, width...  9.87 us
  transfers between devices with their start and end apart: 20, of which 5 were waited for; matrix products, arithmetic and copies ran while one was open for 3% of the time, Pallas kernels for 0%

profile of v4, /device:TPU:24, one launch (start us, length us, event | category | flops | bytes accessed | tf_op | source)
XLA Modules:
  0.0 197.6 jit_solution(17833146411192139992)
XLA Ops:
  0.0 3.5 %prepare.1 = (bf16[384,2048]{1,0:T(8,128)(2,1)}, bf16[1,16,4096]{2,1,0:T(8,128)(2,1)}, bf16[1,64,1280]{2,1,0:T(8,128)(2,1)}) custom-call(bf16[128,2048]{1,0:T(8,128)(2,1)} %refs_0_.1, f32[1,2048]{1,0:T(1,128)} %bitcast.14, s32[1,128]{1,0:T(1,128)} %bitcast.15, bf16[24,4096]{1,0:T(8,128)(2,1)} %bitcast.12, bf16[64,768]{1,0:T(8,128)(2,1)} %bitcast.13), custom_call_target="tpu_custom_call" | custom-call | flops 201326592 | bytes 2097152 | tf_op jit(solution)/shard_map/prepare/pallas_call | solution.py:269
  3.5 3.4 %collective-permute-start = (bf16[1,16,4096]{2,1,0:T(8,128)(2,1)}, bf16[1,16,4096]{2,1,0:T(8,128)(2,1)S(1)}, u32[]{:S(2)}, u32[]{:S(2)}) collective-permute-start(bf16[1,16,4096]{2,1,0:T(8,128)(2,1)} %get-tuple-element.21), channel_id=1, source_target_pairs={{0,128},{16,144},{32,160},{48,176},{64,192},{80,208},{96,224},{112... | collective-permute-start | bytes 393224 | tf_op jit(solution)/shard_map/ppermute | solution.py:20
  6.9 0.0 copy-start
  7.0 15.4 %all-to-all-start = ((bf16[16,24,2048]{2,1,0:T(8,128)(2,1)}), bf16[16,24,2048]{2,1,0:T(8,128)(2,1)}, u32[]{:S(2)}, u32[]{:S(2)}) async-start(bf16[16,24,2048]{2,1,0:T(8,128)(2,1)} %bitcast.11), calls=%async_computation | async-start | bytes 3145728 | tf_op jit(solution)/shard_map/all_to_all | solution.py:260
  22.4 0.0 collective-permute-done
  22.4 2.7 %collective-permute-start.1 = (bf16[1,64,1280]{2,1,0:T(8,128)(2,1)S(1)}, bf16[1,64,1280]{2,1,0:T(8,128)(2,1)S(1)}, u32[]{:S(2)}, u32[]{:S(2)}) collective-permute-start(bf16[1,64,1280]{2,1,0:T(8,128)(2,1)S(1)} %copy-done), channel_id=1, source_target_pairs={{0,32},{16,48},{32,0},{48,16},{64,96},{80,112},{96,64},{112,80},{1... | collective-permute-start | bytes 491528 | tf_op jit(solution)/shard_map/ppermute | solution.py:20
  25.1 4.6 %collective-permute-done.1 = bf16[1,64,1280]{2,1,0:T(8,128)(2,1)S(1)} collective-permute-done((bf16[1,64,1280]{2,1,0:T(8,128)(2,1)S(1)}, bf16[1,64,1280]{2,1,0:T(8,128)(2,1)S(1)}, u32[]{:S(2)}, u32[]{:S(2)}) %collective-permute-start.1) | collective-permute-done | bytes 163872 | tf_op jit(solution)/shard_map/ppermute | solution.py:20
  29.7 2.1 %collective-permute-start.3 = (bf16[2,64,1280]{2,1,0:T(8,128)(2,1)S(1)}, bf16[2,64,1280]{2,1,0:T(8,128)(2,1)S(1)}, u32[]{:S(2)}, u32[]{:S(2)}) collective-permute-start(bf16[2,64,1280]{2,1,0:T(8,128)(2,1)S(1)} %pad_maximum_fusion), channel_id=1, source_target_pairs={{0,96},{16,112},{32,64},{48,80},{64,32},{80,48},{96,0},{112,16},{1... | collective-permute-start | bytes 983048 | tf_op jit(solution)/shard_map/ppermute | solution.py:20
  31.9 4.0 %collective-permute-start.2 = (bf16[2,16,4096]{2,1,0:T(8,128)(2,1)S(1)}, bf16[2,16,4096]{2,1,0:T(8,128)(2,1)S(1)}, u32[]{:S(2)}, u32[]{:S(2)}) collective-permute-start(bf16[2,16,4096]{2,1,0:T(8,128)(2,1)S(1)} %pad_maximum_fusion.1), channel_id=1, source_target_pairs={{0,384},{16,400},{32,416},{48,432},{64,448},{80,464},{96,480},{112... | collective-permute-start | bytes 786440 | tf_op jit(solution)/shard_map/ppermute | solution.py:20
  35.9 5.4 %collective-permute-done.2 = bf16[2,16,4096]{2,1,0:T(8,128)(2,1)S(1)} collective-permute-done((bf16[2,16,4096]{2,1,0:T(8,128)(2,1)S(1)}, bf16[2,16,4096]{2,1,0:T(8,128)(2,1)S(1)}, u32[]{:S(2)}, u32[]{:S(2)}) %collective-permute-start.2) | collective-permute-done | bytes 262176 | tf_op jit(solution)/shard_map/ppermute | solution.py:20
  41.4 0.0 collective-permute-done.3
  41.4 4.9 %collective-permute-start.4 = (bf16[4,16,4096]{2,1,0:T(8,128)(2,1)S(1)}, bf16[4,16,4096]{2,1,0:T(8,128)(2,1)S(1)}, u32[]{:S(2)}, u32[]{:S(2)}) collective-permute-start(bf16[4,16,4096]{2,1,0:T(8,128)(2,1)S(1)} %constant_dynamic-update-slice_fusion.rest_0_), channel_id=1, source_target_pairs={{0,32},{16,48},{32,64},{48,80},{64,96},{80,112},{96,0},{112,16},{1... | collective-permute-start | bytes 1572872 | tf_op jit(solution)/shard_map/ppermute | solution.py:20
  46.4 1.9 collective-permute-start.5
  48.3 5.1 %collective-permute-start.7 = (bf16[4,64,1280]{2,1,0:T(8,128)(2,1)S(1)}, bf16[4,64,1280]{2,1,0:T(8,128)(2,1)S(1)}, u32[]{:S(2)}, u32[]{:S(2)}) collective-permute-start(bf16[4,64,1280]{2,1,0:T(8,128)(2,1)S(1)} %constant_dynamic-update-slice_fusion.3.rest_6_), channel_id=1, source_target_pairs={{0,384},{16,400},{32,416},{48,432},{64,448},{80,464},{96,480},{112... | collective-permute-start | bytes 1966088 | tf_op jit(solution)/shard_map/ppermute | solution.py:20
  53.4 1.9 collective-permute-start.9
  55.4 1.9 collective-permute-start.6
  57.3 2.4 %collective-permute-start.8 = (bf16[4,16,4096]{2,1,0:T(8,128)(2,1)S(1)}, bf16[4,16,4096]{2,1,0:T(8,128)(2,1)S(1)}, u32[]{:S(2)}, u32[]{:S(2)}) collective-permute-start(bf16[4,16,4096]{2,1,0:T(8,128)(2,1)S(1)} %constant_dynamic-update-slice_fusion.rest_0_), channel_id=1, source_target_pairs={{0,16},{16,0},{32,48},{48,32},{64,80},{80,64},{96,112},{112,96},{1... | collective-permute-start | bytes 1572872 | tf_op jit(solution)/shard_map/ppermute | solution.py:20
  59.7 13.1 %collective-permute-done.6 = bf16[4,16,4096]{2,1,0:T(8,128)(2,1)S(1)} collective-permute-done((bf16[4,16,4096]{2,1,0:T(8,128)(2,1)S(1)}, bf16[4,16,4096]{2,1,0:T(8,128)(2,1)S(1)}, u32[]{:S(2)}, u32[]{:S(2)}) %collective-permute-start.6) | collective-permute-done | bytes 524320 | tf_op jit(solution)/shard_map/ppermute | solution.py:20
  72.8 0.0 collective-permute-done.5
  72.8 0.0 collective-permute-done.7
  72.8 0.0 collective-permute-done.9.rest_9_
  72.8 1.9 collective-permute-start.14
  74.8 5.1 %collective-permute-start.15 = (bf16[2,64,1280]{2,1,0:T(8,128)(2,1)S(1)}, bf16[2,64,1280]{2,1,0:T(8,128)(2,1)S(1)}, u32[]{:S(2)}, u32[]{:S(2)}) collective-permute-start(bf16[2,64,1280]{2,1,0:T(8,128)(2,1)S(1)} %slice.15), channel_id=1, source_target_pairs={{0,384},{16,400},{32,416},{48,432},{64,448},{80,464},{96,480},{112... | collective-permute-start | bytes 983048 | tf_op jit(solution)/shard_map/ppermute | solution.py:20
  79.9 0.9 constant_dynamic-update-slice_fusion.11
  80.8 0.9 constant_dynamic-update-slice_fusion.10.rest_7_
  81.7 1.9 collective-permute-start.16
  83.7 1.9 collective-permute-start.10
  85.6 3.9 %collective-permute-start.11 = (bf16[2,16,4096]{2,1,0:T(8,128)(2,1)S(1)}, bf16[2,16,4096]{2,1,0:T(8,128)(2,1)S(1)}, u32[]{:S(2)}, u32[]{:S(2)}) collective-permute-start(bf16[2,16,4096]{2,1,0:T(8,128)(2,1)S(1)} %slice.13), channel_id=1, source_target_pairs={{0,96},{16,112},{32,0},{48,16},{64,32},{80,48},{96,64},{112,80},{1... | collective-permute-start | bytes 786440 | tf_op jit(solution)/shard_map/ppermute | solution.py:20
  89.6 0.9 constant_dynamic-update-slice_fusion.7
  90.4 0.9 constant_dynamic-update-slice_fusion.6.rest_1_
  91.3 3.0 %collective-permute-done.10 = bf16[2,16,4096]{2,1,0:T(8,128)(2,1)S(1)} collective-permute-done((bf16[2,16,4096]{2,1,0:T(8,128)(2,1)S(1)}, bf16[2,16,4096]{2,1,0:T(8,128)(2,1)S(1)}, u32[]{:S(2)}, u32[]{:S(2)}) %collective-permute-start.10) | collective-permute-done | bytes 262176 | tf_op jit(solution)/shard_map/ppermute | solution.py:20
  94.3 1.9 collective-permute-start.12
  96.3 2.4 %collective-permute-start.17 = (bf16[4,64,1280]{2,1,0:T(8,128)(2,1)S(1)}, bf16[4,64,1280]{2,1,0:T(8,128)(2,1)}, u32[]{:S(2)}, u32[]{:S(2)}) collective-permute-start(bf16[4,64,1280]{2,1,0:T(8,128)(2,1)S(1)} %constant_dynamic-update-slice_fusion.12.rest_8_), channel_id=1, source_target_pairs={{0,16},{16,0},{32,48},{48,32},{64,80},{80,64},{96,112},{112,96},{1... | collective-permute-start | bytes 1966088 | tf_op jit(solution)/shard_map/ppermute | solution.py:20
  98.7 0.0 collective-permute-done.11
  98.8 1.9 collective-permute-start.13
  100.7 0.7 multiply_add_fusion
  101.5 1.3 fusion.order_ref
  102.8 0.0 collective-permute-done.13.rest_5_
  102.8 0.0 collective-permute-done.17.rest_11_
  102.8 0.0 collective-permute-done.12.rest_4_
  102.8 9.9 %expert.1 = bf16[384,2048]{1,0:T(8,128)(2,1)} custom-call(bf16[384,2048]{1,0:T(8,128)(2,1)} %bitcast.6.x_ref, bf16[768,768]{1,0:T(8,128)(2,1)} %fusion.order_ref, bf16[4,16,4096]{2,1,0:T(8,128)(2,1)S(1)} %constant_dynamic-update-slice_fusion.rest_0_, bf16[8,16,4096]{2,1,0:T(8,128)(2,1)} %constant_dynamic-update-slice_fusion.6.rest_1_, ...), custom_call_target="tpu_custom_call" | custom-call | flops 3623878656 | bytes 12582912 | tf_op jit(solution)/shard_map/expert/pallas_call | solution.py:211
  112.7 0.0 copy-start.7
  112.7 0.0 copy-start.2
  112.7 11.9 %all-to-all-start.1 = ((bf16[16,24,2048]{2,1,0:T(8,128)(2,1)}), bf16[16,24,2048]{2,1,0:T(8,128)(2,1)S(1)}, u32[]{:S(2)}, u32[]{:S(2)}) async-start(bf16[16,24,2048]{2,1,0:T(8,128)(2,1)} %bitcast.10), calls=%async_computation.1 | async-start | bytes 3145728 | tf_op jit(solution)/shard_map/all_to_all | solution.py:260
  124.6 0.1 copy.13.expert_ref
  124.7 0.1 copy.14.probs_ref
  124.8 71.2 %all-to-all-done.1 = bf16[16,24,2048]{2,1,0:T(8,128)(2,1)S(1)} async-done(((bf16[16,24,2048]{2,1,0:T(8,128)(2,1)}), bf16[16,24,2048]{2,1,0:T(8,128)(2,1)S(1)}, u32[]{:S(2)}, u32[]{:S(2)}) %all-to-all-start.1) | async-done | bytes 1572896 | tf_op jit(solution)/shard_map/all_to_all | solution.py:260
  196.1 1.6 last.1
  (35 shorter events, 0.4 us)
Async XLA Ops:
  3.5 18.9 %collective-permute-start = (bf16[1,16,4096]{2,1,0:T(8,128)(2,1)}, bf16[1,16,4096]{2,1,0:T(8,128)(2,1)S(1)}, u32[]{:S(2)}, u32[]{:S(2)}) collective-permute-start(bf16[1,16,4096]{2,1,0:T(8,128)(2,1)} %get-tuple-element.21), channel_id=1, source_target_pairs={{0,128},{16,144},{32,160},{48,176},{64,192},{80,208},{96,224},{112... | collective-permute-start | bytes 393224 | tf_op jit(solution)/shard_map/ppermute | solution.py:20
  6.9 15.4 %copy-start.1 = (bf16[1,16,4096]{2,1,0:T(8,128)(2,1)S(1)}, bf16[1,16,4096]{2,1,0:T(8,128)(2,1)}, u32[]{:S(2)}) copy-start(bf16[1,16,4096]{2,1,0:T(8,128)(2,1)} %get-tuple-element.21) | copy-start | bytes 393220
  6.9 15.4 %copy-start = (bf16[1,64,1280]{2,1,0:T(8,128)(2,1)S(1)}, bf16[1,64,1280]{2,1,0:T(8,128)(2,1)}, u32[]{:S(2)}) copy-start(bf16[1,64,1280]{2,1,0:T(8,128)(2,1)} %get-tuple-element.24) | copy-start | bytes 491524
  7.0 95.8 %all-to-all-start = ((bf16[16,24,2048]{2,1,0:T(8,128)(2,1)}), bf16[16,24,2048]{2,1,0:T(8,128)(2,1)}, u32[]{:S(2)}, u32[]{:S(2)}) async-start(bf16[16,24,2048]{2,1,0:T(8,128)(2,1)} %bitcast.11), calls=%async_computation | async-start | bytes 3145728 | tf_op jit(solution)/shard_map/all_to_all | solution.py:260
  22.4 7.3 %collective-permute-start.1 = (bf16[1,64,1280]{2,1,0:T(8,128)(2,1)S(1)}, bf16[1,64,1280]{2,1,0:T(8,128)(2,1)S(1)}, u32[]{:S(2)}, u32[]{:S(2)}) collective-permute-start(bf16[1,64,1280]{2,1,0:T(8,128)(2,1)S(1)} %copy-done), channel_id=1, source_target_pairs={{0,32},{16,48},{32,0},{48,16},{64,96},{80,112},{96,64},{112,80},{1... | collective-permute-start | bytes 491528 | tf_op jit(solution)/shard_map/ppermute | solution.py:20
  29.7 11.7 %collective-permute-start.3 = (bf16[2,64,1280]{2,1,0:T(8,128)(2,1)S(1)}, bf16[2,64,1280]{2,1,0:T(8,128)(2,1)S(1)}, u32[]{:S(2)}, u32[]{:S(2)}) collective-permute-start(bf16[2,64,1280]{2,1,0:T(8,128)(2,1)S(1)} %pad_maximum_fusion), channel_id=1, source_target_pairs={{0,96},{16,112},{32,64},{48,80},{64,32},{80,48},{96,0},{112,16},{1... | collective-permute-start | bytes 983048 | tf_op jit(solution)/shard_map/ppermute | solution.py:20
  31.9 9.5 %collective-permute-start.2 = (bf16[2,16,4096]{2,1,0:T(8,128)(2,1)S(1)}, bf16[2,16,4096]{2,1,0:T(8,128)(2,1)S(1)}, u32[]{:S(2)}, u32[]{:S(2)}) collective-permute-start(bf16[2,16,4096]{2,1,0:T(8,128)(2,1)S(1)} %pad_maximum_fusion.1), channel_id=1, source_target_pairs={{0,384},{16,400},{32,416},{48,432},{64,448},{80,464},{96,480},{112... | collective-permute-start | bytes 786440 | tf_op jit(solution)/shard_map/ppermute | solution.py:20
  41.4 15.9 %collective-permute-start.4 = (bf16[4,16,4096]{2,1,0:T(8,128)(2,1)S(1)}, bf16[4,16,4096]{2,1,0:T(8,128)(2,1)S(1)}, u32[]{:S(2)}, u32[]{:S(2)}) collective-permute-start(bf16[4,16,4096]{2,1,0:T(8,128)(2,1)S(1)} %constant_dynamic-update-slice_fusion.rest_0_), channel_id=1, source_target_pairs={{0,32},{16,48},{32,64},{48,80},{64,96},{80,112},{96,0},{112,16},{1... | collective-permute-start | bytes 1572872 | tf_op jit(solution)/shard_map/ppermute | solution.py:20
  46.4 26.4 %collective-permute-start.5 = (bf16[4,64,1280]{2,1,0:T(8,128)(2,1)S(1)}, bf16[4,64,1280]{2,1,0:T(8,128)(2,1)S(1)}, u32[]{:S(2)}, u32[]{:S(2)}) collective-permute-start(bf16[4,64,1280]{2,1,0:T(8,128)(2,1)S(1)} %constant_dynamic-update-slice_fusion.3.rest_6_), channel_id=1, source_target_pairs={{0,128},{16,144},{32,160},{48,176},{64,192},{80,208},{96,224},{112... | collective-permute-start | bytes 1966088 | tf_op jit(solution)/shard_map/ppermute | solution.py:20
  48.3 24.5 %collective-permute-start.7 = (bf16[4,64,1280]{2,1,0:T(8,128)(2,1)S(1)}, bf16[4,64,1280]{2,1,0:T(8,128)(2,1)S(1)}, u32[]{:S(2)}, u32[]{:S(2)}) collective-permute-start(bf16[4,64,1280]{2,1,0:T(8,128)(2,1)S(1)} %constant_dynamic-update-slice_fusion.3.rest_6_), channel_id=1, source_target_pairs={{0,384},{16,400},{32,416},{48,432},{64,448},{80,464},{96,480},{112... | collective-permute-start | bytes 1966088 | tf_op jit(solution)/shard_map/ppermute | solution.py:20
  53.4 19.4 %collective-permute-start.9 = (bf16[4,64,1280]{2,1,0:T(8,128)(2,1)S(1)}, bf16[4,64,1280]{2,1,0:T(8,128)(2,1)S(1)}, u32[]{:S(2)}, u32[]{:S(2)}) collective-permute-start(bf16[4,64,1280]{2,1,0:T(8,128)(2,1)S(1)} %constant_dynamic-update-slice_fusion.3.rest_6_), channel_id=1, source_target_pairs={{0,16},{16,0},{32,48},{48,32},{64,80},{80,64},{96,112},{112,96},{1... | collective-permute-start | bytes 1966088 | tf_op jit(solution)/shard_map/ppermute | solution.py:20
  55.4 17.4 %collective-permute-start.6 = (bf16[4,16,4096]{2,1,0:T(8,128)(2,1)S(1)}, bf16[4,16,4096]{2,1,0:T(8,128)(2,1)S(1)}, u32[]{:S(2)}, u32[]{:S(2)}) collective-permute-start(bf16[4,16,4096]{2,1,0:T(8,128)(2,1)S(1)} %constant_dynamic-update-slice_fusion.rest_0_), channel_id=1, source_target_pairs={{0,96},{16,112},{32,0},{48,16},{64,32},{80,48},{96,64},{112,80},{1... | collective-permute-start | bytes 1572872 | tf_op jit(solution)/shard_map/ppermute | solution.py:20
  57.3 15.5 %collective-permute-start.8 = (bf16[4,16,4096]{2,1,0:T(8,128)(2,1)S(1)}, bf16[4,16,4096]{2,1,0:T(8,128)(2,1)S(1)}, u32[]{:S(2)}, u32[]{:S(2)}) collective-permute-start(bf16[4,16,4096]{2,1,0:T(8,128)(2,1)S(1)} %constant_dynamic-update-slice_fusion.rest_0_), channel_id=1, source_target_pairs={{0,16},{16,0},{32,48},{48,32},{64,80},{80,64},{96,112},{112,96},{1... | collective-permute-start | bytes 1572872 | tf_op jit(solution)/shard_map/ppermute | solution.py:20
  72.8 23.4 %collective-permute-start.14 = (bf16[2,64,1280]{2,1,0:T(8,128)(2,1)S(1)}, bf16[2,64,1280]{2,1,0:T(8,128)(2,1)S(1)}, u32[]{:S(2)}, u32[]{:S(2)}) collective-permute-start(bf16[2,64,1280]{2,1,0:T(8,128)(2,1)S(1)} %slice.14), channel_id=1, source_target_pairs={{0,128},{16,144},{32,160},{48,176},{64,192},{80,208},{96,224},{112... | collective-permute-start | bytes 983048 | tf_op jit(solution)/shard_map/ppermute | solution.py:20
  74.8 21.5 %collective-permute-start.15 = (bf16[2,64,1280]{2,1,0:T(8,128)(2,1)S(1)}, bf16[2,64,1280]{2,1,0:T(8,128)(2,1)S(1)}, u32[]{:S(2)}, u32[]{:S(2)}) collective-permute-start(bf16[2,64,1280]{2,1,0:T(8,128)(2,1)S(1)} %slice.15), channel_id=1, source_target_pairs={{0,384},{16,400},{32,416},{48,432},{64,448},{80,464},{96,480},{112... | collective-permute-start | bytes 983048 | tf_op jit(solution)/shard_map/ppermute | solution.py:20
  81.7 21.0 %collective-permute-start.16 = (bf16[8,64,1280]{2,1,0:T(8,128)(2,1)}, bf16[8,64,1280]{2,1,0:T(8,128)(2,1)}, u32[]{:S(2)}, u32[]{:S(2)}) collective-permute-start(bf16[8,64,1280]{2,1,0:T(8,128)(2,1)} %constant_dynamic-update-slice_fusion.10.rest_7_), channel_id=1, source_target_pairs={{0,16},{16,0},{32,48},{48,32},{64,80},{80,64},{96,112},{112,96},{1... | collective-permute-start | bytes 3932168 | tf_op jit(solution)/shard_map/ppermute | solution.py:20
  83.7 10.6 %collective-permute-start.10 = (bf16[2,16,4096]{2,1,0:T(8,128)(2,1)S(1)}, bf16[2,16,4096]{2,1,0:T(8,128)(2,1)S(1)}, u32[]{:S(2)}, u32[]{:S(2)}) collective-permute-start(bf16[2,16,4096]{2,1,0:T(8,128)(2,1)S(1)} %slice.12), channel_id=1, source_target_pairs={{0,32},{16,48},{32,64},{48,80},{64,96},{80,112},{96,0},{112,16},{1... | collective-permute-start | bytes 786440 | tf_op jit(solution)/shard_map/ppermute | solution.py:20
  85.6 13.1 %collective-permute-start.11 = (bf16[2,16,4096]{2,1,0:T(8,128)(2,1)S(1)}, bf16[2,16,4096]{2,1,0:T(8,128)(2,1)S(1)}, u32[]{:S(2)}, u32[]{:S(2)}) collective-permute-start(bf16[2,16,4096]{2,1,0:T(8,128)(2,1)S(1)} %slice.13), channel_id=1, source_target_pairs={{0,96},{16,112},{32,0},{48,16},{64,32},{80,48},{96,64},{112,80},{1... | collective-permute-start | bytes 786440 | tf_op jit(solution)/shard_map/ppermute | solution.py:20
  91.3 9.4 %copy-start.3 = (s32[768]{0:T(1024)S(1)}, s32[768]{0:T(1024)}, u32[]{:S(2)}) copy-start(s32[768]{0:T(1024)} %constant.26.clone) | copy-start | bytes 9220
  91.3 9.4 %copy-start.4 = (s32[768]{0:T(1024)S(1)}, s32[768]{0:T(1024)}, u32[]{:S(2)}) copy-start(s32[768]{0:T(1024)} %constant.27.clone) | copy-start | bytes 9220
  91.3 9.4 %copy-start.5 = (s32[768]{0:T(1024)S(1)}, s32[768]{0:T(1024)}, u32[]{:S(2)}) copy-start(s32[768]{0:T(1024)} %constant.28.clone) | copy-start | bytes 9220
  91.3 9.4 %copy-start.6 = (s32[768]{0:T(1024)S(1)}, s32[768]{0:T(1024)}, u32[]{:S(2)}) copy-start(s32[768]{0:T(1024)} %constant.29.clone) | copy-start | bytes 9220
  94.3 8.5 %collective-permute-start.12 = (bf16[8,16,4096]{2,1,0:T(8,128)(2,1)}, bf16[8,16,4096]{2,1,0:T(8,128)(2,1)}, u32[]{:S(2)}, u32[]{:S(2)}) collective-permute-start(bf16[8,16,4096]{2,1,0:T(8,128)(2,1)} %constant_dynamic-update-slice_fusion.6.rest_1_), channel_id=1, source_target_pairs={{0,16},{16,0},{32,48},{48,32},{64,80},{80,64},{96,112},{112,96},{1... | collective-permute-start | bytes 3145736 | tf_op jit(solution)/shard_map/ppermute | solution.py:20
  96.3 6.5 %collective-permute-start.17 = (bf16[4,64,1280]{2,1,0:T(8,128)(2,1)S(1)}, bf16[4,64,1280]{2,1,0:T(8,128)(2,1)}, u32[]{:S(2)}, u32[]{:S(2)}) collective-permute-start(bf16[4,64,1280]{2,1,0:T(8,128)(2,1)S(1)} %constant_dynamic-update-slice_fusion.12.rest_8_), channel_id=1, source_target_pairs={{0,16},{16,0},{32,48},{48,32},{64,80},{80,64},{96,112},{112,96},{1... | collective-permute-start | bytes 1966088 | tf_op jit(solution)/shard_map/ppermute | solution.py:20
  98.8 4.0 %collective-permute-start.13 = (bf16[4,16,4096]{2,1,0:T(8,128)(2,1)S(1)}, bf16[4,16,4096]{2,1,0:T(8,128)(2,1)}, u32[]{:S(2)}, u32[]{:S(2)}) collective-permute-start(bf16[4,16,4096]{2,1,0:T(8,128)(2,1)S(1)} %constant_dynamic-update-slice_fusion.8.rest_2_), channel_id=1, source_target_pairs={{0,16},{16,0},{32,48},{48,32},{64,80},{80,64},{96,112},{112,96},{1... | collective-permute-start | bytes 1572872 | tf_op jit(solution)/shard_map/ppermute | solution.py:20
  112.7 12.0 %copy-start.7 = (s32[128]{0:T(128)S(1)}, s32[128]{0:T(128)}, u32[]{:S(2)}) copy-start(s32[128]{0:T(128)} %param.15) | copy-start | bytes 1540
  112.7 12.1 %copy-start.2 = (f32[128,8]{0,1:T(8,128)S(1)}, f32[128,8]{0,1:T(8,128)}, u32[]{:S(2)}) copy-start(f32[128,8]{0,1:T(8,128)} %param.14) | copy-start | bytes 12292
  112.7 83.4 %all-to-all-start.1 = ((bf16[16,24,2048]{2,1,0:T(8,128)(2,1)}), bf16[16,24,2048]{2,1,0:T(8,128)(2,1)S(1)}, u32[]{:S(2)}, u32[]{:S(2)}) async-start(bf16[16,24,2048]{2,1,0:T(8,128)(2,1)} %bitcast.10), calls=%async_computation.1 | async-start | bytes 3145728 | tf_op jit(solution)/shard_map/all_to_all | solution.py:260

commit v5 on v3

--- a/solution.py
+++ b/solution.py
@@ -154,7 +154,7 @@
                 )
             )
         start += each
-    for copy in [copy_x] + copies_a + copies_b + copies_d:
+    for copy in [copy_x] + copies_a:
         copy.start()
     copy_x.wait()
     x = x_ref[...]
@@ -167,6 +167,8 @@
     for c in range(2):
         copies_a[2 * c].wait()
         copies_a[2 * c + 1].wait()
+        for copy in (copies_b, copies_d)[c]:
+            copy.start()
         units(wa[16 * c : 16 * (c + 1)].reshape(256, 2 * width), slice(256 * c, 256 * (c + 1)))
     for copy in copies_b:
         copy.wait()

time: 194 us -> 194 us (level)
  no operation moved by 1% of the time
where the time goes in v5:
time: 194 us; the launch traced here: 193 us
  waiting for transfers between devices  96.9 us (50%)
  starting transfers between devices  72.8 us (38%)
  Pallas kernels  13.3 us (7%)
  local copies, waits for them, and re-layouts  9.61 us (5%)
    all_to_all x2, waiting for transfers between devices, exchange(): lax.all_to_all(blocks, 'expert', split_axis=0, concat_axis=0, tiled=True)  75.5 us
    ppermute x16, starting transfers between devices, trade(): lax.ppermute(x, 'dp', [(i, where(i)) for i in range(lax.axis_size('dp'))])  47.1 us
    all_to_all x2, starting transfers between devices, exchange(): lax.all_to_all(blocks, 'expert', split_axis=0, concat_axis=0, tiled=True)  25.7 us
    ppermute x16, waiting for transfers between devices, trade(): lax.ppermute(x, 'dp', [(i, where(i)) for i in range(lax.axis_size('dp'))])  21.4 us
    pallas_call x1, Pallas kernels, run_expert(): pl.pallas_call(expert_kernel, out_shape=jax.ShapeDtypeStruct((rows, width...  8.52 us
    unnamed x30, local copies, waits for them, and re-layouts  6.15 us
  transfers between devices with their start and end apart: 18, of which 7 were waited for; matrix products, arithmetic and copies ran while one was open for 5% of the time, Pallas kernels for 0%

profile of v5, /device:TPU:24, one launch (start us, length us, event | category | flops | bytes accessed | tf_op | source)
XLA Modules:
  0.0 193.3 jit_solution(12097464618548585497)
XLA Ops:
  0.0 3.2 %prepare.1 = (bf16[384,2048]{1,0:T(8,128)(2,1)}, bf16[1,16,4096]{2,1,0:T(8,128)(2,1)}, bf16[1,64,1280]{2,1,0:T(8,128)(2,1)}) custom-call(bf16[128,2048]{1,0:T(8,128)(2,1)} %refs_0_.1, f32[1,2048]{1,0:T(1,128)} %bitcast.14, s32[1,128]{1,0:T(1,128)} %bitcast.15, bf16[24,4096]{1,0:T(8,128)(2,1)} %bitcast.12, bf16[64,768]{1,0:T(8,128)(2,1)} %bitcast.13), custom_call_target="tpu_custom_call" | custom-call | flops 201326592 | bytes 2097152 | tf_op jit(solution)/shard_map/prepare/pallas_call | solution.py:260
  3.2 2.7 %collective-permute-start.1 = (bf16[1,64,1280]{2,1,0:T(8,128)(2,1)}, bf16[1,64,1280]{2,1,0:T(8,128)(2,1)S(1)}, u32[]{:S(2)}, u32[]{:S(2)}) collective-permute-start(bf16[1,64,1280]{2,1,0:T(8,128)(2,1)} %get-tuple-element.18), channel_id=1, source_target_pairs={{0,32},{16,48},{32,0},{48,16},{64,96},{80,112},{96,64},{112,80},{1... | collective-permute-start | bytes 491528 | tf_op jit(solution)/shard_map/ppermute | solution.py:20
  5.8 3.4 %collective-permute-start = (bf16[1,16,4096]{2,1,0:T(8,128)(2,1)}, bf16[1,16,4096]{2,1,0:T(8,128)(2,1)S(1)}, u32[]{:S(2)}, u32[]{:S(2)}) collective-permute-start(bf16[1,16,4096]{2,1,0:T(8,128)(2,1)} %get-tuple-element.17), channel_id=1, source_target_pairs={{0,128},{16,144},{32,160},{48,176},{64,192},{80,208},{96,224},{112... | collective-permute-start | bytes 393224 | tf_op jit(solution)/shard_map/ppermute | solution.py:20
  9.3 0.0 copy-start
  9.3 15.3 %all-to-all-start = ((bf16[16,24,2048]{2,1,0:T(8,128)(2,1)}), bf16[16,24,2048]{2,1,0:T(8,128)(2,1)S(1)}, u32[]{:S(2)}, u32[]{:S(2)}) async-start(bf16[16,24,2048]{2,1,0:T(8,128)(2,1)} %bitcast.11), calls=%async_computation | async-start | bytes 3145728 | tf_op jit(solution)/shard_map/all_to_all | solution.py:251
  24.6 0.7 constant_dynamic-update-slice_fusion.2
  25.3 0.7 constant_dynamic-update-slice_fusion.17
  26.0 3.0 %collective-permute-start.3 = (bf16[2,64,1280]{2,1,0:T(8,128)(2,1)S(1)}, bf16[2,64,1280]{2,1,0:T(8,128)(2,1)S(1)}, u32[]{:S(2)}, u32[]{:S(2)}) collective-permute-start(bf16[2,64,1280]{2,1,0:T(8,128)(2,1)S(1)} %pad_maximum_fusion), channel_id=1, source_target_pairs={{0,96},{16,112},{32,64},{48,80},{64,32},{80,48},{96,0},{112,16},{1... | collective-permute-start | bytes 983048 | tf_op jit(solution)/shard_map/ppermute | solution.py:20
  29.0 4.0 %collective-permute-start.2 = (bf16[2,16,4096]{2,1,0:T(8,128)(2,1)S(1)}, bf16[2,16,4096]{2,1,0:T(8,128)(2,1)S(1)}, u32[]{:S(2)}, u32[]{:S(2)}) collective-permute-start(bf16[2,16,4096]{2,1,0:T(8,128)(2,1)S(1)} %pad_maximum_fusion.1), channel_id=1, source_target_pairs={{0,384},{16,400},{32,416},{48,432},{64,448},{80,464},{96,480},{112... | collective-permute-start | bytes 786440 | tf_op jit(solution)/shard_map/ppermute | solution.py:20
  33.0 0.7 constant_dynamic-update-slice_fusion.1
  33.7 0.7 constant_dynamic-update-slice_fusion.16
  34.4 4.7 %collective-permute-done.2 = bf16[2,16,4096]{2,1,0:T(8,128)(2,1)S(1)} collective-permute-done((bf16[2,16,4096]{2,1,0:T(8,128)(2,1)S(1)}, bf16[2,16,4096]{2,1,0:T(8,128)(2,1)S(1)}, u32[]{:S(2)}, u32[]{:S(2)}) %collective-permute-start.2) | collective-permute-done | bytes 262176 | tf_op jit(solution)/shard_map/ppermute | solution.py:20
  39.0 0.8 constant_dynamic-update-slice_fusion.15
  39.8 1.9 collective-permute-start.5
  41.7 5.1 %collective-permute-start.7 = (bf16[4,64,1280]{2,1,0:T(8,128)(2,1)S(1)}, bf16[4,64,1280]{2,1,0:T(8,128)(2,1)S(1)}, u32[]{:S(2)}, u32[]{:S(2)}) collective-permute-start(bf16[4,64,1280]{2,1,0:T(8,128)(2,1)S(1)} %get-tuple-element.28), channel_id=1, source_target_pairs={{0,384},{16,400},{32,416},{48,432},{64,448},{80,464},{96,480},{112... | collective-permute-start | bytes 1966088 | tf_op jit(solution)/shard_map/ppermute | solution.py:20
  46.9 0.7 constant_dynamic-update-slice_fusion
  47.6 4.1 %collective-permute-start.4 = (bf16[4,16,4096]{2,1,0:T(8,128)(2,1)S(1)}, bf16[4,16,4096]{2,1,0:T(8,128)(2,1)S(1)}, u32[]{:S(2)}, u32[]{:S(2)}) collective-permute-start(bf16[4,16,4096]{2,1,0:T(8,128)(2,1)S(1)} %get-tuple-element.29), channel_id=1, source_target_pairs={{0,32},{16,48},{32,64},{48,80},{64,96},{80,112},{96,0},{112,16},{1... | collective-permute-start | bytes 1572872 | tf_op jit(solution)/shard_map/ppermute | solution.py:20
  51.7 1.9 collective-permute-start.6
  53.6 6.9 %collective-permute-done.4 = bf16[4,16,4096]{2,1,0:T(8,128)(2,1)S(1)} collective-permute-done((bf16[4,16,4096]{2,1,0:T(8,128)(2,1)S(1)}, bf16[4,16,4096]{2,1,0:T(8,128)(2,1)S(1)}, u32[]{:S(2)}, u32[]{:S(2)}) %collective-permute-start.4) | collective-permute-done | bytes 524320 | tf_op jit(solution)/shard_map/ppermute | solution.py:20
  60.6 5.0 %collective-permute-done.6 = bf16[4,16,4096]{2,1,0:T(8,128)(2,1)S(1)} collective-permute-done((bf16[4,16,4096]{2,1,0:T(8,128)(2,1)S(1)}, bf16[4,16,4096]{2,1,0:T(8,128)(2,1)S(1)}, u32[]{:S(2)}, u32[]{:S(2)}) %collective-permute-start.6) | collective-permute-done | bytes 524320 | tf_op jit(solution)/shard_map/ppermute | solution.py:20
  65.6 1.9 collective-permute-start.12
  67.6 5.1 %collective-permute-start.13 = (bf16[2,64,1280]{2,1,0:T(8,128)(2,1)S(1)}, bf16[2,64,1280]{2,1,0:T(8,128)(2,1)S(1)}, u32[]{:S(2)}, u32[]{:S(2)}) collective-permute-start(bf16[2,64,1280]{2,1,0:T(8,128)(2,1)S(1)} %slice.15), channel_id=1, source_target_pairs={{0,384},{16,400},{32,416},{48,432},{64,448},{80,464},{96,480},{112... | collective-permute-start | bytes 983048 | tf_op jit(solution)/shard_map/ppermute | solution.py:20
  72.7 0.9 constant_dynamic-update-slice_fusion.14
  73.6 0.9 constant_dynamic-update-slice_fusion.13.rest_4_
  74.5 1.9 collective-permute-start.14
  76.5 1.9 collective-permute-start.8
  78.4 3.9 %collective-permute-start.9 = (bf16[2,16,4096]{2,1,0:T(8,128)(2,1)S(1)}, bf16[2,16,4096]{2,1,0:T(8,128)(2,1)S(1)}, u32[]{:S(2)}, u32[]{:S(2)}) collective-permute-start(bf16[2,16,4096]{2,1,0:T(8,128)(2,1)S(1)} %slice.13), channel_id=1, source_target_pairs={{0,96},{16,112},{32,0},{48,16},{64,32},{80,48},{96,64},{112,80},{1... | collective-permute-start | bytes 786440 | tf_op jit(solution)/shard_map/ppermute | solution.py:20
  82.3 0.9 constant_dynamic-update-slice_fusion.7
  83.2 0.0 copy-start.7
  83.2 0.0 copy-start.8
  83.2 0.9 constant_dynamic-update-slice_fusion.6.rest_0_
  84.1 2.9 %collective-permute-done.8 = bf16[2,16,4096]{2,1,0:T(8,128)(2,1)S(1)} collective-permute-done((bf16[2,16,4096]{2,1,0:T(8,128)(2,1)S(1)}, bf16[2,16,4096]{2,1,0:T(8,128)(2,1)S(1)}, u32[]{:S(2)}, u32[]{:S(2)}) %collective-permute-start.8) | collective-permute-done | bytes 262176 | tf_op jit(solution)/shard_map/ppermute | solution.py:20
  87.1 1.9 collective-permute-start.10
  89.0 0.7 constant_dynamic-update-slice_fusion.12
  89.8 2.4 %collective-permute-start.15 = (bf16[4,64,1280]{2,1,0:T(8,128)(2,1)S(1)}, bf16[4,64,1280]{2,1,0:T(8,128)(2,1)}, u32[]{:S(2)}, u32[]{:S(2)}) collective-permute-start(bf16[4,64,1280]{2,1,0:T(8,128)(2,1)S(1)} %constant_dynamic-update-slice_fusion.18.rest_5_), channel_id=1, source_target_pairs={{0,16},{16,0},{32,48},{48,32},{64,80},{80,64},{96,112},{112,96},{1... | collective-permute-start | bytes 1966088 | tf_op jit(solution)/shard_map/ppermute | solution.py:20
  92.2 0.7 constant_dynamic-update-slice_fusion.11.rest_1_
  92.9 1.9 collective-permute-start.11
  94.9 0.3 fusion.order_ref
  95.2 1.9 collective-permute-done.11.rest_3_
  97.1 1.1 all-to-all-done
  98.2 8.5 %expert.1 = bf16[384,2048]{1,0:T(8,128)(2,1)} custom-call(bf16[384,2048]{1,0:T(8,128)(2,1)S(1)} %bitcast.10, bf16[768,768]{1,0:T(8,128)(2,1)S(1)} %fusion.order_ref, bf16[12,16,4096]{2,1,0:T(8,128)(2,1)} %constant_dynamic-update-slice_fusion.6.rest_0_, bf16[4,16,4096]{2,1,0:T(8,128)(2,1)} %constant_dynamic-update-slice_fusion.11.rest_1_, ...), custom_call_target="tpu_custom_call" | custom-call | flops 3623878656 | bytes 12582912 | tf_op jit(solution)/shard_map/expert/pallas_call | solution.py:200
  106.7 0.0 copy-start.9
  106.7 0.0 copy-start.2
  106.7 10.4 %all-to-all-start.1 = ((bf16[16,24,2048]{2,1,0:T(8,128)(2,1)}), bf16[16,24,2048]{2,1,0:T(8,128)(2,1)S(1)}, u32[]{:S(2)}, u32[]{:S(2)}) async-start(bf16[16,24,2048]{2,1,0:T(8,128)(2,1)} %bitcast.7), calls=%async_computation.1 | async-start | bytes 3145728 | tf_op jit(solution)/shard_map/all_to_all | solution.py:251
  117.1 0.1 copy.13.expert_ref
  117.3 0.1 copy.14.probs_ref
  117.4 74.3 %all-to-all-done.1 = bf16[16,24,2048]{2,1,0:T(8,128)(2,1)S(1)} async-done(((bf16[16,24,2048]{2,1,0:T(8,128)(2,1)}), bf16[16,24,2048]{2,1,0:T(8,128)(2,1)S(1)}, u32[]{:S(2)}, u32[]{:S(2)}) %all-to-all-start.1) | async-done | bytes 1572896 | tf_op jit(solution)/shard_map/all_to_all | solution.py:251
  191.7 1.6 last.1
  (35 shorter events, 0.3 us)
Async XLA Ops:
  3.2 22.8 %collective-permute-start.1 = (bf16[1,64,1280]{2,1,0:T(8,128)(2,1)}, bf16[1,64,1280]{2,1,0:T(8,128)(2,1)S(1)}, u32[]{:S(2)}, u32[]{:S(2)}) collective-permute-start(bf16[1,64,1280]{2,1,0:T(8,128)(2,1)} %get-tuple-element.18), channel_id=1, source_target_pairs={{0,32},{16,48},{32,0},{48,16},{64,96},{80,112},{96,64},{112,80},{1... | collective-permute-start | bytes 491528 | tf_op jit(solution)/shard_map/ppermute | solution.py:20
  5.8 20.1 %collective-permute-start = (bf16[1,16,4096]{2,1,0:T(8,128)(2,1)}, bf16[1,16,4096]{2,1,0:T(8,128)(2,1)S(1)}, u32[]{:S(2)}, u32[]{:S(2)}) collective-permute-start(bf16[1,16,4096]{2,1,0:T(8,128)(2,1)} %get-tuple-element.17), channel_id=1, source_target_pairs={{0,128},{16,144},{32,160},{48,176},{64,192},{80,208},{96,224},{112... | collective-permute-start | bytes 393224 | tf_op jit(solution)/shard_map/ppermute | solution.py:20
  9.2 15.4 %copy-start.1 = (bf16[1,16,4096]{2,1,0:T(8,128)(2,1)S(1)}, bf16[1,16,4096]{2,1,0:T(8,128)(2,1)}, u32[]{:S(2)}) copy-start(bf16[1,16,4096]{2,1,0:T(8,128)(2,1)} %get-tuple-element.17) | copy-start | bytes 393220
  9.3 16.0 %copy-start = (bf16[1,64,1280]{2,1,0:T(8,128)(2,1)S(1)}, bf16[1,64,1280]{2,1,0:T(8,128)(2,1)}, u32[]{:S(2)}) copy-start(bf16[1,64,1280]{2,1,0:T(8,128)(2,1)} %get-tuple-element.18) | copy-start | bytes 491524
  9.3 88.9 %all-to-all-start = ((bf16[16,24,2048]{2,1,0:T(8,128)(2,1)}), bf16[16,24,2048]{2,1,0:T(8,128)(2,1)S(1)}, u32[]{:S(2)}, u32[]{:S(2)}) async-start(bf16[16,24,2048]{2,1,0:T(8,128)(2,1)} %bitcast.11), calls=%async_computation | async-start | bytes 3145728 | tf_op jit(solution)/shard_map/all_to_all | solution.py:251
  26.0 13.0 %collective-permute-start.3 = (bf16[2,64,1280]{2,1,0:T(8,128)(2,1)S(1)}, bf16[2,64,1280]{2,1,0:T(8,128)(2,1)S(1)}, u32[]{:S(2)}, u32[]{:S(2)}) collective-permute-start(bf16[2,64,1280]{2,1,0:T(8,128)(2,1)S(1)} %pad_maximum_fusion), channel_id=1, source_target_pairs={{0,96},{16,112},{32,64},{48,80},{64,32},{80,48},{96,0},{112,16},{1... | collective-permute-start | bytes 983048 | tf_op jit(solution)/shard_map/ppermute | solution.py:20
  29.0 10.0 %collective-permute-start.2 = (bf16[2,16,4096]{2,1,0:T(8,128)(2,1)S(1)}, bf16[2,16,4096]{2,1,0:T(8,128)(2,1)S(1)}, u32[]{:S(2)}, u32[]{:S(2)}) collective-permute-start(bf16[2,16,4096]{2,1,0:T(8,128)(2,1)S(1)} %pad_maximum_fusion.1), channel_id=1, source_target_pairs={{0,384},{16,400},{32,416},{48,432},{64,448},{80,464},{96,480},{112... | collective-permute-start | bytes 786440 | tf_op jit(solution)/shard_map/ppermute | solution.py:20
  39.8 25.8 %collective-permute-start.5 = (bf16[4,64,1280]{2,1,0:T(8,128)(2,1)S(1)}, bf16[4,64,1280]{2,1,0:T(8,128)(2,1)S(1)}, u32[]{:S(2)}, u32[]{:S(2)}) collective-permute-start(bf16[4,64,1280]{2,1,0:T(8,128)(2,1)S(1)} %get-tuple-element.28), channel_id=1, source_target_pairs={{0,128},{16,144},{32,160},{48,176},{64,192},{80,208},{96,224},{112... | collective-permute-start | bytes 1966088 | tf_op jit(solution)/shard_map/ppermute | solution.py:20
  41.7 23.9 %collective-permute-start.7 = (bf16[4,64,1280]{2,1,0:T(8,128)(2,1)S(1)}, bf16[4,64,1280]{2,1,0:T(8,128)(2,1)S(1)}, u32[]{:S(2)}, u32[]{:S(2)}) collective-permute-start(bf16[4,64,1280]{2,1,0:T(8,128)(2,1)S(1)} %get-tuple-element.28), channel_id=1, source_target_pairs={{0,384},{16,400},{32,416},{48,432},{64,448},{80,464},{96,480},{112... | collective-permute-start | bytes 1966088 | tf_op jit(solution)/shard_map/ppermute | solution.py:20
  47.6 12.9 %collective-permute-start.4 = (bf16[4,16,4096]{2,1,0:T(8,128)(2,1)S(1)}, bf16[4,16,4096]{2,1,0:T(8,128)(2,1)S(1)}, u32[]{:S(2)}, u32[]{:S(2)}) collective-permute-start(bf16[4,16,4096]{2,1,0:T(8,128)(2,1)S(1)} %get-tuple-element.29), channel_id=1, source_target_pairs={{0,32},{16,48},{32,64},{48,80},{64,96},{80,112},{96,0},{112,16},{1... | collective-permute-start | bytes 1572872 | tf_op jit(solution)/shard_map/ppermute | solution.py:20
  51.7 13.9 %collective-permute-start.6 = (bf16[4,16,4096]{2,1,0:T(8,128)(2,1)S(1)}, bf16[4,16,4096]{2,1,0:T(8,128)(2,1)S(1)}, u32[]{:S(2)}, u32[]{:S(2)}) collective-permute-start(bf16[4,16,4096]{2,1,0:T(8,128)(2,1)S(1)} %get-tuple-element.29), channel_id=1, source_target_pairs={{0,96},{16,112},{32,0},{48,16},{64,32},{80,48},{96,64},{112,80},{1... | collective-permute-start | bytes 1572872 | tf_op jit(solution)/shard_map/ppermute | solution.py:20
  65.6 24.1 %collective-permute-start.12 = (bf16[2,64,1280]{2,1,0:T(8,128)(2,1)S(1)}, bf16[2,64,1280]{2,1,0:T(8,128)(2,1)S(1)}, u32[]{:S(2)}, u32[]{:S(2)}) collective-permute-start(bf16[2,64,1280]{2,1,0:T(8,128)(2,1)S(1)} %slice.14), channel_id=1, source_target_pairs={{0,128},{16,144},{32,160},{48,176},{64,192},{80,208},{96,224},{112... | collective-permute-start | bytes 983048 | tf_op jit(solution)/shard_map/ppermute | solution.py:20
  67.6 22.1 %collective-permute-start.13 = (bf16[2,64,1280]{2,1,0:T(8,128)(2,1)S(1)}, bf16[2,64,1280]{2,1,0:T(8,128)(2,1)S(1)}, u32[]{:S(2)}, u32[]{:S(2)}) collective-permute-start(bf16[2,64,1280]{2,1,0:T(8,128)(2,1)S(1)} %slice.15), channel_id=1, source_target_pairs={{0,384},{16,400},{32,416},{48,432},{64,448},{80,464},{96,480},{112... | collective-permute-start | bytes 983048 | tf_op jit(solution)/shard_map/ppermute | solution.py:20
  74.5 22.6 %collective-permute-start.14 = (bf16[12,64,1280]{2,1,0:T(8,128)(2,1)}, bf16[12,64,1280]{2,1,0:T(8,128)(2,1)}, u32[]{:S(2)}, u32[]{:S(2)}) collective-permute-start(bf16[12,64,1280]{2,1,0:T(8,128)(2,1)} %constant_dynamic-update-slice_fusion.13.rest_4_), channel_id=1, source_target_pairs={{0,16},{16,0},{32,48},{48,32},{64,80},{80,64},{96,112},{112,96},{1... | collective-permute-start | bytes 5898248 | tf_op jit(solution)/shard_map/ppermute | solution.py:20
  76.5 10.6 %collective-permute-start.8 = (bf16[2,16,4096]{2,1,0:T(8,128)(2,1)S(1)}, bf16[2,16,4096]{2,1,0:T(8,128)(2,1)S(1)}, u32[]{:S(2)}, u32[]{:S(2)}) collective-permute-start(bf16[2,16,4096]{2,1,0:T(8,128)(2,1)S(1)} %slice.12), channel_id=1, source_target_pairs={{0,32},{16,48},{32,64},{48,80},{64,96},{80,112},{96,0},{112,16},{1... | collective-permute-start | bytes 786440 | tf_op jit(solution)/shard_map/ppermute | solution.py:20
  78.4 13.8 %collective-permute-start.9 = (bf16[2,16,4096]{2,1,0:T(8,128)(2,1)S(1)}, bf16[2,16,4096]{2,1,0:T(8,128)(2,1)S(1)}, u32[]{:S(2)}, u32[]{:S(2)}) collective-permute-start(bf16[2,16,4096]{2,1,0:T(8,128)(2,1)S(1)} %slice.13), channel_id=1, source_target_pairs={{0,96},{16,112},{32,0},{48,16},{64,32},{80,48},{96,64},{112,80},{1... | collective-permute-start | bytes 786440 | tf_op jit(solution)/shard_map/ppermute | solution.py:20
  83.2 11.6 %copy-start.3 = (s32[768]{0:T(1024)S(1)}, s32[768]{0:T(1024)}, u32[]{:S(2)}) copy-start(s32[768]{0:T(1024)} %constant.26.clone) | copy-start | bytes 9220
  83.2 11.6 %copy-start.4 = (s32[768]{0:T(1024)S(1)}, s32[768]{0:T(1024)}, u32[]{:S(2)}) copy-start(s32[768]{0:T(1024)} %constant.27.clone) | copy-start | bytes 9220
  83.2 11.7 %copy-start.5 = (s32[768]{0:T(1024)S(1)}, s32[768]{0:T(1024)}, u32[]{:S(2)}) copy-start(s32[768]{0:T(1024)} %constant.28.clone) | copy-start | bytes 9220
  83.2 11.7 %copy-start.6 = (s32[768]{0:T(1024)S(1)}, s32[768]{0:T(1024)}, u32[]{:S(2)}) copy-start(s32[768]{0:T(1024)} %constant.29.clone) | copy-start | bytes 9220
  83.2 11.7 %copy-start.7 = (s32[768]{0:T(1024)S(1)}, s32[768]{0:T(1024)}, u32[]{:S(2)}) copy-start(s32[768]{0:T(1024)} %constant.30.clone) | copy-start | bytes 9220
  83.2 11.7 %copy-start.8 = (s32[768]{0:T(1024)S(1)}, s32[768]{0:T(1024)}, u32[]{:S(2)}) copy-start(s32[768]{0:T(1024)} %constant.31.clone) | copy-start | bytes 9220
  87.1 10.0 %collective-permute-start.10 = (bf16[12,16,4096]{2,1,0:T(8,128)(2,1)}, bf16[12,16,4096]{2,1,0:T(8,128)(2,1)}, u32[]{:S(2)}, u32[]{:S(2)}) collective-permute-start(bf16[12,16,4096]{2,1,0:T(8,128)(2,1)} %constant_dynamic-update-slice_fusion.6.rest_0_), channel_id=1, source_target_pairs={{0,16},{16,0},{32,48},{48,32},{64,80},{80,64},{96,112},{112,96},{1... | collective-permute-start | bytes 4718600 | tf_op jit(solution)/shard_map/ppermute | solution.py:20
  89.8 7.3 %collective-permute-start.15 = (bf16[4,64,1280]{2,1,0:T(8,128)(2,1)S(1)}, bf16[4,64,1280]{2,1,0:T(8,128)(2,1)}, u32[]{:S(2)}, u32[]{:S(2)}) collective-permute-start(bf16[4,64,1280]{2,1,0:T(8,128)(2,1)S(1)} %constant_dynamic-update-slice_fusion.18.rest_5_), channel_id=1, source_target_pairs={{0,16},{16,0},{32,48},{48,32},{64,80},{80,64},{96,112},{112,96},{1... | collective-permute-start | bytes 1966088 | tf_op jit(solution)/shard_map/ppermute | solution.py:20
  92.9 4.1 %collective-permute-start.11 = (bf16[4,16,4096]{2,1,0:T(8,128)(2,1)}, bf16[4,16,4096]{2,1,0:T(8,128)(2,1)}, u32[]{:S(2)}, u32[]{:S(2)}) collective-permute-start(bf16[4,16,4096]{2,1,0:T(8,128)(2,1)} %constant_dynamic-update-slice_fusion.11.rest_1_), channel_id=1, source_target_pairs={{0,16},{16,0},{32,48},{48,32},{64,80},{80,64},{96,112},{112,96},{1... | collective-permute-start | bytes 1572872 | tf_op jit(solution)/shard_map/ppermute | solution.py:20
  106.7 10.4 %copy-start.9 = (s32[128]{0:T(128)S(1)}, s32[128]{0:T(128)}, u32[]{:S(2)}) copy-start(s32[128]{0:T(128)} %param.15) | copy-start | bytes 1540
  106.7 10.5 %copy-start.2 = (f32[128,8]{0,1:T(8,128)S(1)}, f32[128,8]{0,1:T(8,128)}, u32[]{:S(2)}) copy-start(f32[128,8]{0,1:T(8,128)} %param.14) | copy-start | bytes 12292
  106.7 85.0 %all-to-all-start.1 = ((bf16[16,24,2048]{2,1,0:T(8,128)(2,1)}), bf16[16,24,2048]{2,1,0:T(8,128)(2,1)S(1)}, u32[]{:S(2)}, u32[]{:S(2)}) async-start(bf16[16,24,2048]{2,1,0:T(8,128)(2,1)} %bitcast.7), calls=%async_computation.1 | async-start | bytes 3145728 | tf_op jit(solution)/shard_map/all_to_all | solution.py:251

commit v6 on v3

--- a/solution.py
+++ b/solution.py
@@ -159,18 +159,26 @@
     copy_x.wait()
     x = x_ref[...]
 
-    def units(w, cols):
+    def products(w):
         gate = lax.dot_general(x, w[:, :width], NT, preferred_element_type=F32)
         upper = lax.dot_general(x, w[:, width:], NT, preferred_element_type=F32)
-        hid[:, cols] = (gate / (1.0 + jnp.exp(-gate)) * upper).astype(BF16)
-
-    for c in range(2):
-        copies_a[2 * c].wait()
-        copies_a[2 * c + 1].wait()
-        units(wa[16 * c : 16 * (c + 1)].reshape(256, 2 * width), slice(256 * c, 256 * (c + 1)))
+        return gate, upper
+
+    def activate(c, gate, upper):
+        hid[:, 256 * c : 256 * (c + 1)] = (gate / (1.0 + jnp.exp(-gate)) * upper).astype(BF16)
+
+    copies_a[0].wait()
+    copies_a[1].wait()
+    first = products(wa[:16].reshape(256, 2 * width))
+    copies_a[2].wait()
+    copies_a[3].wait()
+    second = products(wa[16:].reshape(256, 2 * width))
+    activate(0, *first)
     for copy in copies_b:
         copy.wait()
-    units(wb[...].reshape(256, 2 * width), slice(512, 768))
+    third = products(wb[...].reshape(256, 2 * width))
+    activate(1, *second)
+    activate(2, *third)
     hidden = lax.dot_general(hid[...], order_ref[...], NN, preferred_element_type=F32).astype(BF16)
     for copy in copies_d:
         copy.wait()

time: 194 us -> 194 us (level)
  no operation moved by 1% of the time
where the time goes in v6:
time: 194 us; the launch traced here: 193 us
  waiting for transfers between devices  96.9 us (50%)
  starting transfers between devices  72.8 us (38%)
  Pallas kernels  13.4 us (7%)
  local copies, waits for them, and re-layouts  9.61 us (5%)
    all_to_all x2, waiting for transfers between devices, exchange(): lax.all_to_all(blocks, 'expert', split_axis=0, concat_axis=0, tiled=True)  75.5 us
    ppermute x16, starting transfers between devices, trade(): lax.ppermute(x, 'dp', [(i, where(i)) for i in range(lax.axis_size('dp'))])  47.1 us
    all_to_all x2, starting transfers between devices, exchange(): lax.all_to_all(blocks, 'expert', split_axis=0, concat_axis=0, tiled=True)  25.7 us
    ppermute x16, waiting for transfers between devices, trade(): lax.ppermute(x, 'dp', [(i, where(i)) for i in range(lax.axis_size('dp'))])  21.4 us
    pallas_call x1, Pallas kernels, run_expert(): pl.pallas_call(expert_kernel, out_shape=jax.ShapeDtypeStruct((rows, width...  8.66 us
    unnamed x30, local copies, waits for them, and re-layouts  6.15 us
  transfers between devices with their start and end apart: 18, of which 7 were waited for; matrix products, arithmetic and copies ran while one was open for 5% of the time, Pallas kernels for 0%

profile of v6, /device:TPU:24, one launch (start us, length us, event | category | flops | bytes accessed | tf_op | source)
XLA Modules:
  0.0 193.4 jit_solution(7497445099144842145)
XLA Ops:
  0.0 3.2 %prepare.1 = (bf16[384,2048]{1,0:T(8,128)(2,1)}, bf16[1,16,4096]{2,1,0:T(8,128)(2,1)}, bf16[1,64,1280]{2,1,0:T(8,128)(2,1)}) custom-call(bf16[128,2048]{1,0:T(8,128)(2,1)} %refs_0_.1, f32[1,2048]{1,0:T(1,128)} %bitcast.14, s32[1,128]{1,0:T(1,128)} %bitcast.15, bf16[24,4096]{1,0:T(8,128)(2,1)} %bitcast.12, bf16[64,768]{1,0:T(8,128)(2,1)} %bitcast.13), custom_call_target="tpu_custom_call" | custom-call | flops 201326592 | bytes 2097152 | tf_op jit(solution)/shard_map/prepare/pallas_call | solution.py:266
  3.2 2.7 %collective-permute-start.1 = (bf16[1,64,1280]{2,1,0:T(8,128)(2,1)}, bf16[1,64,1280]{2,1,0:T(8,128)(2,1)S(1)}, u32[]{:S(2)}, u32[]{:S(2)}) collective-permute-start(bf16[1,64,1280]{2,1,0:T(8,128)(2,1)} %get-tuple-element.18), channel_id=1, source_target_pairs={{0,32},{16,48},{32,0},{48,16},{64,96},{80,112},{96,64},{112,80},{1... | collective-permute-start | bytes 491528 | tf_op jit(solution)/shard_map/ppermute | solution.py:20
  5.8 3.4 %collective-permute-start = (bf16[1,16,4096]{2,1,0:T(8,128)(2,1)}, bf16[1,16,4096]{2,1,0:T(8,128)(2,1)S(1)}, u32[]{:S(2)}, u32[]{:S(2)}) collective-permute-start(bf16[1,16,4096]{2,1,0:T(8,128)(2,1)} %get-tuple-element.17), channel_id=1, source_target_pairs={{0,128},{16,144},{32,160},{48,176},{64,192},{80,208},{96,224},{112... | collective-permute-start | bytes 393224 | tf_op jit(solution)/shard_map/ppermute | solution.py:20
  9.3 0.0 copy-start
  9.3 15.3 %all-to-all-start = ((bf16[16,24,2048]{2,1,0:T(8,128)(2,1)}), bf16[16,24,2048]{2,1,0:T(8,128)(2,1)S(1)}, u32[]{:S(2)}, u32[]{:S(2)}) async-start(bf16[16,24,2048]{2,1,0:T(8,128)(2,1)} %bitcast.11), calls=%async_computation | async-start | bytes 3145728 | tf_op jit(solution)/shard_map/all_to_all | solution.py:257
  24.6 0.7 constant_dynamic-update-slice_fusion.2
  25.3 0.7 constant_dynamic-update-slice_fusion.17
  26.0 3.0 %collective-permute-start.3 = (bf16[2,64,1280]{2,1,0:T(8,128)(2,1)S(1)}, bf16[2,64,1280]{2,1,0:T(8,128)(2,1)S(1)}, u32[]{:S(2)}, u32[]{:S(2)}) collective-permute-start(bf16[2,64,1280]{2,1,0:T(8,128)(2,1)S(1)} %pad_maximum_fusion), channel_id=1, source_target_pairs={{0,96},{16,112},{32,64},{48,80},{64,32},{80,48},{96,0},{112,16},{1... | collective-permute-start | bytes 983048 | tf_op jit(solution)/shard_map/ppermute | solution.py:20
  29.0 4.0 %collective-permute-start.2 = (bf16[2,16,4096]{2,1,0:T(8,128)(2,1)S(1)}, bf16[2,16,4096]{2,1,0:T(8,128)(2,1)S(1)}, u32[]{:S(2)}, u32[]{:S(2)}) collective-permute-start(bf16[2,16,4096]{2,1,0:T(8,128)(2,1)S(1)} %pad_maximum_fusion.1), channel_id=1, source_target_pairs={{0,384},{16,400},{32,416},{48,432},{64,448},{80,464},{96,480},{112... | collective-permute-start | bytes 786440 | tf_op jit(solution)/shard_map/ppermute | solution.py:20
  33.0 0.7 constant_dynamic-update-slice_fusion.1
  33.7 0.7 constant_dynamic-update-slice_fusion.16
  34.4 4.7 %collective-permute-done.2 = bf16[2,16,4096]{2,1,0:T(8,128)(2,1)S(1)} collective-permute-done((bf16[2,16,4096]{2,1,0:T(8,128)(2,1)S(1)}, bf16[2,16,4096]{2,1,0:T(8,128)(2,1)S(1)}, u32[]{:S(2)}, u32[]{:S(2)}) %collective-permute-start.2) | collective-permute-done | bytes 262176 | tf_op jit(solution)/shard_map/ppermute | solution.py:20
  39.0 0.8 constant_dynamic-update-slice_fusion.15
  39.8 1.9 collective-permute-start.5
  41.7 5.1 %collective-permute-start.7 = (bf16[4,64,1280]{2,1,0:T(8,128)(2,1)S(1)}, bf16[4,64,1280]{2,1,0:T(8,128)(2,1)S(1)}, u32[]{:S(2)}, u32[]{:S(2)}) collective-permute-start(bf16[4,64,1280]{2,1,0:T(8,128)(2,1)S(1)} %get-tuple-element.28), channel_id=1, source_target_pairs={{0,384},{16,400},{32,416},{48,432},{64,448},{80,464},{96,480},{112... | collective-permute-start | bytes 1966088 | tf_op jit(solution)/shard_map/ppermute | solution.py:20
  46.9 0.7 constant_dynamic-update-slice_fusion
  47.6 4.1 %collective-permute-start.4 = (bf16[4,16,4096]{2,1,0:T(8,128)(2,1)S(1)}, bf16[4,16,4096]{2,1,0:T(8,128)(2,1)S(1)}, u32[]{:S(2)}, u32[]{:S(2)}) collective-permute-start(bf16[4,16,4096]{2,1,0:T(8,128)(2,1)S(1)} %get-tuple-element.29), channel_id=1, source_target_pairs={{0,32},{16,48},{32,64},{48,80},{64,96},{80,112},{96,0},{112,16},{1... | collective-permute-start | bytes 1572872 | tf_op jit(solution)/shard_map/ppermute | solution.py:20
  51.7 1.9 collective-permute-start.6
  53.6 6.9 %collective-permute-done.4 = bf16[4,16,4096]{2,1,0:T(8,128)(2,1)S(1)} collective-permute-done((bf16[4,16,4096]{2,1,0:T(8,128)(2,1)S(1)}, bf16[4,16,4096]{2,1,0:T(8,128)(2,1)S(1)}, u32[]{:S(2)}, u32[]{:S(2)}) %collective-permute-start.4) | collective-permute-done | bytes 524320 | tf_op jit(solution)/shard_map/ppermute | solution.py:20
  60.6 5.0 %collective-permute-done.6 = bf16[4,16,4096]{2,1,0:T(8,128)(2,1)S(1)} collective-permute-done((bf16[4,16,4096]{2,1,0:T(8,128)(2,1)S(1)}, bf16[4,16,4096]{2,1,0:T(8,128)(2,1)S(1)}, u32[]{:S(2)}, u32[]{:S(2)}) %collective-permute-start.6) | collective-permute-done | bytes 524320 | tf_op jit(solution)/shard_map/ppermute | solution.py:20
  65.6 1.9 collective-permute-start.12
  67.6 5.1 %collective-permute-start.13 = (bf16[2,64,1280]{2,1,0:T(8,128)(2,1)S(1)}, bf16[2,64,1280]{2,1,0:T(8,128)(2,1)S(1)}, u32[]{:S(2)}, u32[]{:S(2)}) collective-permute-start(bf16[2,64,1280]{2,1,0:T(8,128)(2,1)S(1)} %slice.15), channel_id=1, source_target_pairs={{0,384},{16,400},{32,416},{48,432},{64,448},{80,464},{96,480},{112... | collective-permute-start | bytes 983048 | tf_op jit(solution)/shard_map/ppermute | solution.py:20
  72.7 0.9 constant_dynamic-update-slice_fusion.14
  73.6 0.9 constant_dynamic-update-slice_fusion.13.rest_4_
  74.5 1.9 collective-permute-start.14
  76.5 1.9 collective-permute-start.8
  78.4 3.9 %collective-permute-start.9 = (bf16[2,16,4096]{2,1,0:T(8,128)(2,1)S(1)}, bf16[2,16,4096]{2,1,0:T(8,128)(2,1)S(1)}, u32[]{:S(2)}, u32[]{:S(2)}) collective-permute-start(bf16[2,16,4096]{2,1,0:T(8,128)(2,1)S(1)} %slice.13), channel_id=1, source_target_pairs={{0,96},{16,112},{32,0},{48,16},{64,32},{80,48},{96,64},{112,80},{1... | collective-permute-start | bytes 786440 | tf_op jit(solution)/shard_map/ppermute | solution.py:20
  82.3 0.9 constant_dynamic-update-slice_fusion.7
  83.2 0.0 copy-start.7
  83.2 0.0 copy-start.8
  83.2 0.9 constant_dynamic-update-slice_fusion.6.rest_0_
  84.1 2.9 %collective-permute-done.8 = bf16[2,16,4096]{2,1,0:T(8,128)(2,1)S(1)} collective-permute-done((bf16[2,16,4096]{2,1,0:T(8,128)(2,1)S(1)}, bf16[2,16,4096]{2,1,0:T(8,128)(2,1)S(1)}, u32[]{:S(2)}, u32[]{:S(2)}) %collective-permute-start.8) | collective-permute-done | bytes 262176 | tf_op jit(solution)/shard_map/ppermute | solution.py:20
  87.1 1.9 collective-permute-start.10
  89.0 0.7 constant_dynamic-update-slice_fusion.12
  89.8 2.4 %collective-permute-start.15 = (bf16[4,64,1280]{2,1,0:T(8,128)(2,1)S(1)}, bf16[4,64,1280]{2,1,0:T(8,128)(2,1)}, u32[]{:S(2)}, u32[]{:S(2)}) collective-permute-start(bf16[4,64,1280]{2,1,0:T(8,128)(2,1)S(1)} %constant_dynamic-update-slice_fusion.18.rest_5_), channel_id=1, source_target_pairs={{0,16},{16,0},{32,48},{48,32},{64,80},{80,64},{96,112},{112,96},{1... | collective-permute-start | bytes 1966088 | tf_op jit(solution)/shard_map/ppermute | solution.py:20
  92.2 0.7 constant_dynamic-update-slice_fusion.11.rest_1_
  92.9 1.9 collective-permute-start.11
  94.9 0.3 fusion.order_ref
  95.2 1.9 collective-permute-done.11.rest_3_
  97.1 1.1 all-to-all-done
  98.2 8.7 %expert.1 = bf16[384,2048]{1,0:T(8,128)(2,1)} custom-call(bf16[384,2048]{1,0:T(8,128)(2,1)S(1)} %bitcast.10, bf16[768,768]{1,0:T(8,128)(2,1)S(1)} %fusion.order_ref, bf16[12,16,4096]{2,1,0:T(8,128)(2,1)} %constant_dynamic-update-slice_fusion.6.rest_0_, bf16[4,16,4096]{2,1,0:T(8,128)(2,1)} %constant_dynamic-update-slice_fusion.11.rest_1_, ...), custom_call_target="tpu_custom_call" | custom-call | flops 3623878656 | bytes 12582912 | tf_op jit(solution)/shard_map/expert/pallas_call | solution.py:206
  106.9 0.0 copy-start.9
  106.9 0.0 copy-start.2
  106.9 10.4 %all-to-all-start.1 = ((bf16[16,24,2048]{2,1,0:T(8,128)(2,1)}), bf16[16,24,2048]{2,1,0:T(8,128)(2,1)S(1)}, u32[]{:S(2)}, u32[]{:S(2)}) async-start(bf16[16,24,2048]{2,1,0:T(8,128)(2,1)} %bitcast.7), calls=%async_computation.1 | async-start | bytes 3145728 | tf_op jit(solution)/shard_map/all_to_all | solution.py:257
  117.3 0.1 copy.13.expert_ref
  117.4 0.1 copy.14.probs_ref
  117.5 74.3 %all-to-all-done.1 = bf16[16,24,2048]{2,1,0:T(8,128)(2,1)S(1)} async-done(((bf16[16,24,2048]{2,1,0:T(8,128)(2,1)}), bf16[16,24,2048]{2,1,0:T(8,128)(2,1)S(1)}, u32[]{:S(2)}, u32[]{:S(2)}) %all-to-all-start.1) | async-done | bytes 1572896 | tf_op jit(solution)/shard_map/all_to_all | solution.py:257
  191.9 1.6 last.1
  (35 shorter events, 0.3 us)
Async XLA Ops:
  3.2 22.8 %collective-permute-start.1 = (bf16[1,64,1280]{2,1,0:T(8,128)(2,1)}, bf16[1,64,1280]{2,1,0:T(8,128)(2,1)S(1)}, u32[]{:S(2)}, u32[]{:S(2)}) collective-permute-start(bf16[1,64,1280]{2,1,0:T(8,128)(2,1)} %get-tuple-element.18), channel_id=1, source_target_pairs={{0,32},{16,48},{32,0},{48,16},{64,96},{80,112},{96,64},{112,80},{1... | collective-permute-start | bytes 491528 | tf_op jit(solution)/shard_map/ppermute | solution.py:20
  5.8 20.1 %collective-permute-start = (bf16[1,16,4096]{2,1,0:T(8,128)(2,1)}, bf16[1,16,4096]{2,1,0:T(8,128)(2,1)S(1)}, u32[]{:S(2)}, u32[]{:S(2)}) collective-permute-start(bf16[1,16,4096]{2,1,0:T(8,128)(2,1)} %get-tuple-element.17), channel_id=1, source_target_pairs={{0,128},{16,144},{32,160},{48,176},{64,192},{80,208},{96,224},{112... | collective-permute-start | bytes 393224 | tf_op jit(solution)/shard_map/ppermute | solution.py:20
  9.2 15.4 %copy-start.1 = (bf16[1,16,4096]{2,1,0:T(8,128)(2,1)S(1)}, bf16[1,16,4096]{2,1,0:T(8,128)(2,1)}, u32[]{:S(2)}) copy-start(bf16[1,16,4096]{2,1,0:T(8,128)(2,1)} %get-tuple-element.17) | copy-start | bytes 393220
  9.3 16.0 %copy-start = (bf16[1,64,1280]{2,1,0:T(8,128)(2,1)S(1)}, bf16[1,64,1280]{2,1,0:T(8,128)(2,1)}, u32[]{:S(2)}) copy-start(bf16[1,64,1280]{2,1,0:T(8,128)(2,1)} %get-tuple-element.18) | copy-start | bytes 491524
  9.3 88.9 %all-to-all-start = ((bf16[16,24,2048]{2,1,0:T(8,128)(2,1)}), bf16[16,24,2048]{2,1,0:T(8,128)(2,1)S(1)}, u32[]{:S(2)}, u32[]{:S(2)}) async-start(bf16[16,24,2048]{2,1,0:T(8,128)(2,1)} %bitcast.11), calls=%async_computation | async-start | bytes 3145728 | tf_op jit(solution)/shard_map/all_to_all | solution.py:257
  26.0 13.0 %collective-permute-start.3 = (bf16[2,64,1280]{2,1,0:T(8,128)(2,1)S(1)}, bf16[2,64,1280]{2,1,0:T(8,128)(2,1)S(1)}, u32[]{:S(2)}, u32[]{:S(2)}) collective-permute-start(bf16[2,64,1280]{2,1,0:T(8,128)(2,1)S(1)} %pad_maximum_fusion), channel_id=1, source_target_pairs={{0,96},{16,112},{32,64},{48,80},{64,32},{80,48},{96,0},{112,16},{1... | collective-permute-start | bytes 983048 | tf_op jit(solution)/shard_map/ppermute | solution.py:20
  29.0 10.0 %collective-permute-start.2 = (bf16[2,16,4096]{2,1,0:T(8,128)(2,1)S(1)}, bf16[2,16,4096]{2,1,0:T(8,128)(2,1)S(1)}, u32[]{:S(2)}, u32[]{:S(2)}) collective-permute-start(bf16[2,16,4096]{2,1,0:T(8,128)(2,1)S(1)} %pad_maximum_fusion.1), channel_id=1, source_target_pairs={{0,384},{16,400},{32,416},{48,432},{64,448},{80,464},{96,480},{112... | collective-permute-start | bytes 786440 | tf_op jit(solution)/shard_map/ppermute | solution.py:20
  39.8 25.8 %collective-permute-start.5 = (bf16[4,64,1280]{2,1,0:T(8,128)(2,1)S(1)}, bf16[4,64,1280]{2,1,0:T(8,128)(2,1)S(1)}, u32[]{:S(2)}, u32[]{:S(2)}) collective-permute-start(bf16[4,64,1280]{2,1,0:T(8,128)(2,1)S(1)} %get-tuple-element.28), channel_id=1, source_target_pairs={{0,128},{16,144},{32,160},{48,176},{64,192},{80,208},{96,224},{112... | collective-permute-start | bytes 1966088 | tf_op jit(solution)/shard_map/ppermute | solution.py:20
  41.7 23.9 %collective-permute-start.7 = (bf16[4,64,1280]{2,1,0:T(8,128)(2,1)S(1)}, bf16[4,64,1280]{2,1,0:T(8,128)(2,1)S(1)}, u32[]{:S(2)}, u32[]{:S(2)}) collective-permute-start(bf16[4,64,1280]{2,1,0:T(8,128)(2,1)S(1)} %get-tuple-element.28), channel_id=1, source_target_pairs={{0,384},{16,400},{32,416},{48,432},{64,448},{80,464},{96,480},{112... | collective-permute-start | bytes 1966088 | tf_op jit(solution)/shard_map/ppermute | solution.py:20
  47.6 12.9 %collective-permute-start.4 = (bf16[4,16,4096]{2,1,0:T(8,128)(2,1)S(1)}, bf16[4,16,4096]{2,1,0:T(8,128)(2,1)S(1)}, u32[]{:S(2)}, u32[]{:S(2)}) collective-permute-start(bf16[4,16,4096]{2,1,0:T(8,128)(2,1)S(1)} %get-tuple-element.29), channel_id=1, source_target_pairs={{0,32},{16,48},{32,64},{48,80},{64,96},{80,112},{96,0},{112,16},{1... | collective-permute-start | bytes 1572872 | tf_op jit(solution)/shard_map/ppermute | solution.py:20
  51.7 13.9 %collective-permute-start.6 = (bf16[4,16,4096]{2,1,0:T(8,128)(2,1)S(1)}, bf16[4,16,4096]{2,1,0:T(8,128)(2,1)S(1)}, u32[]{:S(2)}, u32[]{:S(2)}) collective-permute-start(bf16[4,16,4096]{2,1,0:T(8,128)(2,1)S(1)} %get-tuple-element.29), channel_id=1, source_target_pairs={{0,96},{16,112},{32,0},{48,16},{64,32},{80,48},{96,64},{112,80},{1... | collective-permute-start | bytes 1572872 | tf_op jit(solution)/shard_map/ppermute | solution.py:20
  65.6 24.1 %collective-permute-start.12 = (bf16[2,64,1280]{2,1,0:T(8,128)(2,1)S(1)}, bf16[2,64,1280]{2,1,0:T(8,128)(2,1)S(1)}, u32[]{:S(2)}, u32[]{:S(2)}) collective-permute-start(bf16[2,64,1280]{2,1,0:T(8,128)(2,1)S(1)} %slice.14), channel_id=1, source_target_pairs={{0,128},{16,144},{32,160},{48,176},{64,192},{80,208},{96,224},{112... | collective-permute-start | bytes 983048 | tf_op jit(solution)/shard_map/ppermute | solution.py:20
  67.6 22.1 %collective-permute-start.13 = (bf16[2,64,1280]{2,1,0:T(8,128)(2,1)S(1)}, bf16[2,64,1280]{2,1,0:T(8,128)(2,1)S(1)}, u32[]{:S(2)}, u32[]{:S(2)}) collective-permute-start(bf16[2,64,1280]{2,1,0:T(8,128)(2,1)S(1)} %slice.15), channel_id=1, source_target_pairs={{0,384},{16,400},{32,416},{48,432},{64,448},{80,464},{96,480},{112... | collective-permute-start | bytes 983048 | tf_op jit(solution)/shard_map/ppermute | solution.py:20
  74.5 22.6 %collective-permute-start.14 = (bf16[12,64,1280]{2,1,0:T(8,128)(2,1)}, bf16[12,64,1280]{2,1,0:T(8,128)(2,1)}, u32[]{:S(2)}, u32[]{:S(2)}) collective-permute-start(bf16[12,64,1280]{2,1,0:T(8,128)(2,1)} %constant_dynamic-update-slice_fusion.13.rest_4_), channel_id=1, source_target_pairs={{0,16},{16,0},{32,48},{48,32},{64,80},{80,64},{96,112},{112,96},{1... | collective-permute-start | bytes 5898248 | tf_op jit(solution)/shard_map/ppermute | solution.py:20
  76.5 10.6 %collective-permute-start.8 = (bf16[2,16,4096]{2,1,0:T(8,128)(2,1)S(1)}, bf16[2,16,4096]{2,1,0:T(8,128)(2,1)S(1)}, u32[]{:S(2)}, u32[]{:S(2)}) collective-permute-start(bf16[2,16,4096]{2,1,0:T(8,128)(2,1)S(1)} %slice.12), channel_id=1, source_target_pairs={{0,32},{16,48},{32,64},{48,80},{64,96},{80,112},{96,0},{112,16},{1... | collective-permute-start | bytes 786440 | tf_op jit(solution)/shard_map/ppermute | solution.py:20
  78.4 13.8 %collective-permute-start.9 = (bf16[2,16,4096]{2,1,0:T(8,128)(2,1)S(1)}, bf16[2,16,4096]{2,1,0:T(8,128)(2,1)S(1)}, u32[]{:S(2)}, u32[]{:S(2)}) collective-permute-start(bf16[2,16,4096]{2,1,0:T(8,128)(2,1)S(1)} %slice.13), channel_id=1, source_target_pairs={{0,96},{16,112},{32,0},{48,16},{64,32},{80,48},{96,64},{112,80},{1... | collective-permute-start | bytes 786440 | tf_op jit(solution)/shard_map/ppermute | solution.py:20
  83.2 11.6 %copy-start.3 = (s32[768]{0:T(1024)S(1)}, s32[768]{0:T(1024)}, u32[]{:S(2)}) copy-start(s32[768]{0:T(1024)} %constant.26.clone) | copy-start | bytes 9220
  83.2 11.6 %copy-start.4 = (s32[768]{0:T(1024)S(1)}, s32[768]{0:T(1024)}, u32[]{:S(2)}) copy-start(s32[768]{0:T(1024)} %constant.27.clone) | copy-start | bytes 9220
  83.2 11.7 %copy-start.5 = (s32[768]{0:T(1024)S(1)}, s32[768]{0:T(1024)}, u32[]{:S(2)}) copy-start(s32[768]{0:T(1024)} %constant.28.clone) | copy-start | bytes 9220
  83.2 11.7 %copy-start.6 = (s32[768]{0:T(1024)S(1)}, s32[768]{0:T(1024)}, u32[]{:S(2)}) copy-start(s32[768]{0:T(1024)} %constant.29.clone) | copy-start | bytes 9220
  83.2 11.7 %copy-start.7 = (s32[768]{0:T(1024)S(1)}, s32[768]{0:T(1024)}, u32[]{:S(2)}) copy-start(s32[768]{0:T(1024)} %constant.30.clone) | copy-start | bytes 9220
  83.2 11.7 %copy-start.8 = (s32[768]{0:T(1024)S(1)}, s32[768]{0:T(1024)}, u32[]{:S(2)}) copy-start(s32[768]{0:T(1024)} %constant.31.clone) | copy-start | bytes 9220
  87.1 10.0 %collective-permute-start.10 = (bf16[12,16,4096]{2,1,0:T(8,128)(2,1)}, bf16[12,16,4096]{2,1,0:T(8,128)(2,1)}, u32[]{:S(2)}, u32[]{:S(2)}) collective-permute-start(bf16[12,16,4096]{2,1,0:T(8,128)(2,1)} %constant_dynamic-update-slice_fusion.6.rest_0_), channel_id=1, source_target_pairs={{0,16},{16,0},{32,48},{48,32},{64,80},{80,64},{96,112},{112,96},{1... | collective-permute-start | bytes 4718600 | tf_op jit(solution)/shard_map/ppermute | solution.py:20
  89.8 7.3 %collective-permute-start.15 = (bf16[4,64,1280]{2,1,0:T(8,128)(2,1)S(1)}, bf16[4,64,1280]{2,1,0:T(8,128)(2,1)}, u32[]{:S(2)}, u32[]{:S(2)}) collective-permute-start(bf16[4,64,1280]{2,1,0:T(8,128)(2,1)S(1)} %constant_dynamic-update-slice_fusion.18.rest_5_), channel_id=1, source_target_pairs={{0,16},{16,0},{32,48},{48,32},{64,80},{80,64},{96,112},{112,96},{1... | collective-permute-start | bytes 1966088 | tf_op jit(solution)/shard_map/ppermute | solution.py:20
  92.9 4.1 %collective-permute-start.11 = (bf16[4,16,4096]{2,1,0:T(8,128)(2,1)}, bf16[4,16,4096]{2,1,0:T(8,128)(2,1)}, u32[]{:S(2)}, u32[]{:S(2)}) collective-permute-start(bf16[4,16,4096]{2,1,0:T(8,128)(2,1)} %constant_dynamic-update-slice_fusion.11.rest_1_), channel_id=1, source_target_pairs={{0,16},{16,0},{32,48},{48,32},{64,80},{80,64},{96,112},{112,96},{1... | collective-permute-start | bytes 1572872 | tf_op jit(solution)/shard_map/ppermute | solution.py:20
  106.9 10.4 %copy-start.9 = (s32[128]{0:T(128)S(1)}, s32[128]{0:T(128)}, u32[]{:S(2)}) copy-start(s32[128]{0:T(128)} %param.15) | copy-start | bytes 1540
  106.9 10.5 %copy-start.2 = (f32[128,8]{0,1:T(8,128)S(1)}, f32[128,8]{0,1:T(8,128)}, u32[]{:S(2)}) copy-start(f32[128,8]{0,1:T(8,128)} %param.14) | copy-start | bytes 12292
  106.9 85.0 %all-to-all-start.1 = ((bf16[16,24,2048]{2,1,0:T(8,128)(2,1)}), bf16[16,24,2048]{2,1,0:T(8,128)(2,1)S(1)}, u32[]{:S(2)}, u32[]{:S(2)}) async-start(bf16[16,24,2048]{2,1,0:T(8,128)(2,1)} %bitcast.7), calls=%async_computation.1 | async-start | bytes 3145728 | tf_op jit(solution)/shard_map/all_to_all | solution.py:257

commit v7 on v3

--- a/solution.py
+++ b/solution.py
@@ -54,9 +54,12 @@
         trade(a_r[2:], turn(Y_BIT, -1)),
         trade(b_r[2:], turn(X_BIT, -1)),
     )
+    near = flip(CORE)
+    a_0, b_0, a_1, b_1, a_near, b_near = lax.optimization_barrier(
+        (a_0, b_0, a_1, b_1, trade(a12, near), trade(b12, near))
+    )
     a4, b4 = jnp.concatenate([a_0, a_1], axis=0), jnp.concatenate([b_0, b_1], axis=0)
-    near = flip(CORE)
-    return (a12, a4, trade(a12, near), trade(a4, near)), (b12, b4, trade(b12, near), trade(b4, near))
+    return (a12, a4, a_near, trade(a4, near)), (b12, b4, b_near, trade(b4, near))
 
 
 def shard_of(me, slot, x_first):
@@ -213,7 +216,7 @@
             pltpu.SemaphoreType.DMA((32,)),
             pltpu.SemaphoreType.DMA((4,)),
         ],
-        compiler_params=pltpu.CompilerParams(vmem_limit_bytes=46 << 20),
+        compiler_params=pltpu.CompilerParams(vmem_limit_bytes=50 << 20),
         cost_estimate=pl.CostEstimate(
             flops=6 * rows * width * ff,
             bytes_accessed=6 * width * ff + 4 * x.size,

time: 194 us -> 192 us (0.990)
  the two profiles are of different devices: /device:TPU:24 before, /device:TPU:32 now
where the time goes in v7:
time: 192 us; the launch traced here: 191 us
  waiting for transfers between devices  99.2 us (52%)
  starting transfers between devices  76.7 us (40%)
  Pallas kernels  13.3 us (7%)
    all_to_all x2, waiting for transfers between devices, exchange(): lax.all_to_all(blocks, 'expert', split_axis=0, concat_axis=0, tiled=True)  75.3 us
    ppermute x16, starting transfers between devices, trade(): lax.ppermute(x, 'dp', [(i, where(i)) for i in range(lax.axis_size('dp'))])  51.2 us
    all_to_all x2, starting transfers between devices, exchange(): lax.all_to_all(blocks, 'expert', split_axis=0, concat_axis=0, tiled=True)  25.4 us
    ppermute x16, waiting for transfers between devices, trade(): lax.ppermute(x, 'dp', [(i, where(i)) for i in range(lax.axis_size('dp'))])  23.9 us
    pallas_call x1, Pallas kernels, run_expert(): pl.pallas_call(expert_kernel, out_shape=jax.ShapeDtypeStruct((rows, width...  8.55 us
  transfers between devices with their start and end apart: 18, of which 7 were waited for; matrix products, arithmetic and copies ran while one was open for 1% of the time, Pallas kernels for 0%

profile of v7, /device:TPU:32, one launch (start us, length us, event | category | flops | bytes accessed | tf_op | source)
XLA Modules:
  0.0 190.8 jit_solution(8861816433393438511)
XLA Ops:
  0.0 3.2 %prepare.1 = (bf16[384,2048]{1,0:T(8,128)(2,1)}, bf16[1,16,4096]{2,1,0:T(8,128)(2,1)}, bf16[1,64,1280]{2,1,0:T(8,128)(2,1)}) custom-call(bf16[128,2048]{1,0:T(8,128)(2,1)} %refs_0_.1, f32[1,2048]{1,0:T(1,128)} %bitcast.14, s32[1,128]{1,0:T(1,128)} %bitcast.15, bf16[24,4096]{1,0:T(8,128)(2,1)} %bitcast.12, bf16[64,768]{1,0:T(8,128)(2,1)} %bitcast.13), custom_call_target="tpu_custom_call" | custom-call | flops 201326592 | bytes 2097152 | tf_op jit(solution)/shard_map/prepare/pallas_call | solution.py:261
  3.2 3.5 %collective-permute-start.1 = (bf16[1,64,1280]{2,1,0:T(8,128)(2,1)}, bf16[1,64,1280]{2,1,0:T(8,128)(2,1)S(1)}, u32[]{:S(2)}, u32[]{:S(2)}) collective-permute-start(bf16[1,64,1280]{2,1,0:T(8,128)(2,1)} %get-tuple-element.24), channel_id=1, source_target_pairs={{0,32},{16,48},{32,0},{48,16},{64,96},{80,112},{96,64},{112,80},{1... | collective-permute-start | bytes 491528 | tf_op jit(solution)/shard_map/ppermute | solution.py:20
  6.7 3.4 %collective-permute-start = (bf16[1,16,4096]{2,1,0:T(8,128)(2,1)}, bf16[1,16,4096]{2,1,0:T(8,128)(2,1)S(1)}, u32[]{:S(2)}, u32[]{:S(2)}) collective-permute-start(bf16[1,16,4096]{2,1,0:T(8,128)(2,1)} %get-tuple-element.23), channel_id=1, source_target_pairs={{0,128},{16,144},{32,160},{48,176},{64,192},{80,208},{96,224},{112... | collective-permute-start | bytes 393224 | tf_op jit(solution)/shard_map/ppermute | solution.py:20
  10.1 0.0 copy-start.4
  10.1 15.4 %all-to-all-start = ((bf16[16,24,2048]{2,1,0:T(8,128)(2,1)}), bf16[16,24,2048]{2,1,0:T(8,128)(2,1)}, u32[]{:S(2)}, u32[]{:S(2)}) async-start(bf16[16,24,2048]{2,1,0:T(8,128)(2,1)} %bitcast.11), calls=%async_computation | async-start | bytes 3145728 | tf_op jit(solution)/shard_map/all_to_all | solution.py:252
  25.5 0.0 collective-permute-done
  25.5 0.0 collective-permute-done.1
  25.6 4.1 %collective-permute-start.3 = (bf16[2,64,1280]{2,1,0:T(8,128)(2,1)S(1)}, bf16[2,64,1280]{2,1,0:T(8,128)(2,1)S(1)}, u32[]{:S(2)}, u32[]{:S(2)}) collective-permute-start(bf16[2,64,1280]{2,1,0:T(8,128)(2,1)S(1)} %pad_maximum_fusion), channel_id=1, source_target_pairs={{0,96},{16,112},{32,64},{48,80},{64,32},{80,48},{96,0},{112,16},{1... | collective-permute-start | bytes 983048 | tf_op jit(solution)/shard_map/ppermute | solution.py:20
  29.7 4.0 %collective-permute-start.2 = (bf16[2,16,4096]{2,1,0:T(8,128)(2,1)S(1)}, bf16[2,16,4096]{2,1,0:T(8,128)(2,1)S(1)}, u32[]{:S(2)}, u32[]{:S(2)}) collective-permute-start(bf16[2,16,4096]{2,1,0:T(8,128)(2,1)S(1)} %pad_maximum_fusion.1), channel_id=1, source_target_pairs={{0,384},{16,400},{32,416},{48,432},{64,448},{80,464},{96,480},{112... | collective-permute-start | bytes 786440 | tf_op jit(solution)/shard_map/ppermute | solution.py:20
  33.8 5.7 %collective-permute-done.2 = bf16[2,16,4096]{2,1,0:T(8,128)(2,1)S(1)} collective-permute-done((bf16[2,16,4096]{2,1,0:T(8,128)(2,1)S(1)}, bf16[2,16,4096]{2,1,0:T(8,128)(2,1)S(1)}, u32[]{:S(2)}, u32[]{:S(2)}) %collective-permute-start.2) | collective-permute-done | bytes 262176 | tf_op jit(solution)/shard_map/ppermute | solution.py:20
  39.5 0.0 collective-permute-done.3
  39.5 1.9 %collective-permute-start.5 = (bf16[4,64,1280]{2,1,0:T(8,128)(2,1)S(1)}, bf16[4,64,1280]{2,1,0:T(8,128)(2,1)S(1)}, u32[]{:S(2)}, u32[]{:S(2)}) collective-permute-start(bf16[4,64,1280]{2,1,0:T(8,128)(2,1)S(1)} %get-tuple-element.40), channel_id=1, source_target_pairs={{0,128},{16,144},{32,160},{48,176},{64,192},{80,208},{96,224},{112... | collective-permute-start | bytes 1966088 | tf_op jit(solution)/shard_map/ppermute | solution.py:20
  41.4 5.1 %collective-permute-start.7 = (bf16[4,64,1280]{2,1,0:T(8,128)(2,1)S(1)}, bf16[4,64,1280]{2,1,0:T(8,128)(2,1)S(1)}, u32[]{:S(2)}, u32[]{:S(2)}) collective-permute-start(bf16[4,64,1280]{2,1,0:T(8,128)(2,1)S(1)} %get-tuple-element.40), channel_id=1, source_target_pairs={{0,384},{16,400},{32,416},{48,432},{64,448},{80,464},{96,480},{112... | collective-permute-start | bytes 1966088 | tf_op jit(solution)/shard_map/ppermute | solution.py:20
  46.6 2.6 %collective-permute-start.4 = (bf16[4,16,4096]{2,1,0:T(8,128)(2,1)S(1)}, bf16[4,16,4096]{2,1,0:T(8,128)(2,1)S(1)}, u32[]{:S(2)}, u32[]{:S(2)}) collective-permute-start(bf16[4,16,4096]{2,1,0:T(8,128)(2,1)S(1)} %get-tuple-element.41), channel_id=1, source_target_pairs={{0,32},{16,48},{32,64},{48,80},{64,96},{80,112},{96,0},{112,16},{1... | collective-permute-start | bytes 1572872 | tf_op jit(solution)/shard_map/ppermute | solution.py:20
  49.2 4.5 %collective-permute-start.6 = (bf16[4,16,4096]{2,1,0:T(8,128)(2,1)S(1)}, bf16[4,16,4096]{2,1,0:T(8,128)(2,1)S(1)}, u32[]{:S(2)}, u32[]{:S(2)}) collective-permute-start(bf16[4,16,4096]{2,1,0:T(8,128)(2,1)S(1)} %get-tuple-element.41), channel_id=1, source_target_pairs={{0,96},{16,112},{32,0},{48,16},{64,32},{80,48},{96,64},{112,80},{1... | collective-permute-start | bytes 1572872 | tf_op jit(solution)/shard_map/ppermute | solution.py:20
  53.7 6.9 %collective-permute-done.4 = bf16[4,16,4096]{2,1,0:T(8,128)(2,1)S(1)} collective-permute-done((bf16[4,16,4096]{2,1,0:T(8,128)(2,1)S(1)}, bf16[4,16,4096]{2,1,0:T(8,128)(2,1)S(1)}, u32[]{:S(2)}, u32[]{:S(2)}) %collective-permute-start.4) | collective-permute-done | bytes 524320 | tf_op jit(solution)/shard_map/ppermute | solution.py:20
  60.6 1.2 collective-permute-done.6
  61.9 1.9 %collective-permute-start.13 = (bf16[12,64,1280]{2,1,0:T(8,128)(2,1)S(1)}, bf16[12,64,1280]{2,1,0:T(8,128)(2,1)S(1)}, u32[]{:S(2)}, u32[]{:S(2)}) collective-permute-start(bf16[12,64,1280]{2,1,0:T(8,128)(2,1)S(1)} %constant_dynamic-update-slice_fusion.11.rest_4_), channel_id=1, source_target_pairs={{0,16},{16,0},{32,48},{48,32},{64,80},{80,64},{96,112},{112,96},{1... | collective-permute-start | bytes 5898248 | tf_op jit(solution)/shard_map/ppermute | solution.py:20
  63.9 2.4 %collective-permute-start.12 = (bf16[12,16,4096]{2,1,0:T(8,128)(2,1)S(1)}, bf16[12,16,4096]{2,1,0:T(8,128)(2,1)S(1)}, u32[]{:S(2)}, u32[]{:S(2)}) collective-permute-start(bf16[12,16,4096]{2,1,0:T(8,128)(2,1)S(1)} %constant_dynamic-update-slice_fusion.6.rest_0_), channel_id=1, source_target_pairs={{0,16},{16,0},{32,48},{48,32},{64,80},{80,64},{96,112},{112,96},{1... | collective-permute-start | bytes 4718600 | tf_op jit(solution)/shard_map/ppermute | solution.py:20
  66.4 5.6 %collective-permute-start.10 = (bf16[2,16,4096]{2,1,0:T(8,128)(2,1)S(1)}, bf16[2,16,4096]{2,1,0:T(8,128)(2,1)S(1)}, u32[]{:S(2)}, u32[]{:S(2)}) collective-permute-start(bf16[2,16,4096]{2,1,0:T(8,128)(2,1)S(1)} %slice.14), channel_id=1, source_target_pairs={{0,96},{16,112},{32,0},{48,16},{64,32},{80,48},{96,64},{112,80},{1... | collective-permute-start | bytes 786440 | tf_op jit(solution)/shard_map/ppermute | solution.py:20
  72.1 0.0 copy-start.7
  72.1 0.0 copy-start.8
  72.1 0.0 copy-start.9
  72.1 0.0 copy-start.10
  72.1 0.0 copy-start.11
  72.1 0.0 copy-start.12
  72.1 2.9 %collective-permute-start.11 = (bf16[2,64,1280]{2,1,0:T(8,128)(2,1)S(1)}, bf16[2,64,1280]{2,1,0:T(8,128)(2,1)S(1)}, u32[]{:S(2)}, u32[]{:S(2)}) collective-permute-start(bf16[2,64,1280]{2,1,0:T(8,128)(2,1)S(1)} %slice.15), channel_id=1, source_target_pairs={{0,384},{16,400},{32,416},{48,432},{64,448},{80,464},{96,480},{112... | collective-permute-start | bytes 983048 | tf_op jit(solution)/shard_map/ppermute | solution.py:20
  75.1 3.0 %collective-permute-start.9 = (bf16[2,64,1280]{2,1,0:T(8,128)(2,1)S(1)}, bf16[2,64,1280]{2,1,0:T(8,128)(2,1)S(1)}, u32[]{:S(2)}, u32[]{:S(2)}) collective-permute-start(bf16[2,64,1280]{2,1,0:T(8,128)(2,1)S(1)} %slice.13), channel_id=1, source_target_pairs={{0,128},{16,144},{32,160},{48,176},{64,192},{80,208},{96,224},{112... | collective-permute-start | bytes 983048 | tf_op jit(solution)/shard_map/ppermute | solution.py:20
  78.2 1.9 %collective-permute-start.8 = (bf16[2,16,4096]{2,1,0:T(8,128)(2,1)S(1)}, bf16[2,16,4096]{2,1,0:T(8,128)(2,1)S(1)}, u32[]{:S(2)}, u32[]{:S(2)}) collective-permute-start(bf16[2,16,4096]{2,1,0:T(8,128)(2,1)S(1)} %slice.12), channel_id=1, source_target_pairs={{0,32},{16,48},{32,64},{48,80},{64,96},{80,112},{96,0},{112,16},{1... | collective-permute-start | bytes 786440 | tf_op jit(solution)/shard_map/ppermute | solution.py:20
  80.1 8.9 %collective-permute-done.8 = bf16[2,16,4096]{2,1,0:T(8,128)(2,1)S(1)} collective-permute-done((bf16[2,16,4096]{2,1,0:T(8,128)(2,1)S(1)}, bf16[2,16,4096]{2,1,0:T(8,128)(2,1)S(1)}, u32[]{:S(2)}, u32[]{:S(2)}) %collective-permute-start.8) | collective-permute-done | bytes 262176 | tf_op jit(solution)/shard_map/ppermute | solution.py:20
  89.0 0.0 collective-permute-done.11
  89.0 0.0 collective-permute-done.9
  89.0 0.0 collective-permute-done.12.rest_2_
  89.0 0.0 collective-permute-done.13.rest_6_
  89.1 1.9 %collective-permute-start.15 = (bf16[4,64,1280]{2,1,0:T(8,128)(2,1)S(1)}, bf16[4,64,1280]{2,1,0:T(8,128)(2,1)S(1)}, u32[]{:S(2)}, u32[]{:S(2)}) collective-permute-start(bf16[4,64,1280]{2,1,0:T(8,128)(2,1)S(1)} %constant_dynamic-update-slice_fusion.18.rest_5_), channel_id=1, source_target_pairs={{0,16},{16,0},{32,48},{48,32},{64,80},{80,64},{96,112},{112,96},{1... | collective-permute-start | bytes 1966088 | tf_op jit(solution)/shard_map/ppermute | solution.py:20
  91.1 2.4 %collective-permute-start.14 = (bf16[4,16,4096]{2,1,0:T(8,128)(2,1)S(1)}, bf16[4,16,4096]{2,1,0:T(8,128)(2,1)S(1)}, u32[]{:S(2)}, u32[]{:S(2)}) collective-permute-start(bf16[4,16,4096]{2,1,0:T(8,128)(2,1)S(1)} %constant_dynamic-update-slice_fusion.16.rest_1_), channel_id=1, source_target_pairs={{0,16},{16,0},{32,48},{48,32},{64,80},{80,64},{96,112},{112,96},{1... | collective-permute-start | bytes 1572872 | tf_op jit(solution)/shard_map/ppermute | solution.py:20
  93.6 0.3 fusion.order_ref
  93.9 1.2 collective-permute-done.14.rest_3_
  95.1 0.0 collective-permute-done.15.rest_7_
  95.1 2.0 %all-to-all-done = bf16[16,24,2048]{2,1,0:T(8,128)(2,1)} async-done(((bf16[16,24,2048]{2,1,0:T(8,128)(2,1)}), bf16[16,24,2048]{2,1,0:T(8,128)(2,1)}, u32[]{:S(2)}, u32[]{:S(2)}) %all-to-all-start) | async-done | bytes 1572896 | tf_op jit(solution)/shard_map/all_to_all | solution.py:252
  97.1 8.6 %expert.1 = bf16[384,2048]{1,0:T(8,128)(2,1)} custom-call(bf16[384,2048]{1,0:T(8,128)(2,1)} %bitcast.6.x_hbm, bf16[768,768]{1,0:T(8,128)(2,1)S(1)} %fusion.order_ref, bf16[12,16,4096]{2,1,0:T(8,128)(2,1)} %copy-done.2, bf16[4,16,4096]{2,1,0:T(8,128)(2,1)S(1)} %constant_dynamic-update-slice_fusion.16.rest_1_, bf16[12,16,4096]{2,1,0:T(8,128)(2,1)} %copy-done.3, ...), custom_call_target="tpu_custom_call" | custom-call | flops 3623878656 | bytes 12582912 | tf_op jit(solution)/shard_map/expert/pallas_call | solution.py:201
  105.6 0.0 copy-start.13
  105.6 0.0 copy-start.6
  105.6 10.1 %all-to-all-start.1 = ((bf16[16,24,2048]{2,1,0:T(8,128)(2,1)}), bf16[16,24,2048]{2,1,0:T(8,128)(2,1)S(1)}, u32[]{:S(2)}, u32[]{:S(2)}) async-start(bf16[16,24,2048]{2,1,0:T(8,128)(2,1)} %bitcast.10), calls=%async_computation.1 | async-start | bytes 3145728 | tf_op jit(solution)/shard_map/all_to_all | solution.py:252
  115.7 0.1 copy.13.expert_ref
  115.8 0.1 copy.14.probs_ref
  115.9 73.3 %all-to-all-done.1 = bf16[16,24,2048]{2,1,0:T(8,128)(2,1)S(1)} async-done(((bf16[16,24,2048]{2,1,0:T(8,128)(2,1)}), bf16[16,24,2048]{2,1,0:T(8,128)(2,1)S(1)}, u32[]{:S(2)}, u32[]{:S(2)}) %all-to-all-start.1) | async-done | bytes 1572896 | tf_op jit(solution)/shard_map/all_to_all | solution.py:252
  189.3 1.6 last.1
  (43 shorter events, 0.6 us)
Async XLA Ops:
  3.2 22.4 %collective-permute-start.1 = (bf16[1,64,1280]{2,1,0:T(8,128)(2,1)}, bf16[1,64,1280]{2,1,0:T(8,128)(2,1)S(1)}, u32[]{:S(2)}, u32[]{:S(2)}) collective-permute-start(bf16[1,64,1280]{2,1,0:T(8,128)(2,1)} %get-tuple-element.24), channel_id=1, source_target_pairs={{0,32},{16,48},{32,0},{48,16},{64,96},{80,112},{96,64},{112,80},{1... | collective-permute-start | bytes 491528 | tf_op jit(solution)/shard_map/ppermute | solution.py:20
  6.7 18.9 %collective-permute-start = (bf16[1,16,4096]{2,1,0:T(8,128)(2,1)}, bf16[1,16,4096]{2,1,0:T(8,128)(2,1)S(1)}, u32[]{:S(2)}, u32[]{:S(2)}) collective-permute-start(bf16[1,16,4096]{2,1,0:T(8,128)(2,1)} %get-tuple-element.23), channel_id=1, source_target_pairs={{0,128},{16,144},{32,160},{48,176},{64,192},{80,208},{96,224},{112... | collective-permute-start | bytes 393224 | tf_op jit(solution)/shard_map/ppermute | solution.py:20
  10.1 15.4 %copy-start.5 = (bf16[1,16,4096]{2,1,0:T(8,128)(2,1)S(1)}, bf16[1,16,4096]{2,1,0:T(8,128)(2,1)}, u32[]{:S(2)}) copy-start(bf16[1,16,4096]{2,1,0:T(8,128)(2,1)} %get-tuple-element.23) | copy-start | bytes 393220
  10.1 15.4 %copy-start.4 = (bf16[1,64,1280]{2,1,0:T(8,128)(2,1)S(1)}, bf16[1,64,1280]{2,1,0:T(8,128)(2,1)}, u32[]{:S(2)}) copy-start(bf16[1,64,1280]{2,1,0:T(8,128)(2,1)} %get-tuple-element.24) | copy-start | bytes 491524
  10.1 87.0 %all-to-all-start = ((bf16[16,24,2048]{2,1,0:T(8,128)(2,1)}), bf16[16,24,2048]{2,1,0:T(8,128)(2,1)}, u32[]{:S(2)}, u32[]{:S(2)}) async-start(bf16[16,24,2048]{2,1,0:T(8,128)(2,1)} %bitcast.11), calls=%async_computation | async-start | bytes 3145728 | tf_op jit(solution)/shard_map/all_to_all | solution.py:252
  25.6 13.9 %collective-permute-start.3 = (bf16[2,64,1280]{2,1,0:T(8,128)(2,1)S(1)}, bf16[2,64,1280]{2,1,0:T(8,128)(2,1)S(1)}, u32[]{:S(2)}, u32[]{:S(2)}) collective-permute-start(bf16[2,64,1280]{2,1,0:T(8,128)(2,1)S(1)} %pad_maximum_fusion), channel_id=1, source_target_pairs={{0,96},{16,112},{32,64},{48,80},{64,32},{80,48},{96,0},{112,16},{1... | collective-permute-start | bytes 983048 | tf_op jit(solution)/shard_map/ppermute | solution.py:20
  29.7 9.7 %collective-permute-start.2 = (bf16[2,16,4096]{2,1,0:T(8,128)(2,1)S(1)}, bf16[2,16,4096]{2,1,0:T(8,128)(2,1)S(1)}, u32[]{:S(2)}, u32[]{:S(2)}) collective-permute-start(bf16[2,16,4096]{2,1,0:T(8,128)(2,1)S(1)} %pad_maximum_fusion.1), channel_id=1, source_target_pairs={{0,384},{16,400},{32,416},{48,432},{64,448},{80,464},{96,480},{112... | collective-permute-start | bytes 786440 | tf_op jit(solution)/shard_map/ppermute | solution.py:20
  39.5 22.3 %collective-permute-start.5 = (bf16[4,64,1280]{2,1,0:T(8,128)(2,1)S(1)}, bf16[4,64,1280]{2,1,0:T(8,128)(2,1)S(1)}, u32[]{:S(2)}, u32[]{:S(2)}) collective-permute-start(bf16[4,64,1280]{2,1,0:T(8,128)(2,1)S(1)} %get-tuple-element.40), channel_id=1, source_target_pairs={{0,128},{16,144},{32,160},{48,176},{64,192},{80,208},{96,224},{112... | collective-permute-start | bytes 1966088 | tf_op jit(solution)/shard_map/ppermute | solution.py:20
  41.4 20.4 %collective-permute-start.7 = (bf16[4,64,1280]{2,1,0:T(8,128)(2,1)S(1)}, bf16[4,64,1280]{2,1,0:T(8,128)(2,1)S(1)}, u32[]{:S(2)}, u32[]{:S(2)}) collective-permute-start(bf16[4,64,1280]{2,1,0:T(8,128)(2,1)S(1)} %get-tuple-element.40), channel_id=1, source_target_pairs={{0,384},{16,400},{32,416},{48,432},{64,448},{80,464},{96,480},{112... | collective-permute-start | bytes 1966088 | tf_op jit(solution)/shard_map/ppermute | solution.py:20
  46.6 14.0 %collective-permute-start.4 = (bf16[4,16,4096]{2,1,0:T(8,128)(2,1)S(1)}, bf16[4,16,4096]{2,1,0:T(8,128)(2,1)S(1)}, u32[]{:S(2)}, u32[]{:S(2)}) collective-permute-start(bf16[4,16,4096]{2,1,0:T(8,128)(2,1)S(1)} %get-tuple-element.41), channel_id=1, source_target_pairs={{0,32},{16,48},{32,64},{48,80},{64,96},{80,112},{96,0},{112,16},{1... | collective-permute-start | bytes 1572872 | tf_op jit(solution)/shard_map/ppermute | solution.py:20
  49.2 12.6 %collective-permute-start.6 = (bf16[4,16,4096]{2,1,0:T(8,128)(2,1)S(1)}, bf16[4,16,4096]{2,1,0:T(8,128)(2,1)S(1)}, u32[]{:S(2)}, u32[]{:S(2)}) collective-permute-start(bf16[4,16,4096]{2,1,0:T(8,128)(2,1)S(1)} %get-tuple-element.41), channel_id=1, source_target_pairs={{0,96},{16,112},{32,0},{48,16},{64,32},{80,48},{96,64},{112,80},{1... | collective-permute-start | bytes 1572872 | tf_op jit(solution)/shard_map/ppermute | solution.py:20
  61.9 10.1 %copy-start = (bf16[12,64,1280]{2,1,0:T(8,128)(2,1)}, bf16[12,64,1280]{2,1,0:T(8,128)(2,1)S(1)}, u32[]{:S(2)}) copy-start(bf16[12,64,1280]{2,1,0:T(8,128)(2,1)S(1)} %constant_dynamic-update-slice_fusion.11.rest_4_) | copy-start | bytes 5898244
  61.9 27.1 %collective-permute-start.13 = (bf16[12,64,1280]{2,1,0:T(8,128)(2,1)S(1)}, bf16[12,64,1280]{2,1,0:T(8,128)(2,1)S(1)}, u32[]{:S(2)}, u32[]{:S(2)}) collective-permute-start(bf16[12,64,1280]{2,1,0:T(8,128)(2,1)S(1)} %constant_dynamic-update-slice_fusion.11.rest_4_), channel_id=1, source_target_pairs={{0,16},{16,0},{32,48},{48,32},{64,80},{80,64},{96,112},{112,96},{1... | collective-permute-start | bytes 5898248 | tf_op jit(solution)/shard_map/ppermute | solution.py:20
  63.9 25.2 %copy-start.2 = (bf16[12,16,4096]{2,1,0:T(8,128)(2,1)}, bf16[12,16,4096]{2,1,0:T(8,128)(2,1)S(1)}, u32[]{:S(2)}) copy-start(bf16[12,16,4096]{2,1,0:T(8,128)(2,1)S(1)} %constant_dynamic-update-slice_fusion.6.rest_0_) | copy-start | bytes 4718596
  63.9 25.1 %collective-permute-start.12 = (bf16[12,16,4096]{2,1,0:T(8,128)(2,1)S(1)}, bf16[12,16,4096]{2,1,0:T(8,128)(2,1)S(1)}, u32[]{:S(2)}, u32[]{:S(2)}) collective-permute-start(bf16[12,16,4096]{2,1,0:T(8,128)(2,1)S(1)} %constant_dynamic-update-slice_fusion.6.rest_0_), channel_id=1, source_target_pairs={{0,16},{16,0},{32,48},{48,32},{64,80},{80,64},{96,112},{112,96},{1... | collective-permute-start | bytes 4718600 | tf_op jit(solution)/shard_map/ppermute | solution.py:20
  66.4 11.8 %collective-permute-start.10 = (bf16[2,16,4096]{2,1,0:T(8,128)(2,1)S(1)}, bf16[2,16,4096]{2,1,0:T(8,128)(2,1)S(1)}, u32[]{:S(2)}, u32[]{:S(2)}) collective-permute-start(bf16[2,16,4096]{2,1,0:T(8,128)(2,1)S(1)} %slice.14), channel_id=1, source_target_pairs={{0,96},{16,112},{32,0},{48,16},{64,32},{80,48},{96,64},{112,80},{1... | collective-permute-start | bytes 786440 | tf_op jit(solution)/shard_map/ppermute | solution.py:20
  72.1 21.5 %copy-start.7 = (s32[768]{0:T(1024)S(1)}, s32[768]{0:T(1024)}, u32[]{:S(2)}) copy-start(s32[768]{0:T(1024)} %constant.26.clone) | copy-start | bytes 9220
  72.1 21.5 %copy-start.8 = (s32[768]{0:T(1024)S(1)}, s32[768]{0:T(1024)}, u32[]{:S(2)}) copy-start(s32[768]{0:T(1024)} %constant.27.clone) | copy-start | bytes 9220
  72.1 21.5 %copy-start.9 = (s32[768]{0:T(1024)S(1)}, s32[768]{0:T(1024)}, u32[]{:S(2)}) copy-start(s32[768]{0:T(1024)} %constant.28.clone) | copy-start | bytes 9220
  72.1 21.5 %copy-start.10 = (s32[768]{0:T(1024)S(1)}, s32[768]{0:T(1024)}, u32[]{:S(2)}) copy-start(s32[768]{0:T(1024)} %constant.29.clone) | copy-start | bytes 9220
  72.1 21.5 %copy-start.11 = (s32[768]{0:T(1024)S(1)}, s32[768]{0:T(1024)}, u32[]{:S(2)}) copy-start(s32[768]{0:T(1024)} %constant.30.clone) | copy-start | bytes 9220
  72.1 21.5 %copy-start.12 = (s32[768]{0:T(1024)S(1)}, s32[768]{0:T(1024)}, u32[]{:S(2)}) copy-start(s32[768]{0:T(1024)} %constant.31.clone) | copy-start | bytes 9220
  72.1 16.9 %collective-permute-start.11 = (bf16[2,64,1280]{2,1,0:T(8,128)(2,1)S(1)}, bf16[2,64,1280]{2,1,0:T(8,128)(2,1)S(1)}, u32[]{:S(2)}, u32[]{:S(2)}) collective-permute-start(bf16[2,64,1280]{2,1,0:T(8,128)(2,1)S(1)} %slice.15), channel_id=1, source_target_pairs={{0,384},{16,400},{32,416},{48,432},{64,448},{80,464},{96,480},{112... | collective-permute-start | bytes 983048 | tf_op jit(solution)/shard_map/ppermute | solution.py:20
  75.1 14.0 %collective-permute-start.9 = (bf16[2,64,1280]{2,1,0:T(8,128)(2,1)S(1)}, bf16[2,64,1280]{2,1,0:T(8,128)(2,1)S(1)}, u32[]{:S(2)}, u32[]{:S(2)}) collective-permute-start(bf16[2,64,1280]{2,1,0:T(8,128)(2,1)S(1)} %slice.13), channel_id=1, source_target_pairs={{0,128},{16,144},{32,160},{48,176},{64,192},{80,208},{96,224},{112... | collective-permute-start | bytes 983048 | tf_op jit(solution)/shard_map/ppermute | solution.py:20
  78.2 10.9 %collective-permute-start.8 = (bf16[2,16,4096]{2,1,0:T(8,128)(2,1)S(1)}, bf16[2,16,4096]{2,1,0:T(8,128)(2,1)S(1)}, u32[]{:S(2)}, u32[]{:S(2)}) collective-permute-start(bf16[2,16,4096]{2,1,0:T(8,128)(2,1)S(1)} %slice.12), channel_id=1, source_target_pairs={{0,32},{16,48},{32,64},{48,80},{64,96},{80,112},{96,0},{112,16},{1... | collective-permute-start | bytes 786440 | tf_op jit(solution)/shard_map/ppermute | solution.py:20
  89.0 4.5 %copy-start.3 = (bf16[12,16,4096]{2,1,0:T(8,128)(2,1)}, bf16[12,16,4096]{2,1,0:T(8,128)(2,1)S(1)}, u32[]{:S(2)}) copy-start(bf16[12,16,4096]{2,1,0:T(8,128)(2,1)S(1)} %collective-permute-done.12.rest_2_) | copy-start | bytes 4718596
  89.1 2.1 %copy-start.1 = (bf16[12,64,1280]{2,1,0:T(8,128)(2,1)}, bf16[12,64,1280]{2,1,0:T(8,128)(2,1)S(1)}, u32[]{:S(2)}) copy-start(bf16[12,64,1280]{2,1,0:T(8,128)(2,1)S(1)} %collective-permute-done.13.rest_6_) | copy-start | bytes 5898244
  89.1 5.9 %collective-permute-start.15 = (bf16[4,64,1280]{2,1,0:T(8,128)(2,1)S(1)}, bf16[4,64,1280]{2,1,0:T(8,128)(2,1)S(1)}, u32[]{:S(2)}, u32[]{:S(2)}) collective-permute-start(bf16[4,64,1280]{2,1,0:T(8,128)(2,1)S(1)} %constant_dynamic-update-slice_fusion.18.rest_5_), channel_id=1, source_target_pairs={{0,16},{16,0},{32,48},{48,32},{64,80},{80,64},{96,112},{112,96},{1... | collective-permute-start | bytes 1966088 | tf_op jit(solution)/shard_map/ppermute | solution.py:20
  91.1 3.9 %collective-permute-start.14 = (bf16[4,16,4096]{2,1,0:T(8,128)(2,1)S(1)}, bf16[4,16,4096]{2,1,0:T(8,128)(2,1)S(1)}, u32[]{:S(2)}, u32[]{:S(2)}) collective-permute-start(bf16[4,16,4096]{2,1,0:T(8,128)(2,1)S(1)} %constant_dynamic-update-slice_fusion.16.rest_1_), channel_id=1, source_target_pairs={{0,16},{16,0},{32,48},{48,32},{64,80},{80,64},{96,112},{112,96},{1... | collective-permute-start | bytes 1572872 | tf_op jit(solution)/shard_map/ppermute | solution.py:20
  105.6 10.1 %copy-start.13 = (s32[128]{0:T(128)S(1)}, s32[128]{0:T(128)}, u32[]{:S(2)}) copy-start(s32[128]{0:T(128)} %param.15) | copy-start | bytes 1540
  105.6 10.2 %copy-start.6 = (f32[128,8]{0,1:T(8,128)S(1)}, f32[128,8]{0,1:T(8,128)}, u32[]{:S(2)}) copy-start(f32[128,8]{0,1:T(8,128)} %param.14) | copy-start | bytes 12292
  105.6 83.6 %all-to-all-start.1 = ((bf16[16,24,2048]{2,1,0:T(8,128)(2,1)}), bf16[16,24,2048]{2,1,0:T(8,128)(2,1)S(1)}, u32[]{:S(2)}, u32[]{:S(2)}) async-start(bf16[16,24,2048]{2,1,0:T(8,128)(2,1)} %bitcast.10), calls=%async_computation.1 | async-start | bytes 3145728 | tf_op jit(solution)/shard_map/all_to_all | solution.py:252
